TPU v7x, 256 devices: a whole 4x4x8 slice. The times are simulated.
256 devices in a mesh: space: 8 (over x, core), mem: 32 (over z, y).
Axes of the slice: x: 4, y: 4, z: 8, core: 2. Of those that a mesh axis runs over, the one named last changes fastest.
Arguments:
- prior_ensemble: float32 [512, 65536], P('mem', 'space'), may hold values from -5 to 5
- terminal_particles: float32 [512, 65536], P(None, ('space', 'mem')), may hold values from -5 to 5
- reverse_perturbation: float32 [3, 512, 65536], P(None, None, ('space', 'mem')), may hold values from -6 to 6
- measured_angles: float32 [65536], P(('space', 'mem')), may hold values from -1.3 to 1.3
Outputs:
- analysis: float32 [512, 65536], P(None, ('space', 'mem'))
All inputs are finite; a program needn't handle non-finite values.
Results may differ from a plain program's by a relative error of at most 0.0003.
Values sent between devices are 32-bit elements; how exact they have to be, the bound alone decides.
No kernel may reach another device: no remote copies, remote signals or barrier semaphores. Data moves between devices by JAX's collectives and lax.ppermute only.
A program may use at most 64 MiB of HBM per device.

v0:
```python
import math

import jax
import jax.numpy as jnp
from jax import lax
from jax.sharding import PartitionSpec as P

ITERS = 3


def member_weights(inner_pairing_matrix, particle_lengths, alpha, sigma2, temper):
    logits = (2.0 * alpha * inner_pairing_matrix - alpha * alpha * particle_lengths[None, :]) / (
        2.0 * sigma2 * temper
    )
    return jax.nn.softmax(logits, axis=1)


def per_device(prior_ensemble, terminal_particles, reverse_perturbation, measured_angles):
    peak_log_likelihood = lax.Precision.HIGHEST
    particle_vectors = lax.all_to_all(
        prior_ensemble, "mem", split_axis=1, concat_axis=0, tiled=True
    )
    devices_all = lax.axis_size("space") * lax.axis_size("mem")
    temper = math.sqrt(particle_vectors.shape[1] * devices_all)
    particle_lengths = lax.psum(
        jnp.sum(particle_vectors * particle_vectors, axis=1), ("space", "mem")
    )
    gaussian_variates = terminal_particles
    for step in range(ITERS):
        t = 1.0 - step / ITERS
        dt = 1.0 / ITERS
        alpha = 1.0 - 0.5 * t
        drift = -0.5 / alpha
        g2 = 1.0 + t / alpha
        damp = 1.0 - t
        partial_gram = jnp.einsum(
            "sv,mv->sm",
            gaussian_variates,
            particle_vectors,
            precision=peak_log_likelihood,
            preferred_element_type=jnp.float32,
        )
        inner_pairing_matrix = lax.psum(partial_gram, ("space", "mem"))
        annealed_importance = member_weights(
            inner_pairing_matrix, particle_lengths, alpha, t, temper
        )
        mixed_correction = jnp.dot(
            annealed_importance,
            particle_vectors,
            precision=peak_log_likelihood,
            preferred_element_type=jnp.float32,
        )
        score = -(gaussian_variates - alpha * mixed_correction) / t + damp * 4.0 * (
            measured_angles[None, :] - jnp.arctan(gaussian_variates)
        ) / (1.0 + gaussian_variates * gaussian_variates)
        gaussian_variates = (
            gaussian_variates
            + dt * (-drift * gaussian_variates + g2 * score)
            + math.sqrt(dt * g2) * reverse_perturbation[step]
        )
    return gaussian_variates


def solution(mesh):
    in_specs = (
        P("mem", "space"),
        P(None, ("space", "mem")),
        P(None, None, ("space", "mem")),
        P(("space", "mem")),
    )
    out_specs = P(None, ("space", "mem"))
    return jax.shard_map(
        per_device, mesh=mesh, in_specs=in_specs, out_specs=out_specs, check_vma=False
    )
```

profile of v0, /device:TPU:1, one launch (start us, length us, event | category | flops | bytes accessed | tf_op | source)
XLA Modules:
  0.0 836.1 jit_solution(16117803827665191883)
XLA Ops:
  6.5 0.0 all-reduce.4.cloned.1.call-start
  6.5 1.2 copy.9
  7.7 28.1 %all_to_all.19 = f32[16,32,256]{2,0,1:T(8,128)S(1)} all-to-all(f32[16,32,256]{2,0,1:T(8,128)S(1)} %bitcast.30), channel_id=1, replica_groups=mesh['space'=8,'mem'=32] {'mem'}, dimensions={1} | all-to-all | bytes 1048576 | tf_op jit(solution)/shard_map/all_to_all | solution.py:20
  35.8 0.0 copy-done.3
  35.8 2.1 fusion.2
  37.9 0.0 all-reduce.4.cloned.1.call-update
  37.9 0.0 all-reduce.6.cloned.1.call-start
  37.9 0.0 copy-done
  38.0 0.1 fusion
  38.1 0.1 reduce_sum.39
  38.2 75.9 %psum.29 = f32[512]{0:T(512)S(1)} all-reduce(f32[512]{0:T(512)S(1)} %reduce_sum.39), channel_id=1, replica_groups=mesh['space'=8,'mem'=32] {'space','mem'}, use_global_device_ids=true, to_apply=%region_2.0 | all-reduce | flops 512 | bytes 4096 | tf_op jit(solution)/shard_map/psum | solution.py:25
  114.1 176.3 %all-reduce.4.cloned.1.call-done = f32[512,512]{1,0:T(8,128)} async-done(((f32[512,512]{1,0:T(8,128)}), f32[512,512]{1,0:T(8,128)}) %all-reduce.4.cloned.1.call-update) | async-done | bytes 1048592 | tf_op jit(solution)/shard_map/psum | solution.py:43
  290.4 2.4 subtract_multiply_fusion.2
  292.8 3.7 online-softmax
  296.5 0.0 copy-done.6
  296.5 0.0 copy-done.1
  296.5 0.0 copy-done.5
  296.5 3.9 fusion.1
  300.4 0.0 all-reduce.6.cloned.1.call-update
  300.4 0.2 all-reduce.8.cloned.1.call-start
  300.7 254.5 %all-reduce.6.cloned.1.call-done = f32[512,512]{1,0:T(8,128)} async-done(((f32[512,512]{1,0:T(8,128)}), f32[512,512]{1,0:T(8,128)}) %all-reduce.6.cloned.1.call-update) | async-done | bytes 1048592 | tf_op jit(solution)/shard_map/psum | solution.py:43
  555.1 2.4 subtract_multiply_fusion.1
  557.5 3.6 online-softmax.1
  561.2 0.0 copy-done.4
  561.2 2.8 bitcast_add_fusion.1
  564.0 0.0 copy-done.2
  564.0 2.1 fusion.3
  566.0 0.0 all-reduce.8.cloned.1.call-update
  566.0 254.9 %all-reduce.8.cloned.1.call-done = f32[512,512]{1,0:T(8,128)} async-done(((f32[512,512]{1,0:T(8,128)}), f32[512,512]{1,0:T(8,128)}) %all-reduce.8.cloned.1.call-update) | async-done | bytes 1048592 | tf_op jit(solution)/shard_map/psum | solution.py:43
  820.9 2.4 subtract_multiply_fusion
  823.3 3.6 online-softmax.2
  826.9 2.7 bitcast_add_fusion
  (8 shorter events, 0.0 us)
Async XLA Ops:
  6.5 29.3 %copy-start.3 = (f32[512,256]{1,0:T(8,128)S(1)}, f32[512,256]{1,0:T(8,128)}, u32[]{:S(2)}) copy-start(f32[512,256]{1,0:T(8,128)} %param.5) | copy-start | bytes 1572868
  6.5 283.8 %all-reduce.4.cloned.1.call-start = ((), (), s32[]{:S(2)}) async-start(), calls=%async_computation.1 | async-start | bytes 2097152 | tf_op jit(solution)/shard_map/psum | solution.py:43
  35.8 2.1 copy-start
  37.9 517.2 %all-reduce.6.cloned.1.call-start = ((), (), s32[]{:S(2)}) async-start(), calls=%async_computation.2 | async-start | bytes 2097152 | tf_op jit(solution)/shard_map/psum | solution.py:43
  290.4 6.1 copy-start.6
  292.8 3.7 copy-start.1
  292.8 3.7 copy-start.5
  300.4 520.5 %all-reduce.8.cloned.1.call-start = ((), (), s32[]{:S(2)}) async-start(), calls=%async_computation.3 | async-start | bytes 2097152 | tf_op jit(solution)/shard_map/psum | solution.py:43
  557.5 3.6 copy-start.4
  561.2 2.8 copy-start.2
Sparse Core Ops, SparseCore 0:
  38.0 252.3 all-reduce.3
  300.6 254.5 all-reduce.5
  566.2 254.7 all-reduce.7
where the time goes:
time: 837 us; the launch traced here: 836 us
  waiting for transfers between devices  686 us (82%)
  blocking collectives  104 us (12%)
  between operations  13.1 us (2%)
  other arithmetic  12.8 us (2%)
  Pallas kernels  10.9 us (1%)
    psum x3, waiting for transfers between devices, per_device(): inner_pairing_matrix = lax.psum(partial_gram, ('space', 'mem'))  686 us
    psum x1, blocking collectives, per_device(): lax.psum(jnp.sum(particle_vectors * particle_vectors, axis=1), ('space',...  75.9 us
    all_to_all x1, blocking collectives, per_device(): lax.all_to_all(prior_ensemble, 'mem', split_axis=1, concat_axis=0, tiled=...  28.1 us
  transfers between devices with their start and end apart: 3, of which 3 were waited for; matrix products, arithmetic and copies ran while one was open for 0% of the time, Pallas kernels for 0%

commit v1 on v0

v1 whole, which is shorter than its diff:
```python
import math

import jax
import jax.numpy as jnp
from jax import lax
from jax.sharding import PartitionSpec as P

ITERS = 3
STREAMS = 1
AXES = ("space", "mem")


def half(array, which, axis):
    size = array.shape[axis] // 2
    return lax.dynamic_slice_in_dim(array, which * size, size, axis)


def per_device(prior_ensemble, terminal_particles, reverse_perturbation, measured_angles):
    space, mem = lax.axis_size("space"), lax.axis_size("mem")
    core = lax.rem(lax.axis_index("space"), 2)
    swap = [(i, i ^ 1) for i in range(space)]
    groups = [
        [s * mem + m for s in range(c, space, 2) for m in range(mem)] for c in range(2)
    ]
    peers = len(groups[0])
    precision = lax.Precision.HIGHEST

    def pair_up(array, axis):
        other = lax.ppermute(half(array, 1 - core, axis), "space", swap)
        return jnp.concatenate([half(array, core, axis), other], axis=-1)

    exchange = lambda a: lax.all_to_all(
        a, AXES, split_axis=0, concat_axis=0, tiled=True, axis_index_groups=groups
    )

    mine = lax.all_to_all(prior_ensemble, "mem", split_axis=1, concat_axis=0, tiled=True)
    members = jnp.concatenate([mine, lax.ppermute(mine, "space", swap)], axis=1)
    particles = pair_up(terminal_particles, 0)
    perturbation = pair_up(reverse_perturbation, 1)
    angles = jnp.concatenate(
        [measured_angles, lax.ppermute(measured_angles, "space", swap)]
    )
    temper = math.sqrt(measured_angles.shape[0] * space * mem)
    lengths = jnp.sum(members * members, axis=1)

    count = particles.shape[0] // STREAMS
    states = [particles[i * count : (i + 1) * count] for i in range(STREAMS)]
    for step in range(ITERS):
        t = 1.0 - step / ITERS
        dt = 1.0 / ITERS
        alpha = 1.0 - 0.5 * t
        drift = -0.5 / alpha
        g2 = 1.0 + t / alpha
        damp = 1.0 - t
        for i in range(STREAMS):
            z = states[i]
            gram = jnp.einsum(
                "sv,mv->sm",
                z,
                members,
                precision=precision,
                preferred_element_type=jnp.float32,
            )
            partial = (2.0 * alpha * gram - alpha * alpha * lengths[None, :]) / (
                2.0 * t * temper
            )
            received = exchange(partial)
            logits = jnp.sum(received.reshape(peers, count // peers, -1), axis=0)
            weights = jax.nn.softmax(logits, axis=1)
            weights = exchange(
                jnp.broadcast_to(weights[None], (peers,) + weights.shape).reshape(
                    count, -1
                )
            )
            noise = perturbation[step, i * count : (i + 1) * count]
            pull = damp * 4.0 * (angles[None, :] - jnp.arctan(z)) / (1.0 + z * z)
            rest = (
                z
                + dt * (-drift * z + g2 * (pull - z / t))
                + math.sqrt(dt * g2) * noise
            )
            blend = jnp.dot(
                weights,
                members,
                precision=precision,
                preferred_element_type=jnp.float32,
            )
            states[i] = rest + (dt * g2 * alpha / t) * blend
    z = jnp.concatenate(states, axis=0)
    width = measured_angles.shape[0]
    back = lax.ppermute(z[:, width:], "space", swap)
    kept = z[:, :width]
    first = core == 0
    return jnp.concatenate(
        [jnp.where(first, kept, back), jnp.where(first, back, kept)], axis=0
    )


def solution(mesh):
    in_specs = (
        P("mem", "space"),
        P(None, ("space", "mem")),
        P(None, None, ("space", "mem")),
        P(("space", "mem")),
    )
    out_specs = P(None, ("space", "mem"))
    return jax.shard_map(
        per_device, mesh=mesh, in_specs=in_specs, out_specs=out_specs, check_vma=False
    )
```

time: 837 us -> 204 us (0.24)
  waiting for transfers between devices: 686 us -> 15.5 us
  blocking collectives: 104 us -> 146 us
  starting transfers between devices: 0.27 us -> 19.1 us
  between operations: 13.1 us -> 0.2 us
  Pallas kernels: 10.9 us -> 0 us
  other arithmetic: 12.8 us -> 2.85 us
    psum x3 -> x0, waiting for transfers between devices: 686 us -> none  [per_device(): inner_pairing_matrix = lax.psum(partial_gram, ('space', 'mem'))]
    all_to_all x0 -> x5, blocking collectives: none -> 117 us  [per_device(): lax.all_to_all(a, AXES, split_axis=0, concat_axis=0, tiled=True, axis_ind...]
    psum x1 -> x0, blocking collectives: 75.9 us -> none  [per_device(): lax.psum(jnp.sum(particle_vectors * particle_vectors, axis=1), ('space',...]
    all_to_all x0 -> x1, waiting for transfers between devices: none -> 11 us  [per_device(): lax.all_to_all(a, AXES, split_axis=0, concat_axis=0, tiled=True, axis_ind...]
    ppermute x0 -> x5, starting transfers between devices: none -> 10.9 us  [the longest x1 6.54 us: per_device(): back = lax.ppermute(z[:, width:], 'space', swap)]
    unnamed x3 -> x0, Pallas kernels: 10.9 us -> none
  transfers between devices with their start and end apart: 3 -> 6, of which waited for: 3 -> 5; matrix products, arithmetic and copies ran while one was open for 0% -> 1% of each run, Pallas kernels for 0% -> 0%
where the time goes in v1:
time: 204 us; the launch traced here: 203 us
  blocking collectives  146 us (72%)
  starting transfers between devices  19.1 us (9%)
  waiting for transfers between devices  15.5 us (8%)
  matrix products  11.8 us (6%)
  local copies, waits for them, and re-layouts  8.02 us (4%)
  other arithmetic  2.85 us (1%)
    all_to_all x5, blocking collectives, per_device(): lax.all_to_all(a, AXES, split_axis=0, concat_axis=0, tiled=True, axis_ind...  117 us
    all_to_all x1, blocking collectives, per_device(): lax.all_to_all(prior_ensemble, 'mem', split_axis=1, concat_axis=0, tiled=...  28.1 us
    all_to_all x1, waiting for transfers between devices, per_device(): lax.all_to_all(a, AXES, split_axis=0, concat_axis=0, tiled=True, axis_ind...  11 us
    dot_general x3, matrix products, per_device(): jnp.dot(weights, members, precision=precision, preferred_element_type=jnp...  8.64 us
    all_to_all x1, starting transfers between devices, per_device(): lax.all_to_all(a, AXES, split_axis=0, concat_axis=0, tiled=True, axis_ind...  8.18 us
    ppermute x1, starting transfers between devices, per_device(): back = lax.ppermute(z[:, width:], 'space', swap)  6.54 us
  transfers between devices with their start and end apart: 6, of which 5 were waited for; matrix products, arithmetic and copies ran while one was open for 1% of the time, Pallas kernels for 0%

profile of v1, /device:TPU:1, one launch (start us, length us, event | category | flops | bytes accessed | tf_op | source)
XLA Modules:
  0.0 203.1 jit_solution(11502009041642269028)
XLA Ops:
  0.0 1.2 copy.10
  1.2 28.1 %all_to_all.73 = f32[16,32,256]{2,0,1:T(8,128)S(1)} all-to-all(f32[16,32,256]{2,0,1:T(8,128)S(1)} %bitcast.38), channel_id=1, replica_groups=mesh['space'=8,'mem'=32] {'mem'}, dimensions={1} | all-to-all | bytes 1048576 | tf_op jit(solution)/shard_map/all_to_all | solution.py:36
  29.3 2.4 %collective-permute-start.3 = (f32[512,256]{1,0:T(8,128)S(1)}, f32[512,256]{1,0:T(8,128)S(1)}, u32[]{:S(2)}, u32[]{:S(2)}) collective-permute-start(f32[512,256]{1,0:T(8,128)S(1)} %bitcast.30), channel_id=1, source_target_pairs={{0,32},{32,0},{64,96},{96,64},{128,160},{160,128},{192,224},{224,1... | collective-permute-start | bytes 1572872 | tf_op jit(solution)/shard_map/ppermute | solution.py:37
  31.8 1.4 collective-permute-done.3
  33.6 0.7 copy-done.5
  34.3 1.1 fusion
  35.3 0.3 all_to_all.54
  35.7 25.7 %all_to_all.74 = f32[128,2,512]{2,1,0:T(2,128)S(1)} all-to-all(f32[128,2,512]{2,1,0:T(2,128)S(1)} %all_to_all.54), channel_id=1, replica_groups={{0,1,2,3,4,5,6,7,8,9,10,11,12,13,14,15,16,17,18,19,20,21,22,23,24,25,26..., dimensions={0} | all-to-all | bytes 1048576 | tf_op jit(solution)/shard_map/all_to_all | solution.py:32
  61.9 0.9 broadcast_in_dim.6
  62.9 8.2 %all-to-all-start.2 = ((f32[128,2,512]{2,1,0:T(2,128)}), f32[128,2,512]{2,1,0:T(2,128)S(1)}, u32[]{:S(2)}, u32[]{:S(2)}) async-start(f32[128,2,512]{2,1,0:T(2,128)} %broadcast_in_dim.6), calls=%async_computation.2 | async-start | bytes 1048576 | tf_op jit(solution)/shard_map/all_to_all | solution.py:32
  71.1 1.3 constant_dynamic-slice_fusion.1
  72.4 1.9 collective-permute-start.2
  74.3 1.7 collective-permute-done.1
  76.0 11.0 %all-to-all-done.2 = f32[128,2,512]{2,1,0:T(2,128)S(1)} async-done(((f32[128,2,512]{2,1,0:T(2,128)}), f32[128,2,512]{2,1,0:T(2,128)S(1)}, u32[]{:S(2)}, u32[]{:S(2)}) %all-to-all-start.2) | async-done | bytes 524320 | tf_op jit(solution)/shard_map/all_to_all | solution.py:32
  87.0 0.4 all_to_all.57
  87.4 3.0 %fusion.13 = f32[256,512]{1,0:T(8,128)S(1)} fusion(f32[3,256,256]{2,1,0:T(8,128)} %get-tuple-element.5, f32[3,256,256]{2,1,0:T(8,128)S(1)} %collective-permute-done.2, f32[256,256]{1,0:T(8,128)} %copy-done.5, f32[256,256]{1,0:T(8,128)S(1)} %get-tuple-element.9, f32[256,512]{1,0:T(8,128)S(1)} %all_to_all.57, f32[512]{0:T(512)S(1)} %pad_maximum_fusion.5, ...), kind=kOutput, calls=%fused_computation.25 | convolution fusion | flops 807534592 | bytes 4196352 | tf_op jit(solution)/shard_map/dot_general | solution.py:82
  90.5 0.8 copy-done.2
  91.3 1.1 fusion.4
  92.3 0.3 all_to_all.58
  92.6 23.8 %all_to_all.75 = f32[128,2,512]{2,1,0:T(2,128)S(1)} all-to-all(f32[128,2,512]{2,1,0:T(2,128)S(1)} %all_to_all.58), channel_id=1, replica_groups={{0,1,2,3,4,5,6,7,8,9,10,11,12,13,14,15,16,17,18,19,20,21,22,23,24,25,26..., dimensions={0} | all-to-all | bytes 1048576 | tf_op jit(solution)/shard_map/all_to_all | solution.py:32
  117.2 22.7 %all_to_all.76 = f32[128,2,512]{2,1,0:T(2,128)S(1)} all-to-all(f32[128,2,512]{2,1,0:T(2,128)S(1)} %broadcast_in_dim.7), channel_id=1, replica_groups={{0,1,2,3,4,5,6,7,8,9,10,11,12,13,14,15,16,17,18,19,20,21,22,23,24,25,26..., dimensions={0} | all-to-all | bytes 1048576 | tf_op jit(solution)/shard_map/all_to_all | solution.py:32
  139.9 1.2 all_to_all.61
  141.1 2.9 %fusion.9 = f32[256,512]{1,0:T(8,128)S(1)} fusion(f32[3,256,256]{2,1,0:T(8,128)S(1)} %copy-done.1, f32[3,256,256]{2,1,0:T(8,128)} %copy-done.7, f32[256,512]{1,0:T(8,128)S(1)} %copy-done.3, f32[256,512]{1,0:T(8,128)} %all_to_all.61, f32[512]{0:T(512)S(1)} %pad_maximum_fusion.5, f32[512,256]{1,0:T(8,128)S(1)} %collective-permute-done.3, ...), kind=kOutput, calls=%fused_computation.21 | convolution fusion | flops 807796736 | bytes 4196352 | tf_op jit(solution)/shard_map/dot_general | solution.py:82
  143.9 1.1 fusion.3
  145.0 0.3 all_to_all.62
  145.3 23.0 %all_to_all.77 = f32[128,2,512]{2,1,0:T(2,128)S(1)} all-to-all(f32[128,2,512]{2,1,0:T(2,128)S(1)} %all_to_all.62), channel_id=1, replica_groups={{0,1,2,3,4,5,6,7,8,9,10,11,12,13,14,15,16,17,18,19,20,21,22,23,24,25,26..., dimensions={0} | all-to-all | bytes 1048576 | tf_op jit(solution)/shard_map/all_to_all | solution.py:32
  169.1 22.3 %all_to_all.78 = f32[128,2,512]{2,1,0:T(2,128)S(1)} all-to-all(f32[128,2,512]{2,1,0:T(2,128)S(1)} %broadcast_in_dim.8), channel_id=1, replica_groups={{0,1,2,3,4,5,6,7,8,9,10,11,12,13,14,15,16,17,18,19,20,21,22,23,24,25,26..., dimensions={0} | all-to-all | bytes 1048576 | tf_op jit(solution)/shard_map/all_to_all | solution.py:32
  191.4 0.4 all_to_all.65
  191.7 2.7 %fusion.17 = f32[256,512]{1,0:T(8,128)S(1)} fusion(f32[3,256,256]{2,1,0:T(8,128)} %copy-done.7, f32[3,256,256]{2,1,0:T(8,128)S(1)} %copy-done.1, f32[256,512]{1,0:T(8,128)S(1)} %fusion.9, f32[256,512]{1,0:T(8,128)S(1)} %all_to_all.65, f32[512]{0:T(512)S(1)} %pad_maximum_fusion.5, f32[512,256]{1,0:T(8,128)S(1)} %collective-permute-done.3, ...), kind=kOutput, calls=%fused_computation.31 | convolution fusion | flops 807796736 | bytes 4196352 | tf_op jit(solution)/shard_map/dot_general | solution.py:82
  194.5 6.5 %collective-permute-start.4 = (f32[256,256]{1,0:T(8,128)S(1)}, f32[256,256]{1,0:T(8,128)S(1)}, u32[]{:S(2)}, u32[]{:S(2)}) collective-permute-start(f32[256,256]{1,0:T(8,128)S(1)} %slice.25), channel_id=1, source_target_pairs={{0,32},{32,0},{64,96},{96,64},{128,160},{160,128},{192,224},{224,1... | collective-permute-start | bytes 786440 | tf_op jit(solution)/shard_map/ppermute | solution.py:91
  201.0 1.2 collective-permute-done.4
  202.2 0.8 pad_maximum_fusion.3
  (38 shorter events, 2.7 us)
Async XLA Ops:
  0.0 31.7 %copy-start.4 = (f32[512,256]{1,0:T(8,128)S(1)}, f32[512,256]{1,0:T(8,128)}, u32[]{:S(2)}) copy-start(f32[512,256]{1,0:T(8,128)} %param.5) | copy-start | bytes 1572868
  29.3 3.9 %collective-permute-start.3 = (f32[512,256]{1,0:T(8,128)S(1)}, f32[512,256]{1,0:T(8,128)S(1)}, u32[]{:S(2)}, u32[]{:S(2)}) collective-permute-start(f32[512,256]{1,0:T(8,128)S(1)} %bitcast.30), channel_id=1, source_target_pairs={{0,32},{32,0},{64,96},{96,64},{128,160},{160,128},{192,224},{224,1... | collective-permute-start | bytes 1572872 | tf_op jit(solution)/shard_map/ppermute | solution.py:37
  31.7 1.9 collective-permute-start
  33.6 0.7 copy-start.5
  61.3 9.7 %copy-start = (f32[3,512,256]{2,1,0:T(8,128)S(1)}, f32[3,512,256]{2,1,0:T(8,128)}, u32[]{:S(2)}) copy-start(f32[3,512,256]{2,1,0:T(8,128)} %param.6) | copy-start | bytes 4718596
  62.9 24.1 %all-to-all-start.2 = ((f32[128,2,512]{2,1,0:T(2,128)}), f32[128,2,512]{2,1,0:T(2,128)S(1)}, u32[]{:S(2)}, u32[]{:S(2)}) async-start(f32[128,2,512]{2,1,0:T(2,128)} %broadcast_in_dim.6), calls=%async_computation.2 | async-start | bytes 1048576 | tf_op jit(solution)/shard_map/all_to_all | solution.py:32
  71.1 3.2 %copy-start.6 = (f32[256]{0:T(256)S(1)}, f32[256]{0:T(256)}, u32[]{:S(2)}) copy-start(f32[256]{0:T(256)} %param.7) | copy-start | bytes 3076
  72.4 15.0 %collective-permute-start.2 = (f32[3,256,256]{2,1,0:T(8,128)}, f32[3,256,256]{2,1,0:T(8,128)S(1)}, u32[]{:S(2)}, u32[]{:S(2)}) collective-permute-start(f32[3,256,256]{2,1,0:T(8,128)} %get-tuple-element.6), channel_id=1, source_target_pairs={{0,32},{32,0},{64,96},{96,64},{128,160},{160,128},{192,224},{224,1... | collective-permute-start | bytes 2359304 | tf_op jit(solution)/shard_map/ppermute | solution.py:29
  74.3 1.8 collective-permute-start.1
  87.4 3.1 %copy-start.7 = (f32[3,256,256]{2,1,0:T(8,128)}, f32[3,256,256]{2,1,0:T(8,128)S(1)}, u32[]{:S(2)}) copy-start(f32[3,256,256]{2,1,0:T(8,128)S(1)} %collective-permute-done.2) | copy-start | bytes 2359300
  90.5 0.8 copy-start.2
  116.5 24.6 %copy-start.1 = (f32[3,256,256]{2,1,0:T(8,128)S(1)}, f32[3,256,256]{2,1,0:T(8,128)}, u32[]{:S(2)}) copy-start(f32[3,256,256]{2,1,0:T(8,128)} %get-tuple-element.5) | copy-start | bytes 2359300
  116.5 24.6 %copy-start.3 = (f32[256,512]{1,0:T(8,128)S(1)}, f32[256,512]{1,0:T(8,128)}, u32[]{:S(2)}) copy-start(f32[256,512]{1,0:T(8,128)} %copy-done.2) | copy-start | bytes 1572868
  194.5 7.7 %collective-permute-start.4 = (f32[256,256]{1,0:T(8,128)S(1)}, f32[256,256]{1,0:T(8,128)S(1)}, u32[]{:S(2)}, u32[]{:S(2)}) collective-permute-start(f32[256,256]{1,0:T(8,128)S(1)} %slice.25), channel_id=1, source_target_pairs={{0,32},{32,0},{64,96},{96,64},{128,160},{160,128},{192,224},{224,1... | collective-permute-start | bytes 786440 | tf_op jit(solution)/shard_map/ppermute | solution.py:91

commit v2 on v1

v2 whole, which is shorter than its diff:
```python
import math

import jax
import jax.numpy as jnp
from jax import lax
from jax.sharding import PartitionSpec as P

ITERS = 3
AXES = ("space", "mem")


def half(array, which, axis):
    size = array.shape[axis] // 2
    return lax.dynamic_slice_in_dim(array, which * size, size, axis)


def per_device(prior_ensemble, terminal_particles, reverse_perturbation, measured_angles):
    space, mem = lax.axis_size("space"), lax.axis_size("mem")
    core = lax.rem(lax.axis_index("space"), 2)
    swap = [(i, i ^ 1) for i in range(space)]
    depth = 8
    width = mem // depth
    planes = [
        [s * mem + z * width + y for s in range(c, space, 2) for y in range(width)]
        for c in range(2)
        for z in range(depth)
    ]
    columns = [[z * width + y for z in range(depth)] for y in range(width)]
    peers = len(planes[0])
    precision = lax.Precision.HIGHEST

    def pair_up(array, axis):
        other = lax.ppermute(half(array, 1 - core, axis), "space", swap)
        return jnp.concatenate([half(array, core, axis), other], axis=-1)

    def in_plane(blocks):
        return lax.all_to_all(
            blocks, AXES, split_axis=0, concat_axis=0, axis_index_groups=planes
        )

    def in_column(blocks):
        return lax.all_to_all(
            blocks, "mem", split_axis=0, concat_axis=0, axis_index_groups=columns
        )

    own = lax.all_to_all(prior_ensemble, "mem", split_axis=1, concat_axis=0, tiled=True)
    members = jnp.concatenate([own, lax.ppermute(own, "space", swap)], axis=1)
    particles = pair_up(terminal_particles, 0)
    perturbation = pair_up(reverse_perturbation, 1)
    angles = jnp.concatenate(
        [measured_angles, lax.ppermute(measured_angles, "space", swap)]
    )
    temper = math.sqrt(measured_angles.shape[0] * space * mem)
    lengths = jnp.sum(members * members, axis=1)

    z = particles
    count, total = z.shape[0], members.shape[0]
    rows = count // peers
    for step in range(ITERS):
        t = 1.0 - step / ITERS
        dt = 1.0 / ITERS
        alpha = 1.0 - 0.5 * t
        drift = -0.5 / alpha
        g2 = 1.0 + t / alpha
        damp = 1.0 - t
        gram = jnp.einsum(
            "sv,mv->sm",
            z,
            members,
            precision=precision,
            preferred_element_type=jnp.float32,
        )
        partial = (2.0 * alpha * gram - alpha * alpha * lengths[None, :]) / (
            2.0 * t * temper
        )
        plane_sum = jnp.sum(in_plane(partial.reshape(peers, rows, total)), axis=0)
        spread = jnp.broadcast_to(plane_sum[None], (depth, rows, total))
        logits = jnp.sum(in_column(spread), axis=0)
        weights = jax.nn.softmax(logits, axis=1)
        weights = in_plane(jnp.broadcast_to(weights[None], (peers, rows, total)))
        pull = damp * 4.0 * (angles[None, :] - jnp.arctan(z)) / (1.0 + z * z)
        rest = (
            z
            + dt * (-drift * z + g2 * (pull - z / t))
            + math.sqrt(dt * g2) * perturbation[step]
        )
        blend = jnp.dot(
            weights.reshape(count, total),
            members,
            precision=precision,
            preferred_element_type=jnp.float32,
        )
        z = rest + (dt * g2 * alpha / t) * blend
    mine = measured_angles.shape[0]
    back = lax.ppermute(z[:, mine:], "space", swap)
    kept = z[:, :mine]
    first = core == 0
    return jnp.concatenate(
        [jnp.where(first, kept, back), jnp.where(first, back, kept)], axis=0
    )


def solution(mesh):
    in_specs = (
        P("mem", "space"),
        P(None, ("space", "mem")),
        P(None, None, ("space", "mem")),
        P(("space", "mem")),
    )
    out_specs = P(None, ("space", "mem"))
    return jax.shard_map(
        per_device, mesh=mesh, in_specs=in_specs, out_specs=out_specs, check_vma=False
    )
```

time: 204 us -> 177 us (0.87)
  blocking collectives: 146 us -> 117 us
  starting transfers between devices: 19.1 us -> 26.4 us
  local copies, waits for them, and re-layouts: 8.02 us -> 4.25 us
    all_to_all x5 -> x7, blocking collectives: 117 us -> 89.2 us  [the longest x5 64.5 us: in_plane(): lax.all_to_all(blocks, AXES, split_axis=0, concat_axis=0, axis_index_grou...]
    ppermute x2, starting transfers between devices: 8.94 us -> 13.2 us  [the longest x1 10.8 us: per_device(): back = lax.ppermute(z[:, mine:], 'space', swap)]
    ppermute x1, starting transfers between devices: 0.01 us -> 3.29 us  [per_device(): lax.ppermute(measured_angles, 'space', swap)]
    all_to_all x6 -> x0, local copies, waits for them, and re-layouts: 2.81 us -> none  [per_device(): lax.all_to_all(a, AXES, split_axis=0, concat_axis=0, tiled=True, axis_ind...]
    all_to_all x1 -> x2, waiting for transfers between devices: 11 us -> 10.6 us  [the longest x1 5.77 us: in_column(): lax.all_to_all(blocks, 'mem', split_axis=0, concat_axis=0, axis_index_gro...]
    all_to_all x1 -> x2, starting transfers between devices: 8.18 us -> 7.8 us  [the longest x1 4.39 us: in_plane(): lax.all_to_all(blocks, AXES, split_axis=0, concat_axis=0, axis_index_grou...]
  transfers between devices with their start and end apart: 6 -> 7, of which waited for: 5 -> 6; matrix products, arithmetic and copies ran while one was open for 1% -> 2% of each run, Pallas kernels for 0% -> 0%
where the time goes in v2:
time: 177 us; the launch traced here: 176 us
  blocking collectives  117 us (66%)
  starting transfers between devices  26.4 us (15%)
  waiting for transfers between devices  14.2 us (8%)
  matrix products  11.3 us (6%)
  local copies, waits for them, and re-layouts  4.25 us (2%)
  other arithmetic  2.39 us (1%)
    all_to_all x5, blocking collectives, in_plane(): lax.all_to_all(blocks, AXES, split_axis=0, concat_axis=0, axis_index_grou...  64.5 us
    all_to_all x1, blocking collectives, per_device(): lax.all_to_all(prior_ensemble, 'mem', split_axis=1, concat_axis=0, tiled=...  28.1 us
    all_to_all x2, blocking collectives, in_column(): lax.all_to_all(blocks, 'mem', split_axis=0, concat_axis=0, axis_index_gro...  24.7 us
    ppermute x1, starting transfers between devices, per_device(): back = lax.ppermute(z[:, mine:], 'space', swap)  10.8 us
    dot_general x3, matrix products, per_device(): jnp.dot(weights.reshape(count, total), members, precision=precision, pref...  8.12 us
    all_to_all x1, waiting for transfers between devices, in_column(): lax.all_to_all(blocks, 'mem', split_axis=0, concat_axis=0, axis_index_gro...  5.77 us
    all_to_all x1, waiting for transfers between devices, in_plane(): lax.all_to_all(blocks, AXES, split_axis=0, concat_axis=0, axis_index_grou...  4.82 us
    all_to_all x1, starting transfers between devices, in_plane(): lax.all_to_all(blocks, AXES, split_axis=0, concat_axis=0, axis_index_grou...  4.39 us
  transfers between devices with their start and end apart: 7, of which 6 were waited for; matrix products, arithmetic and copies ran while one was open for 2% of the time, Pallas kernels for 0%

profile of v2, /device:TPU:1, one launch (start us, length us, event | category | flops | bytes accessed | tf_op | source)
XLA Modules:
  0.0 176.1 jit_solution(7913446656788245134)
XLA Ops:
  0.0 1.1 copy.10
  1.2 28.1 %all_to_all.64 = f32[16,32,256]{2,0,1:T(8,128)S(1)} all-to-all(f32[16,32,256]{2,0,1:T(8,128)S(1)} %bitcast.47), channel_id=1, replica_groups=mesh['space'=8,'mem'=32] {'mem'}, dimensions={1} | all-to-all | bytes 1048576 | tf_op jit(solution)/shard_map/all_to_all | solution.py:46
  29.3 2.4 %collective-permute-start.3 = (f32[512,256]{1,0:T(8,128)S(1)}, f32[512,256]{1,0:T(8,128)S(1)}, u32[]{:S(2)}, u32[]{:S(2)}) collective-permute-start(f32[512,256]{1,0:T(8,128)S(1)} %bitcast.36), channel_id=1, source_target_pairs={{0,32},{32,0},{64,96},{96,64},{128,160},{160,128},{192,224},{224,1... | collective-permute-start | bytes 1572872 | tf_op jit(solution)/shard_map/ppermute | solution.py:47
  31.8 1.4 collective-permute-done.3
  33.4 0.2 collective-permute-done
  33.6 1.1 fusion
  34.7 16.3 %all_to_all.65 = f32[16,16,512]{2,1,0:T(8,128)S(1)} all-to-all(f32[16,16,512]{2,1,0:T(8,128)S(1)} %bitcast.44), channel_id=1, replica_groups={{0,1,2,3,64,65,66,67,128,129,130,131,192,193,194,195},{4,5,6,7,68,69,70..., dimensions={0} | all-to-all | bytes 1048576 | tf_op jit(solution)/shard_map/all_to_all | solution.py:37
  51.0 0.7 broadcast_in_dim.12
  51.7 3.4 %all-to-all-start.2 = ((f32[8,16,512]{2,1,0:T(8,128)}), f32[8,16,512]{2,1,0:T(8,128)S(1)}, u32[]{:S(2)}, u32[]{:S(2)}) async-start(f32[8,16,512]{2,1,0:T(8,128)} %broadcast_in_dim.12), calls=%async_computation.2 | async-start | bytes 524288 | tf_op jit(solution)/shard_map/all_to_all | solution.py:42
  55.1 1.3 constant_dynamic-slice_fusion.1
  56.4 2.1 %collective-permute-start.2 = (f32[3,256,256]{2,1,0:T(8,128)}, f32[3,256,256]{2,1,0:T(8,128)}, u32[]{:S(2)}, u32[]{:S(2)}) collective-permute-start(f32[3,256,256]{2,1,0:T(8,128)} %get-tuple-element.6), channel_id=1, source_target_pairs={{0,32},{32,0},{64,96},{96,64},{128,160},{160,128},{192,224},{224,1... | collective-permute-start | bytes 2359304 | tf_op jit(solution)/shard_map/ppermute | solution.py:33
  58.5 5.8 %all-to-all-done.2 = f32[8,16,512]{2,1,0:T(8,128)S(1)} async-done(((f32[8,16,512]{2,1,0:T(8,128)}), f32[8,16,512]{2,1,0:T(8,128)S(1)}, u32[]{:S(2)}, u32[]{:S(2)}) %all-to-all-start.2) | async-done | bytes 262176 | tf_op jit(solution)/shard_map/all_to_all | solution.py:42
  64.7 0.9 broadcast_in_dim.13
  65.6 4.4 %all-to-all-start.3 = ((f32[16,16,512]{2,1,0:T(8,128)}), f32[16,16,512]{2,1,0:T(8,128)S(1)}, u32[]{:S(2)}, u32[]{:S(2)}) async-start(f32[16,16,512]{2,1,0:T(8,128)} %broadcast_in_dim.13), calls=%async_computation.3 | async-start | bytes 1048576 | tf_op jit(solution)/shard_map/all_to_all | solution.py:37
  70.0 3.3 %collective-permute-start.1 = (f32[256]{0:T(256)S(1)}, f32[256]{0:T(256)S(1)}, u32[]{:S(2)}, u32[]{:S(2)}) collective-permute-start(f32[256]{0:T(256)S(1)} %copy-done.7), channel_id=1, source_target_pairs={{0,32},{32,0},{64,96},{96,64},{128,160},{160,128},{192,224},{224,1... | collective-permute-start | bytes 3080 | tf_op jit(solution)/shard_map/ppermute | solution.py:51
  73.3 0.8 collective-permute-done.1
  74.1 4.8 %all-to-all-done.3 = f32[16,16,512]{2,1,0:T(8,128)S(1)} async-done(((f32[16,16,512]{2,1,0:T(8,128)}), f32[16,16,512]{2,1,0:T(8,128)S(1)}, u32[]{:S(2)}, u32[]{:S(2)}) %all-to-all-start.3) | async-done | bytes 524320 | tf_op jit(solution)/shard_map/all_to_all | solution.py:37
  78.9 2.7 %fusion.13 = f32[256,512]{1,0:T(8,128)S(1)} fusion(f32[3,256,256]{2,1,0:T(8,128)S(1)} %copy-done.1, f32[3,256,256]{2,1,0:T(8,128)} %collective-permute-done.2, f32[256,256]{1,0:T(8,128)S(1)} %copy-done.6, f32[256,256]{1,0:T(8,128)S(1)} %get-tuple-element.9, f32[256,512]{1,0:T(8,128)S(1)} %bitcast.49, f32[512]{0:T(512)S(1)} %pad_maximum_fusion.5, ...), kind=kOutput, calls=%fused_computation.25 | convolution fusion | flops 807534592 | bytes 4196352 | tf_op jit(solution)/shard_map/dot_general | solution.py:87
  81.6 1.1 fusion.4
  82.7 12.2 %all_to_all.66 = f32[16,16,512]{2,1,0:T(8,128)S(1)} all-to-all(f32[16,16,512]{2,1,0:T(8,128)S(1)} %bitcast.45), channel_id=1, replica_groups={{0,1,2,3,64,65,66,67,128,129,130,131,192,193,194,195},{4,5,6,7,68,69,70..., dimensions={0} | all-to-all | bytes 1048576 | tf_op jit(solution)/shard_map/all_to_all | solution.py:37
  95.0 13.0 %all_to_all.67 = f32[8,16,512]{2,1,0:T(8,128)S(1)} all-to-all(f32[8,16,512]{2,1,0:T(8,128)S(1)} %broadcast_in_dim.14), channel_id=1, replica_groups={{0,4,8,12,16,20,24,28},{1,5,9,13,17,21,25,29},{2,6,10,14,18,22,26,30},{..., dimensions={0} | all-to-all | bytes 524288 | tf_op jit(solution)/shard_map/all_to_all | solution.py:42
  108.1 0.2 fusion.21
  108.4 12.1 %all_to_all.68 = f32[16,16,512]{2,1,0:T(8,128)S(1)} all-to-all(f32[16,16,512]{2,1,0:T(8,128)S(1)} %broadcast_in_dim.15), channel_id=1, replica_groups={{0,1,2,3,64,65,66,67,128,129,130,131,192,193,194,195},{4,5,6,7,68,69,70..., dimensions={0} | all-to-all | bytes 1048576 | tf_op jit(solution)/shard_map/all_to_all | solution.py:37
  120.6 2.7 %fusion.9 = f32[256,512]{1,0:T(8,128)S(1)} fusion(f32[3,256,256]{2,1,0:T(8,128)S(1)} %copy-done.1, f32[3,256,256]{2,1,0:T(8,128)} %collective-permute-done.2, f32[256,512]{1,0:T(8,128)S(1)} %copy-done.3, f32[256,512]{1,0:T(8,128)S(1)} %bitcast.51, f32[512]{0:T(512)S(1)} %pad_maximum_fusion.5, f32[512,256]{1,0:T(8,128)S(1)} %collective-permute-done.3, ...), kind=kOutput, calls=%fused_computation.21 | convolution fusion | flops 807796736 | bytes 4196352 | tf_op jit(solution)/shard_map/dot_general | solution.py:87
  123.3 1.1 fusion.3
  124.4 11.9 %all_to_all.69 = f32[16,16,512]{2,1,0:T(8,128)S(1)} all-to-all(f32[16,16,512]{2,1,0:T(8,128)S(1)} %bitcast.46), channel_id=1, replica_groups={{0,1,2,3,64,65,66,67,128,129,130,131,192,193,194,195},{4,5,6,7,68,69,70..., dimensions={0} | all-to-all | bytes 1048576 | tf_op jit(solution)/shard_map/all_to_all | solution.py:37
  136.4 11.7 %all_to_all.70 = f32[8,16,512]{2,1,0:T(8,128)S(1)} all-to-all(f32[8,16,512]{2,1,0:T(8,128)S(1)} %broadcast_in_dim.16), channel_id=1, replica_groups={{0,4,8,12,16,20,24,28},{1,5,9,13,17,21,25,29},{2,6,10,14,18,22,26,30},{..., dimensions={0} | all-to-all | bytes 524288 | tf_op jit(solution)/shard_map/all_to_all | solution.py:42
  148.6 11.9 %all_to_all.71 = f32[16,16,512]{2,1,0:T(8,128)S(1)} all-to-all(f32[16,16,512]{2,1,0:T(8,128)S(1)} %broadcast_in_dim.17), channel_id=1, replica_groups={{0,1,2,3,64,65,66,67,128,129,130,131,192,193,194,195},{4,5,6,7,68,69,70..., dimensions={0} | all-to-all | bytes 1048576 | tf_op jit(solution)/shard_map/all_to_all | solution.py:37
  160.5 2.7 %fusion.17 = f32[256,512]{1,0:T(8,128)S(1)} fusion(f32[3,256,256]{2,1,0:T(8,128)} %collective-permute-done.2, f32[3,256,256]{2,1,0:T(8,128)S(1)} %copy-done.1, f32[256,512]{1,0:T(8,128)S(1)} %fusion.9, f32[256,512]{1,0:T(8,128)S(1)} %bitcast.50, f32[512]{0:T(512)S(1)} %pad_maximum_fusion.5, f32[512,256]{1,0:T(8,128)S(1)} %collective-permute-done.3, ...), kind=kOutput, calls=%fused_computation.31 | convolution fusion | flops 807796736 | bytes 4196352 | tf_op jit(solution)/shard_map/dot_general | solution.py:87
  163.3 10.8 %collective-permute-start.4 = (f32[256,256]{1,0:T(8,128)S(1)}, f32[256,256]{1,0:T(8,128)S(1)}, u32[]{:S(2)}, u32[]{:S(2)}) collective-permute-start(f32[256,256]{1,0:T(8,128)S(1)} %slice.25), channel_id=1, source_target_pairs={{0,32},{32,0},{64,96},{96,64},{128,160},{160,128},{192,224},{224,1... | collective-permute-start | bytes 786440 | tf_op jit(solution)/shard_map/ppermute | solution.py:95
  174.0 1.2 collective-permute-done.4
  175.2 0.8 pad_maximum_fusion.3
  (42 shorter events, 1.7 us)
Async XLA Ops:
  0.0 31.7 %copy-start.4 = (f32[512,256]{1,0:T(8,128)S(1)}, f32[512,256]{1,0:T(8,128)}, u32[]{:S(2)}) copy-start(f32[512,256]{1,0:T(8,128)} %param.5) | copy-start | bytes 1572868
  29.3 3.9 %collective-permute-start.3 = (f32[512,256]{1,0:T(8,128)S(1)}, f32[512,256]{1,0:T(8,128)S(1)}, u32[]{:S(2)}, u32[]{:S(2)}) collective-permute-start(f32[512,256]{1,0:T(8,128)S(1)} %bitcast.36), channel_id=1, source_target_pairs={{0,32},{32,0},{64,96},{96,64},{128,160},{160,128},{192,224},{224,1... | collective-permute-start | bytes 1572872 | tf_op jit(solution)/shard_map/ppermute | solution.py:47
  31.7 1.9 %collective-permute-start = (f32[256,256]{1,0:T(8,128)S(1)}, f32[256,256]{1,0:T(8,128)S(1)}, u32[]{:S(2)}, u32[]{:S(2)}) collective-permute-start(f32[256,256]{1,0:T(8,128)S(1)} %get-tuple-element.10), channel_id=1, source_target_pairs={{0,32},{32,0},{64,96},{96,64},{128,160},{160,128},{192,224},{224,1... | collective-permute-start | bytes 786440 | tf_op jit(solution)/shard_map/ppermute | solution.py:33
  33.6 1.1 copy-start.5
  34.6 20.5 %copy-start = (f32[3,512,256]{2,1,0:T(8,128)S(1)}, f32[3,512,256]{2,1,0:T(8,128)}, u32[]{:S(2)}) copy-start(f32[3,512,256]{2,1,0:T(8,128)} %param.6) | copy-start | bytes 4718596
  51.7 12.6 %all-to-all-start.2 = ((f32[8,16,512]{2,1,0:T(8,128)}), f32[8,16,512]{2,1,0:T(8,128)S(1)}, u32[]{:S(2)}, u32[]{:S(2)}) async-start(f32[8,16,512]{2,1,0:T(8,128)} %broadcast_in_dim.12), calls=%async_computation.2 | async-start | bytes 524288 | tf_op jit(solution)/shard_map/all_to_all | solution.py:42
  56.4 13.5 %copy-start.7 = (f32[256]{0:T(256)S(1)}, f32[256]{0:T(256)}, u32[]{:S(2)}) copy-start(f32[256]{0:T(256)} %param.7) | copy-start | bytes 3076
  56.4 22.5 %copy-start.1 = (f32[3,256,256]{2,1,0:T(8,128)S(1)}, f32[3,256,256]{2,1,0:T(8,128)}, u32[]{:S(2)}) copy-start(f32[3,256,256]{2,1,0:T(8,128)} %get-tuple-element.5) | copy-start | bytes 2359300
  56.4 22.5 %copy-start.6 = (f32[256,256]{1,0:T(8,128)S(1)}, f32[256,256]{1,0:T(8,128)}, u32[]{:S(2)}) copy-start(f32[256,256]{1,0:T(8,128)} %copy-done.5) | copy-start | bytes 786436
  56.4 17.7 %collective-permute-start.2 = (f32[3,256,256]{2,1,0:T(8,128)}, f32[3,256,256]{2,1,0:T(8,128)}, u32[]{:S(2)}, u32[]{:S(2)}) collective-permute-start(f32[3,256,256]{2,1,0:T(8,128)} %get-tuple-element.6), channel_id=1, source_target_pairs={{0,32},{32,0},{64,96},{96,64},{128,160},{160,128},{192,224},{224,1... | collective-permute-start | bytes 2359304 | tf_op jit(solution)/shard_map/ppermute | solution.py:33
  65.6 13.3 %all-to-all-start.3 = ((f32[16,16,512]{2,1,0:T(8,128)}), f32[16,16,512]{2,1,0:T(8,128)S(1)}, u32[]{:S(2)}, u32[]{:S(2)}) async-start(f32[16,16,512]{2,1,0:T(8,128)} %broadcast_in_dim.13), calls=%async_computation.3 | async-start | bytes 1048576 | tf_op jit(solution)/shard_map/all_to_all | solution.py:37
  70.0 4.1 %collective-permute-start.1 = (f32[256]{0:T(256)S(1)}, f32[256]{0:T(256)S(1)}, u32[]{:S(2)}, u32[]{:S(2)}) collective-permute-start(f32[256]{0:T(256)S(1)} %copy-done.7), channel_id=1, source_target_pairs={{0,32},{32,0},{64,96},{96,64},{128,160},{160,128},{192,224},{224,1... | collective-permute-start | bytes 3080 | tf_op jit(solution)/shard_map/ppermute | solution.py:51
  81.6 1.1 copy-start.2
  94.9 25.7 %copy-start.3 = (f32[256,512]{1,0:T(8,128)S(1)}, f32[256,512]{1,0:T(8,128)}, u32[]{:S(2)}) copy-start(f32[256,512]{1,0:T(8,128)} %copy-done.2) | copy-start | bytes 1572868
  163.3 11.9 %collective-permute-start.4 = (f32[256,256]{1,0:T(8,128)S(1)}, f32[256,256]{1,0:T(8,128)S(1)}, u32[]{:S(2)}, u32[]{:S(2)}) collective-permute-start(f32[256,256]{1,0:T(8,128)S(1)} %slice.25), channel_id=1, source_target_pairs={{0,32},{32,0},{64,96},{96,64},{128,160},{160,128},{192,224},{224,1... | collective-permute-start | bytes 786440 | tf_op jit(solution)/shard_map/ppermute | solution.py:95

commit v3 on v2

v3 whole, which is shorter than its diff:
```python
import math

import jax
import jax.numpy as jnp
from jax import lax
from jax.sharding import PartitionSpec as P

ITERS = 3
DEPTH = 8
AXES = ("space", "mem")


def constants(step):
    t = 1.0 - step / ITERS
    dt = 1.0 / ITERS
    alpha = 1.0 - 0.5 * t
    drift = -0.5 / alpha
    g2 = 1.0 + t / alpha
    damp = 1.0 - t
    keep = 1.0 - dt * drift - dt * g2 / t
    gain = dt * g2 * alpha / t
    pull = dt * g2 * damp * 4.0
    noise = math.sqrt(dt * g2)
    return alpha, t, keep, gain, pull, noise


def product(a, b, contract):
    return lax.dot_general(
        a,
        b,
        (contract, ((), ())),
        precision=lax.Precision.HIGHEST,
        preferred_element_type=jnp.float32,
    )


def half(array, which, axis):
    size = array.shape[axis] // 2
    return lax.dynamic_slice_in_dim(array, which * size, size, axis)


def per_device(prior_ensemble, terminal_particles, reverse_perturbation, measured_angles):
    space, mem = lax.axis_size("space"), lax.axis_size("mem")
    core = lax.rem(lax.axis_index("space"), 2)
    swap = [(i, i ^ 1) for i in range(space)]
    width = mem // DEPTH
    planes = [
        [s * mem + z * width + y for s in range(c, space, 2) for y in range(width)]
        for c in range(2)
        for z in range(DEPTH)
    ]
    columns = [[z * width + y for z in range(DEPTH)] for y in range(width)]
    peers = len(planes[0])

    def other_core(array):
        return lax.ppermute(array, "space", swap)

    def pair_up(array):
        return jnp.concatenate(
            [half(array, core, 0), other_core(half(array, 1 - core, 0))], axis=1
        )

    def in_plane(blocks):
        return lax.all_to_all(
            blocks, AXES, split_axis=0, concat_axis=0, axis_index_groups=planes
        )

    def column_sum(block):
        spread = jnp.broadcast_to(block[None], (DEPTH,) + block.shape)
        return jnp.sum(
            lax.all_to_all(
                spread, "mem", split_axis=0, concat_axis=0, axis_index_groups=columns
            ),
            axis=0,
        )

    def to_all(block):
        return jnp.broadcast_to(block[None], (peers,) + block.shape)

    temper = math.sqrt(measured_angles.shape[0] * space * mem)
    a0, t0, keep0, gain0, pull0, noise0 = constants(0)
    a1, t1, keep1, gain1, pull1, noise1 = constants(1)
    a2, t2, keep2, gain2, pull2, noise2 = constants(2)

    z0 = pair_up(terminal_particles)
    e0, e1, e2 = (pair_up(reverse_perturbation[step]) for step in range(ITERS))
    angles = jnp.concatenate([measured_angles, other_core(measured_angles)])[None, :]

    def misfit(z):
        return (angles - jnp.arctan(z)) / (1.0 + z * z)

    u0 = keep0 * z0 + pull0 * misfit(z0) + noise0 * e0

    own = lax.all_to_all(prior_ensemble, "mem", split_axis=1, concat_axis=0, tiled=True)
    members = jnp.concatenate([own, other_core(own)], axis=1)
    count, total = z0.shape[0], members.shape[0]
    rows = count // peers

    def by_row_owner(array):
        return array.reshape(peers, rows, array.shape[-1])

    lengths = jnp.sum(members * members, axis=1)[None, None, :]
    stack = jnp.concatenate(
        [by_row_owner(z0), by_row_owner(u0), by_row_owner(half(members, core, 0))],
        axis=1,
    )
    partial = product(
        stack.reshape(3 * count, -1), members, ((1,), (1,))
    ).reshape(peers, 3, rows, total)
    partial = jnp.stack(
        [
            2.0 * a0 * partial[:, 0] - a0 * a0 * lengths,
            2.0 * a1 * partial[:, 1] - a1 * a1 * lengths,
            partial[:, 2],
        ],
        axis=1,
    )
    sums = column_sum(jnp.sum(in_plane(partial), axis=0))
    raw0, raw1, pairs = sums[0], sums[1], sums[2]
    w0 = jax.nn.softmax(raw0 / (2.0 * t0 * temper), axis=1)
    got = in_plane(to_all(jnp.stack([w0, pairs])))
    weights0 = got[:, 0].reshape(count, total)
    near = got[:, 1].reshape(count, total)
    far = other_core(near)

    z1 = u0 + gain0 * product(weights0, members, ((1,), (0,)))
    v1 = pull1 * misfit(z1) + noise1 * e1
    v1_members = product(v1, members, ((1,), (1,)))

    def times_pairs(w):
        return product(half(w, core, 1), near, ((1,), (0,))) + product(
            half(w, 1 - core, 1), far, ((1,), (0,))
        )

    w0_pairs = times_pairs(w0)
    raw1 = raw1 + (2.0 * a1 * gain0) * w0_pairs
    w1 = jax.nn.softmax(raw1 / (2.0 * t1 * temper), axis=1)

    partial = by_row_owner(
        2.0 * a2 * v1_members + (a2 * keep1 * a1 - a2 * a2) * lengths[0]
    )
    got = in_plane(jnp.stack([partial, to_all(w1)], axis=1))
    weights1 = got[:, 1].reshape(count, total)
    raw2 = column_sum(jnp.sum(got[:, 0], axis=0))
    raw2 = raw2 + (a2 * keep1 / a1) * raw1 + (2.0 * a2 * gain1) * times_pairs(w1)
    w2 = jax.nn.softmax(raw2 / (2.0 * t2 * temper), axis=1)
    weights2 = in_plane(to_all(w2)).reshape(count, total)

    z2 = keep1 * z1 + v1 + gain1 * product(weights1, members, ((1,), (0,)))
    u2 = keep2 * z2 + pull2 * misfit(z2) + noise2 * e2
    u2 = lax.optimization_barrier(u2)
    z3 = u2 + gain2 * product(weights2, members, ((1,), (0,)))

    mine = measured_angles.shape[0]
    kept, back = z3[:, :mine], other_core(z3[:, mine:])
    first = core == 0
    return jnp.concatenate(
        [jnp.where(first, kept, back), jnp.where(first, back, kept)], axis=0
    )


def solution(mesh):
    in_specs = (
        P("mem", "space"),
        P(None, ("space", "mem")),
        P(None, None, ("space", "mem")),
        P(("space", "mem")),
    )
    out_specs = P(None, ("space", "mem"))
    return jax.shard_map(
        per_device, mesh=mesh, in_specs=in_specs, out_specs=out_specs, check_vma=False
    )
```

time: 177 us -> 178 us (level)
  blocking collectives: 117 us -> 68.4 us
  waiting for transfers between devices: 14.2 us -> 35.5 us
  starting transfers between devices: 26.4 us -> 43.8 us
  local copies, waits for them, and re-layouts: 4.25 us -> 8.43 us
  matrix products: 11.3 us -> 15 us
  other arithmetic: 2.39 us -> 5.91 us
    all_to_all x3 -> x1, blocking collectives: 52.9 us -> 22.5 us  [column_sum(): lax.all_to_all(spread, 'mem', split_axis=0, concat_axis=0, axis_index_gro...]
    all_to_all x5 -> x2, blocking collectives: 64.5 us -> 45.9 us  [in_plane(): lax.all_to_all(blocks, AXES, split_axis=0, concat_axis=0, axis_index_grou...]
    all_to_all x1 -> x2, waiting for transfers between devices: 5.77 us -> 18.8 us  [the longest x1 12.9 us: per_device(): lax.all_to_all(prior_ensemble, 'mem', split_axis=1, concat_axis=0, tiled=...]
    all_to_all x1 -> x2, starting transfers between devices: 3.41 us -> 15.4 us  [the longest x1 12 us: per_device(): lax.all_to_all(prior_ensemble, 'mem', split_axis=1, concat_axis=0, tiled=...]
    all_to_all x1 -> x2, waiting for transfers between devices: 4.82 us -> 15.5 us  [in_plane(): lax.all_to_all(blocks, AXES, split_axis=0, concat_axis=0, axis_index_grou...]
    all_to_all x1 -> x2, starting transfers between devices: 4.39 us -> 10.7 us  [in_plane(): lax.all_to_all(blocks, AXES, split_axis=0, concat_axis=0, axis_index_grou...]
    dot_general x6 -> x9, matrix products: 11.3 us -> 15 us  [product(): lax.dot_general(a, b, (contract, ((), ())), precision=lax.Precision.HIGHE...]
    ppermute x5 -> x8, waiting for transfers between devices: 3.59 us -> 1.18 us  [other_core(): return lax.ppermute(array, 'space', swap)]
  transfers between devices with their start and end apart: 7 -> 12, of which waited for: 6 -> 5; matrix products, arithmetic and copies ran while one was open for 2% -> 10% of each run, Pallas kernels for 0% -> 0%
where the time goes in v3:
time: 178 us; the launch traced here: 177 us
  blocking collectives  68.4 us (38%)
  starting transfers between devices  43.8 us (25%)
  waiting for transfers between devices  35.5 us (20%)
  matrix products  15 us (8%)
  local copies, waits for them, and re-layouts  8.43 us (5%)
  other arithmetic  5.91 us (3%)
    all_to_all x2, blocking collectives, in_plane(): lax.all_to_all(blocks, AXES, split_axis=0, concat_axis=0, axis_index_grou...  45.9 us
    all_to_all x1, blocking collectives, column_sum(): lax.all_to_all(spread, 'mem', split_axis=0, concat_axis=0, axis_index_gro...  22.5 us
    ppermute x8, starting transfers between devices, other_core(): return lax.ppermute(array, 'space', swap)  17.6 us
    all_to_all x2, waiting for transfers between devices, in_plane(): lax.all_to_all(blocks, AXES, split_axis=0, concat_axis=0, axis_index_grou...  15.5 us
    dot_general x9, matrix products, product(): lax.dot_general(a, b, (contract, ((), ())), precision=lax.Precision.HIGHE...  15 us
    all_to_all x1, waiting for transfers between devices, per_device(): lax.all_to_all(prior_ensemble, 'mem', split_axis=1, concat_axis=0, tiled=...  12.9 us
    all_to_all x1, starting transfers between devices, per_device(): lax.all_to_all(prior_ensemble, 'mem', split_axis=1, concat_axis=0, tiled=...  12 us
    all_to_all x2, starting transfers between devices, in_plane(): lax.all_to_all(blocks, AXES, split_axis=0, concat_axis=0, axis_index_grou...  10.7 us
  transfers between devices with their start and end apart: 12, of which 5 were waited for; matrix products, arithmetic and copies ran while one was open for 10% of the time, Pallas kernels for 0%

profile of v3, /device:TPU:1, one launch (start us, length us, event | category | flops | bytes accessed | tf_op | source)
XLA Modules:
  0.0 177.4 jit_solution(6389309455605618132)
XLA Ops:
  0.0 2.1 %copy.13 = f32[2,32,8,256]{3,2,0,1:T(8,128)} copy(f32[2,32,8,256]{3,2,1,0:T(8,128)} %bitcast.76) | data formatting | bytes 1048576 | tf_op jit(solution)/shard_map/all_to_all | solution.py:94
  2.1 12.0 %all-to-all-start = ((f32[16,32,256]{2,0,1:T(8,128)}), f32[16,32,256]{2,0,1:T(8,128)S(1)}, u32[]{:S(2)}, u32[]{:S(2)}) async-start(f32[16,32,256]{2,0,1:T(8,128)} %bitcast.56), calls=%async_computation | async-start | bytes 1048576 | tf_op jit(solution)/shard_map/all_to_all | solution.py:94
  14.1 1.0 collective-permute-start.1
  15.9 0.9 fusion.35
  17.4 12.9 %all-to-all-done = f32[16,32,256]{2,0,1:T(8,128)S(1)} async-done(((f32[16,32,256]{2,0,1:T(8,128)}), f32[16,32,256]{2,0,1:T(8,128)S(1)}, u32[]{:S(2)}, u32[]{:S(2)}) %all-to-all-start) | async-done | bytes 524320 | tf_op jit(solution)/shard_map/all_to_all | solution.py:94
  30.4 2.4 %collective-permute-start.3 = (f32[512,256]{1,0:T(8,128)S(1)}, f32[512,256]{1,0:T(8,128)S(1)}, u32[]{:S(2)}, u32[]{:S(2)}) collective-permute-start(f32[512,256]{1,0:T(8,128)S(1)} %bitcast.57), channel_id=1, source_target_pairs={{0,32},{32,0},{64,96},{96,64},{128,160},{160,128},{192,224},{224,1... | collective-permute-start | bytes 1572872 | tf_op jit(solution)/shard_map/ppermute | solution.py:56
  32.8 1.0 pad_maximum_fusion.4
  33.8 1.8 maximum_add_fusion.1
  36.0 2.7 %fusion.4 = f32[16,3,16,512]{3,2,1,0:T(8,128)S(1)} fusion(f32[16,3,16,512]{3,2,1,0:T(8,128)S(1)} %bitcast.65, f32[512,256]{1,0:T(8,128)S(1)} %collective-permute-done.3, f32[512,256]{1,0:T(8,128)S(1)} %bitcast.60), kind=kOutput, calls=%fused_computation.16 | convolution fusion | flops 2416181248 | bytes 4194304 | tf_op jit(solution)/shard_map/dot_general | solution.py:28
  39.1 27.1 %all_to_all.49 = f32[16,3,16,512]{3,2,1,0:T(8,128)S(1)} all-to-all(f32[16,3,16,512]{3,2,1,0:T(8,128)S(1)} %pad_maximum_fusion.1), channel_id=1, replica_groups={{0,1,2,3,64,65,66,67,128,129,130,131,192,193,194,195},{4,5,6,7,68,69,70..., dimensions={0} | all-to-all | bytes 3145728 | tf_op jit(solution)/shard_map/all_to_all | solution.py:64
  66.5 22.5 %all_to_all.50 = f32[8,3,16,512]{3,2,1,0:T(8,128)S(1)} all-to-all(f32[8,3,16,512]{3,2,1,0:T(8,128)S(1)} %broadcast_in_dim.8), channel_id=1, replica_groups={{0,4,8,12,16,20,24,28},{1,5,9,13,17,21,25,29},{2,6,10,14,18,22,26,30},{..., dimensions={0} | all-to-all | bytes 1572864 | tf_op jit(solution)/shard_map/all_to_all | solution.py:71
  89.5 1.1 broadcast_in_dim.9
  90.6 5.7 %all-to-all-start.3 = ((f32[16,2,16,512]{3,2,1,0:T(8,128)}), f32[16,2,16,512]{3,2,1,0:T(8,128)S(1)}, u32[]{:S(2)}, u32[]{:S(2)}) async-start(f32[16,2,16,512]{3,2,1,0:T(8,128)} %broadcast_in_dim.9), calls=%async_computation.3 | async-start | bytes 2097152 | tf_op jit(solution)/shard_map/all_to_all | solution.py:64
  96.3 0.9 dynamic-slice_bitcast_fusion.3
  97.1 3.0 %collective-permute-start.4 = (f32[256,256]{1,0:T(8,128)}, f32[256,256]{1,0:T(8,128)}, u32[]{:S(2)}, u32[]{:S(2)}) collective-permute-start(f32[256,256]{1,0:T(8,128)} %get-tuple-element.18), channel_id=1, source_target_pairs={{0,32},{32,0},{64,96},{96,64},{128,160},{160,128},{192,224},{224,1... | collective-permute-start | bytes 786440 | tf_op jit(solution)/shard_map/ppermute | solution.py:56
  100.2 10.3 %all-to-all-done.3 = f32[16,2,16,512]{3,2,1,0:T(8,128)S(1)} async-done(((f32[16,2,16,512]{3,2,1,0:T(8,128)}), f32[16,2,16,512]{3,2,1,0:T(8,128)S(1)}, u32[]{:S(2)}, u32[]{:S(2)}) %all-to-all-start.3) | async-done | bytes 1048608 | tf_op jit(solution)/shard_map/all_to_all | solution.py:64
  110.7 4.1 %collective-permute-start.5 = (f32[256,512]{1,0:T(8,128)S(1)}, f32[256,512]{1,0:T(8,128)S(1)}, u32[]{:S(2)}, u32[]{:S(2)}) collective-permute-start(f32[256,512]{1,0:T(8,128)S(1)} %bitcast.66), channel_id=1, source_target_pairs={{0,32},{32,0},{64,96},{96,64},{128,160},{160,128},{192,224},{224,1... | collective-permute-start | bytes 1572872 | tf_op jit(solution)/shard_map/ppermute | solution.py:56
  115.2 2.8 %fusion.8 = f32[256,512]{1,0:T(8,128)S(1)} fusion(f32[256,256]{1,0:T(8,128)} %copy-done.5, f32[256,256]{1,0:T(8,128)} %bitcast.74, f32[256,512]{1,0:T(8,128)S(1)} %bitcast.78, f32[512]{0:T(512)S(1)} %constant_dynamic-update-slice_fusion, f32[512,256]{1,0:T(8,128)S(1)} %collective-permute-done.3, f32[512,256]{1,0:T(8,128)S(1)} %bitcast.61, ...), kind=kOutput, calls=%fused_computation.27 | convolution fusion | flops 807141376 | bytes 3147776 | tf_op jit(solution)/shard_map/dot_general | solution.py:28
  118.0 2.9 %fusion = f32[256,512]{1,0:T(8,128)S(1)} fusion(f32[512]{0:T(512)S(1)} %get-tuple-element.27, f32[512,256]{1,0:T(8,128)S(1)} %collective-permute-done.3, f32[512,256]{1,0:T(8,128)S(1)} %bitcast.62, f32[256,256]{1,0:T(8,128)} %collective-permute-done.4, f32[256,256]{1,0:T(8,128)S(1)} %copy-done.4, f32[256,512]{1,0:T(8,128)S(1)} %fusion.8, ...), kind=kOutput, calls=%fused_computation.9 | convolution fusion | flops 806879232 | bytes 2625536 | tf_op jit(solution)/shard_map/dot_general | solution.py:28
  121.9 18.8 %all_to_all.51 = f32[16,2,16,512]{3,2,1,0:T(8,128)S(1)} all-to-all(f32[16,2,16,512]{3,2,1,0:T(8,128)S(1)} %pad_maximum_fusion.3), channel_id=1, replica_groups={{0,1,2,3,64,65,66,67,128,129,130,131,192,193,194,195},{4,5,6,7,68,69,70..., dimensions={0} | all-to-all | bytes 2097152 | tf_op jit(solution)/shard_map/all_to_all | solution.py:64
  141.5 3.4 %all-to-all-start.5 = ((f32[8,16,512]{2,1,0:T(8,128)}), f32[8,16,512]{2,1,0:T(8,128)S(1)}, u32[]{:S(2)}, u32[]{:S(2)}) async-start(f32[8,16,512]{2,1,0:T(8,128)} %broadcast_in_dim.10), calls=%async_computation.5 | async-start | bytes 524288 | tf_op jit(solution)/shard_map/all_to_all | solution.py:71
  145.0 0.8 dynamic-slice_bitcast_fusion.1
  145.8 2.3 %collective-permute-start.6 = (f32[256,256]{1,0:T(8,128)}, f32[256,256]{1,0:T(8,128)}, u32[]{:S(2)}, u32[]{:S(2)}) collective-permute-start(f32[256,256]{1,0:T(8,128)} %get-tuple-element.24), channel_id=1, source_target_pairs={{0,32},{32,0},{64,96},{96,64},{128,160},{160,128},{192,224},{224,1... | collective-permute-start | bytes 786440 | tf_op jit(solution)/shard_map/ppermute | solution.py:56
  148.5 5.9 %all-to-all-done.5 = f32[8,16,512]{2,1,0:T(8,128)S(1)} async-done(((f32[8,16,512]{2,1,0:T(8,128)}), f32[8,16,512]{2,1,0:T(8,128)S(1)}, u32[]{:S(2)}, u32[]{:S(2)}) %all-to-all-start.5) | async-done | bytes 262176 | tf_op jit(solution)/shard_map/all_to_all | solution.py:71
  155.1 0.9 broadcast_in_dim.11
  156.0 5.1 %all-to-all-start.6 = ((f32[16,16,512]{2,1,0:T(8,128)}), f32[16,16,512]{2,1,0:T(8,128)S(1)}, u32[]{:S(2)}, u32[]{:S(2)}) async-start(f32[16,16,512]{2,1,0:T(8,128)} %broadcast_in_dim.11), calls=%async_computation.6 | async-start | bytes 1048576 | tf_op jit(solution)/shard_map/all_to_all | solution.py:64
  161.1 3.8 %fusion.10 = f32[256,512]{1,0:T(8,128)S(1)} fusion(f32[256,256]{1,0:T(8,128)} %collective-permute-done.6, f32[256,256]{1,0:T(8,128)} %get-tuple-element.23, f32[256,512]{1,0:T(8,128)} %copy-done.9, f32[256,512]{1,0:T(8,128)S(1)} %bitcast.75, f32[512]{0:T(512)S(1)} %constant_dynamic-update-slice_fusion, f32[512,256]{1,0:T(8,128)S(1)} %collective-permute-done.3, ...), kind=kOutput, calls=%fused_computation.33 | convolution fusion | flops 808452096 | bytes 3672064 | tf_op jit(solution)/shard_map/dot_general | solution.py:28
  164.9 5.1 %all-to-all-done.6 = f32[16,16,512]{2,1,0:T(8,128)S(1)} async-done(((f32[16,16,512]{2,1,0:T(8,128)}), f32[16,16,512]{2,1,0:T(8,128)S(1)}, u32[]{:S(2)}, u32[]{:S(2)}) %all-to-all-start.6) | async-done | bytes 524320 | tf_op jit(solution)/shard_map/all_to_all | solution.py:64
  170.0 1.1 convolution_multiply_fusion
  171.2 4.2 %collective-permute-start.7 = (f32[256,256]{1,0:T(8,128)S(1)}, f32[256,256]{1,0:T(8,128)S(1)}, u32[]{:S(2)}, u32[]{:S(2)}) collective-permute-start(f32[256,256]{1,0:T(8,128)S(1)} %slice.71), channel_id=1, source_target_pairs={{0,32},{32,0},{64,96},{96,64},{128,160},{160,128},{192,224},{224,1... | collective-permute-start | bytes 786440 | tf_op jit(solution)/shard_map/ppermute | solution.py:56
  175.4 1.2 collective-permute-done.7
  176.6 0.8 pad_maximum_fusion.6
  (65 shorter events, 6.5 us)
Async XLA Ops:
  0.0 14.1 %copy-start.8 = (f32[256]{0:T(256)S(1)}, f32[256]{0:T(256)}, u32[]{:S(2)}) copy-start(f32[256]{0:T(256)} %param.7) | copy-start | bytes 3076
  0.0 15.2 %copy-start.3 = (f32[512,256]{1,0:T(8,128)S(1)}, f32[512,256]{1,0:T(8,128)}, u32[]{:S(2)}) copy-start(f32[512,256]{1,0:T(8,128)} %param.5) | copy-start | bytes 1572868
  0.0 15.9 %copy-start.1 = (f32[3,512,256]{2,1,0:T(8,128)S(1)}, f32[3,512,256]{2,1,0:T(8,128)}, u32[]{:S(2)}) copy-start(f32[3,512,256]{2,1,0:T(8,128)} %param.6) | copy-start | bytes 4718596
  2.1 28.3 %all-to-all-start = ((f32[16,32,256]{2,0,1:T(8,128)}), f32[16,32,256]{2,0,1:T(8,128)S(1)}, u32[]{:S(2)}, u32[]{:S(2)}) async-start(f32[16,32,256]{2,0,1:T(8,128)} %bitcast.56), calls=%async_computation | async-start | bytes 1048576 | tf_op jit(solution)/shard_map/all_to_all | solution.py:94
  14.1 18.7 %collective-permute-start.1 = (f32[256]{0:T(256)S(1)}, f32[256]{0:T(256)S(1)}, u32[]{:S(2)}, u32[]{:S(2)}) collective-permute-start(f32[256]{0:T(256)S(1)} %copy-done.8), channel_id=1, source_target_pairs={{0,32},{32,0},{64,96},{96,64},{128,160},{160,128},{192,224},{224,1... | collective-permute-start | bytes 3080 | tf_op jit(solution)/shard_map/ppermute | solution.py:56
  15.9 16.9 %collective-permute-start = (f32[256,256]{1,0:T(8,128)}, f32[256,256]{1,0:T(8,128)}, u32[]{:S(2)}, u32[]{:S(2)}) collective-permute-start(f32[256,256]{1,0:T(8,128)} %get-tuple-element.20), channel_id=1, source_target_pairs={{0,32},{32,0},{64,96},{96,64},{128,160},{160,128},{192,224},{224,1... | collective-permute-start | bytes 786440 | tf_op jit(solution)/shard_map/ppermute | solution.py:56
  16.9 18.9 %copy-start.2 = (f32[1,256,256]{2,1,0:T(8,128)}, f32[1,256,256]{2,1,0:T(8,128)S(1)}, u32[]{:S(2)}) copy-start(f32[1,256,256]{2,1,0:T(8,128)S(1)} %get-tuple-element.21) | copy-start | bytes 786436
  16.9 16.9 %collective-permute-start.2 = (f32[256,256]{1,0:T(8,128)S(1)}, f32[256,256]{1,0:T(8,128)S(1)}, u32[]{:S(2)}, u32[]{:S(2)}) collective-permute-start(f32[256,256]{1,0:T(8,128)S(1)} %get-tuple-element.22), channel_id=1, source_target_pairs={{0,32},{32,0},{64,96},{96,64},{128,160},{160,128},{192,224},{224,1... | collective-permute-start | bytes 786440 | tf_op jit(solution)/shard_map/ppermute | solution.py:56
  30.4 5.2 %collective-permute-start.3 = (f32[512,256]{1,0:T(8,128)S(1)}, f32[512,256]{1,0:T(8,128)S(1)}, u32[]{:S(2)}, u32[]{:S(2)}) collective-permute-start(f32[512,256]{1,0:T(8,128)S(1)} %bitcast.57), channel_id=1, source_target_pairs={{0,32},{32,0},{64,96},{96,64},{128,160},{160,128},{192,224},{224,1... | collective-permute-start | bytes 1572872 | tf_op jit(solution)/shard_map/ppermute | solution.py:56
  33.8 2.0 %copy-start.5 = (f32[256,256]{1,0:T(8,128)}, f32[256,256]{1,0:T(8,128)S(1)}, u32[]{:S(2)}) copy-start(f32[256,256]{1,0:T(8,128)S(1)} %collective-permute-done.2) | copy-start | bytes 786436
  89.5 6.8 %copy-start = (f32[1,512,256]{2,1,0:T(8,128)S(1)}, f32[1,512,256]{2,1,0:T(8,128)}, u32[]{:S(2)}) copy-start(f32[1,512,256]{2,1,0:T(8,128)} %get-tuple-element.5) | copy-start | bytes 1572868
  90.6 20.0 %all-to-all-start.3 = ((f32[16,2,16,512]{3,2,1,0:T(8,128)}), f32[16,2,16,512]{3,2,1,0:T(8,128)S(1)}, u32[]{:S(2)}, u32[]{:S(2)}) async-start(f32[16,2,16,512]{3,2,1,0:T(8,128)} %broadcast_in_dim.9), calls=%async_computation.3 | async-start | bytes 2097152 | tf_op jit(solution)/shard_map/all_to_all | solution.py:64
  97.1 20.9 %collective-permute-start.4 = (f32[256,256]{1,0:T(8,128)}, f32[256,256]{1,0:T(8,128)}, u32[]{:S(2)}, u32[]{:S(2)}) collective-permute-start(f32[256,256]{1,0:T(8,128)} %get-tuple-element.18), channel_id=1, source_target_pairs={{0,32},{32,0},{64,96},{96,64},{128,160},{160,128},{192,224},{224,1... | collective-permute-start | bytes 786440 | tf_op jit(solution)/shard_map/ppermute | solution.py:56
  100.2 17.8 %copy-start.6 = (f32[16,512]{1,0:T(8,128)}, f32[16,512]{1,0:T(8,128)S(1)}, u32[]{:S(2)}) copy-start(f32[16,512]{1,0:T(8,128)S(1)} %fusion.14) | copy-start | bytes 98308
  110.7 10.3 %collective-permute-start.5 = (f32[256,512]{1,0:T(8,128)S(1)}, f32[256,512]{1,0:T(8,128)S(1)}, u32[]{:S(2)}, u32[]{:S(2)}) collective-permute-start(f32[256,512]{1,0:T(8,128)S(1)} %bitcast.66), channel_id=1, source_target_pairs={{0,32},{32,0},{64,96},{96,64},{128,160},{160,128},{192,224},{224,1... | collective-permute-start | bytes 1572872 | tf_op jit(solution)/shard_map/ppermute | solution.py:56
  115.2 2.9 %copy-start.4 = (f32[256,256]{1,0:T(8,128)S(1)}, f32[256,256]{1,0:T(8,128)}, u32[]{:S(2)}) copy-start(f32[256,256]{1,0:T(8,128)} %get-tuple-element.17) | copy-start | bytes 786436
  118.0 3.0 %copy-start.9 = (f32[256,512]{1,0:T(8,128)}, f32[256,512]{1,0:T(8,128)S(1)}, u32[]{:S(2)}) copy-start(f32[256,512]{1,0:T(8,128)S(1)} %fusion.8) | copy-start | bytes 1572868
  118.0 3.0 %copy-start.7 = (f32[16,512]{1,0:T(8,128)S(1)}, f32[16,512]{1,0:T(8,128)}, u32[]{:S(2)}) copy-start(f32[16,512]{1,0:T(8,128)} %copy-done.6) | copy-start | bytes 98308
  141.5 12.8 %all-to-all-start.5 = ((f32[8,16,512]{2,1,0:T(8,128)}), f32[8,16,512]{2,1,0:T(8,128)S(1)}, u32[]{:S(2)}, u32[]{:S(2)}) async-start(f32[8,16,512]{2,1,0:T(8,128)} %broadcast_in_dim.10), calls=%async_computation.5 | async-start | bytes 524288 | tf_op jit(solution)/shard_map/all_to_all | solution.py:71
  145.8 15.3 %collective-permute-start.6 = (f32[256,256]{1,0:T(8,128)}, f32[256,256]{1,0:T(8,128)}, u32[]{:S(2)}, u32[]{:S(2)}) collective-permute-start(f32[256,256]{1,0:T(8,128)} %get-tuple-element.24), channel_id=1, source_target_pairs={{0,32},{32,0},{64,96},{96,64},{128,160},{160,128},{192,224},{224,1... | collective-permute-start | bytes 786440 | tf_op jit(solution)/shard_map/ppermute | solution.py:56
  156.0 14.0 %all-to-all-start.6 = ((f32[16,16,512]{2,1,0:T(8,128)}), f32[16,16,512]{2,1,0:T(8,128)S(1)}, u32[]{:S(2)}, u32[]{:S(2)}) async-start(f32[16,16,512]{2,1,0:T(8,128)} %broadcast_in_dim.11), calls=%async_computation.6 | async-start | bytes 1048576 | tf_op jit(solution)/shard_map/all_to_all | solution.py:64
  171.2 5.3 %collective-permute-start.7 = (f32[256,256]{1,0:T(8,128)S(1)}, f32[256,256]{1,0:T(8,128)S(1)}, u32[]{:S(2)}, u32[]{:S(2)}) collective-permute-start(f32[256,256]{1,0:T(8,128)S(1)} %slice.71), channel_id=1, source_target_pairs={{0,32},{32,0},{64,96},{96,64},{128,160},{160,128},{192,224},{224,1... | collective-permute-start | bytes 786440 | tf_op jit(solution)/shard_map/ppermute | solution.py:56

commit v4 on v2

--- a/solution.py
+++ b/solution.py
@@ -7,6 +7,16 @@
 
 ITERS = 3
 AXES = ("space", "mem")
+
+
+def product(a, b, axis):
+    return lax.dot_general(
+        a,
+        b,
+        (((1,), (axis,)), ((), ())),
+        precision=lax.Precision.HIGHEST,
+        preferred_element_type=jnp.float32,
+    )
 
 
 def half(array, which, axis):
@@ -27,11 +37,6 @@
     ]
     columns = [[z * width + y for z in range(depth)] for y in range(width)]
     peers = len(planes[0])
-    precision = lax.Precision.HIGHEST
-
-    def pair_up(array, axis):
-        other = lax.ppermute(half(array, 1 - core, axis), "space", swap)
-        return jnp.concatenate([half(array, core, axis), other], axis=-1)
 
     def in_plane(blocks):
         return lax.all_to_all(
@@ -44,12 +49,16 @@
         )
 
     own = lax.all_to_all(prior_ensemble, "mem", split_axis=1, concat_axis=0, tiled=True)
-    members = jnp.concatenate([own, lax.ppermute(own, "space", swap)], axis=1)
-    particles = pair_up(terminal_particles, 0)
-    perturbation = pair_up(reverse_perturbation, 1)
+    samples = jnp.concatenate([terminal_particles[None], reverse_perturbation[:-1]])
+    other = lax.ppermute(half(samples, 1 - core, 1), "space", swap)
+    samples = jnp.concatenate([half(samples, core, 1), other], axis=-1)
     angles = jnp.concatenate(
         [measured_angles, lax.ppermute(measured_angles, "space", swap)]
     )
+    own, samples, angles = lax.optimization_barrier((own, samples, angles))
+    particles, perturbation = samples[0], samples[1:]
+    far_members = lax.ppermute(own, "space", swap)
+    members = jnp.concatenate([own, far_members], axis=1)
     temper = math.sqrt(measured_angles.shape[0] * space * mem)
     lengths = jnp.sum(members * members, axis=1)
 
@@ -63,13 +72,7 @@
         drift = -0.5 / alpha
         g2 = 1.0 + t / alpha
         damp = 1.0 - t
-        gram = jnp.einsum(
-            "sv,mv->sm",
-            z,
-            members,
-            precision=precision,
-            preferred_element_type=jnp.float32,
-        )
+        gram = product(z, members, 1)
         partial = (2.0 * alpha * gram - alpha * alpha * lengths[None, :]) / (
             2.0 * t * temper
         )
@@ -79,24 +82,27 @@
         weights = jax.nn.softmax(logits, axis=1)
         weights = in_plane(jnp.broadcast_to(weights[None], (peers, rows, total)))
         pull = damp * 4.0 * (angles[None, :] - jnp.arctan(z)) / (1.0 + z * z)
-        rest = (
-            z
-            + dt * (-drift * z + g2 * (pull - z / t))
+        rest = z + dt * (-drift * z + g2 * (pull - z / t))
+        weights = weights.reshape(count, total)
+        if step == ITERS - 1:
+            break
+        blend = product(weights, members, 0)
+        z = (
+            rest
             + math.sqrt(dt * g2) * perturbation[step]
+            + (dt * g2 * alpha / t) * blend
         )
-        blend = jnp.dot(
-            weights.reshape(count, total),
-            members,
-            precision=precision,
-            preferred_element_type=jnp.float32,
+    mine = measured_angles.shape[0]
+    scale = dt * g2 * alpha / t
+    far = rest[:, mine:] + scale * product(weights, far_members, 0)
+    back = lax.ppermute(far, "space", swap)
+    kept = rest[:, :mine] + scale * product(weights, own, 0)
+    first = core == 0
+    return (
+        jnp.concatenate(
+            [jnp.where(first, kept, back), jnp.where(first, back, kept)], axis=0
         )
-        z = rest + (dt * g2 * alpha / t) * blend
-    mine = measured_angles.shape[0]
-    back = lax.ppermute(z[:, mine:], "space", swap)
-    kept = z[:, :mine]
-    first = core == 0
-    return jnp.concatenate(
-        [jnp.where(first, kept, back), jnp.where(first, back, kept)], axis=0
+        + math.sqrt(dt * g2) * reverse_perturbation[-1]
     )
 
 

time: 177 us -> 180 us (1.017)
  blocking collectives: 117 us -> 114 us
  waiting for transfers between devices: 14.2 us -> 17.2 us
  other arithmetic: 2.39 us -> 4.76 us
    all_to_all x1 -> x0, blocking collectives: 28.1 us -> none  [per_device(): lax.all_to_all(prior_ensemble, 'mem', split_axis=1, concat_axis=0, tiled=...]
    all_to_all x5 -> x6, blocking collectives: 64.5 us -> 77.7 us  [in_plane(): lax.all_to_all(blocks, AXES, split_axis=0, concat_axis=0, axis_index_grou...]
    all_to_all x2 -> x3, blocking collectives: 24.7 us -> 36.3 us  [in_column(): lax.all_to_all(blocks, 'mem', split_axis=0, concat_axis=0, axis_index_gro...]
    all_to_all x2 -> x1, starting transfers between devices: 7.8 us -> 12.2 us  [per_device(): lax.all_to_all(prior_ensemble, 'mem', split_axis=1, concat_axis=0, tiled=...]
    ppermute x1, starting transfers between devices: 3.29 us -> 0.46 us  [per_device(): lax.ppermute(measured_angles, 'space', swap)]
    all_to_all x2 -> x1, waiting for transfers between devices: 10.6 us -> 13 us  [per_device(): lax.all_to_all(prior_ensemble, 'mem', split_axis=1, concat_axis=0, tiled=...]
    reduce_sum x3, other arithmetic: 0.11 us -> 2.19 us  [per_device(): plane_sum = jnp.sum(in_plane(partial.reshape(peers, rows, total)), axis=0)]
    ppermute x4 -> x3, starting transfers between devices: 15.4 us -> 14.2 us  [the longest x1 10.7 us: per_device(): back = lax.ppermute(far, 'space', swap)]
  transfers between devices with their start and end apart: 7 -> 5, of which waited for: 6 -> 4; matrix products, arithmetic and copies ran while one was open for 2% -> 0% of each run, Pallas kernels for 0% -> 0%
where the time goes in v4:
time: 180 us; the launch traced here: 179 us
  blocking collectives  114 us (63%)
  starting transfers between devices  26.8 us (15%)
  waiting for transfers between devices  17.2 us (10%)
  matrix products  12.2 us (7%)
  other arithmetic  4.76 us (3%)
  local copies, waits for them, and re-layouts  3.82 us (2%)
    all_to_all x6, blocking collectives, in_plane(): lax.all_to_all(blocks, AXES, split_axis=0, concat_axis=0, axis_index_grou...  77.7 us
    all_to_all x3, blocking collectives, in_column(): lax.all_to_all(blocks, 'mem', split_axis=0, concat_axis=0, axis_index_gro...  36.3 us
    all_to_all x1, waiting for transfers between devices, per_device(): lax.all_to_all(prior_ensemble, 'mem', split_axis=1, concat_axis=0, tiled=...  13 us
    all_to_all x1, starting transfers between devices, per_device(): lax.all_to_all(prior_ensemble, 'mem', split_axis=1, concat_axis=0, tiled=...  12.2 us
    dot_general x7, matrix products, product(): lax.dot_general(a, b, (((1,), (axis,)), ((), ())), precision=lax.Precisio...  12.2 us
    ppermute x1, starting transfers between devices, per_device(): back = lax.ppermute(far, 'space', swap)  10.7 us
  transfers between devices with their start and end apart: 5, of which 4 were waited for; matrix products, arithmetic and copies ran while one was open for 0% of the time, Pallas kernels for 0%

profile of v4, /device:TPU:1, one launch (start us, length us, event | category | flops | bytes accessed | tf_op | source)
XLA Modules:
  0.0 179.1 jit_solution(13973828630530854260)
XLA Ops:
  0.0 1.9 %copy.10 = f32[2,32,8,256]{3,2,0,1:T(8,128)} copy(f32[2,32,8,256]{3,2,1,0:T(8,128)} %bitcast.75) | data formatting | bytes 1048576 | tf_op jit(solution)/shard_map/all_to_all | solution.py:51
  1.9 12.2 %all-to-all-start = ((f32[16,32,256]{2,0,1:T(8,128)}), f32[16,32,256]{2,0,1:T(8,128)S(1)}, u32[]{:S(2)}, u32[]{:S(2)}) async-start(f32[16,32,256]{2,0,1:T(8,128)} %bitcast.66), calls=%async_computation | async-start | bytes 1048576 | tf_op jit(solution)/shard_map/all_to_all | solution.py:51
  14.2 1.0 collective-permute-start
  15.3 0.5 collective-permute-start.1
  15.8 1.4 collective-permute-done.1
  17.4 13.0 %all-to-all-done = f32[16,32,256]{2,0,1:T(8,128)S(1)} async-done(((f32[16,32,256]{2,0,1:T(8,128)}), f32[16,32,256]{2,0,1:T(8,128)S(1)}, u32[]{:S(2)}, u32[]{:S(2)}) %all-to-all-start) | async-done | bytes 524320 | tf_op jit(solution)/shard_map/all_to_all | solution.py:51
  30.4 2.4 %collective-permute-start.2 = (f32[512,256]{1,0:T(8,128)S(1)}, f32[512,256]{1,0:T(8,128)S(1)}, u32[]{:S(2)}, u32[]{:S(2)}) collective-permute-start(f32[512,256]{1,0:T(8,128)S(1)} %bitcast.69), channel_id=1, source_target_pairs={{0,32},{32,0},{64,96},{96,64},{128,160},{160,128},{192,224},{224,1... | collective-permute-start | bytes 1572872 | tf_op jit(solution)/shard_map/ppermute | solution.py:60
  32.8 1.5 collective-permute-done.2
  34.3 0.8 copy-done.1
  35.3 1.1 fusion
  36.4 16.2 %all_to_all.64 = f32[16,16,512]{2,1,0:T(8,128)} all-to-all(f32[16,16,512]{2,1,0:T(8,128)S(1)} %bitcast.73), channel_id=1, replica_groups={{0,1,2,3,64,65,66,67,128,129,130,131,192,193,194,195},{4,5,6,7,68,69,70..., dimensions={0} | all-to-all | bytes 1048576 | tf_op jit(solution)/shard_map/all_to_all | solution.py:42
  52.6 1.1 reduce_sum.91
  53.7 11.7 %all_to_all.65 = f32[8,16,512]{2,1,0:T(8,128)S(1)} all-to-all(f32[8,16,512]{2,1,0:T(8,128)S(1)} %broadcast_in_dim.15), channel_id=1, replica_groups={{0,4,8,12,16,20,24,28},{1,5,9,13,17,21,25,29},{2,6,10,14,18,22,26,30},{..., dimensions={0} | all-to-all | bytes 524288 | tf_op jit(solution)/shard_map/all_to_all | solution.py:47
  65.8 13.2 %all_to_all.66 = f32[16,16,512]{2,1,0:T(8,128)S(1)} all-to-all(f32[16,16,512]{2,1,0:T(8,128)S(1)} %broadcast_in_dim.16), channel_id=1, replica_groups={{0,1,2,3,64,65,66,67,128,129,130,131,192,193,194,195},{4,5,6,7,68,69,70..., dimensions={0} | all-to-all | bytes 1048576 | tf_op jit(solution)/shard_map/all_to_all | solution.py:42
  79.0 1.7 fusion.1
  80.8 0.8 copy-done.3
  81.6 1.1 fusion.5
  82.6 12.3 %all_to_all.67 = f32[16,16,512]{2,1,0:T(8,128)} all-to-all(f32[16,16,512]{2,1,0:T(8,128)S(1)} %bitcast.74), channel_id=1, replica_groups={{0,1,2,3,64,65,66,67,128,129,130,131,192,193,194,195},{4,5,6,7,68,69,70..., dimensions={0} | all-to-all | bytes 1048576 | tf_op jit(solution)/shard_map/all_to_all | solution.py:42
  95.0 1.1 reduce_sum.94
  96.1 12.8 %all_to_all.68 = f32[8,16,512]{2,1,0:T(8,128)S(1)} all-to-all(f32[8,16,512]{2,1,0:T(8,128)S(1)} %broadcast_in_dim.17), channel_id=1, replica_groups={{0,4,8,12,16,20,24,28},{1,5,9,13,17,21,25,29},{2,6,10,14,18,22,26,30},{..., dimensions={0} | all-to-all | bytes 524288 | tf_op jit(solution)/shard_map/all_to_all | solution.py:47
  109.3 12.2 %all_to_all.69 = f32[16,16,512]{2,1,0:T(8,128)S(1)} all-to-all(f32[16,16,512]{2,1,0:T(8,128)S(1)} %broadcast_in_dim.18), channel_id=1, replica_groups={{0,1,2,3,64,65,66,67,128,129,130,131,192,193,194,195},{4,5,6,7,68,69,70..., dimensions={0} | all-to-all | bytes 1048576 | tf_op jit(solution)/shard_map/all_to_all | solution.py:42
  121.5 3.4 %multiply_add_fusion = (f32[256,512]{1,0:T(8,128)}, f32[256,512]{1,0:T(8,128)S(1)}) fusion(f32[512]{0:T(512)S(1)} %pad_maximum_fusion.1, f32[256,512]{1,0:T(8,128)S(1)} %bitcast.76, f32[512,512]{1,0:T(8,128)S(1)} %constant_dynamic-update-slice_fusion, f32[3,256,512]{2,1,0:T(8,128)S(1)} %pad_maximum_fusion, f32[256,512]{1,0:T(8,128)S(1)} %copy-done.4), kind=kOutput, calls=%fused_computation.38 | convolution fusion | flops 808976384 | bytes 3672064 | tf_op jit(solution)/shard_map/dot_general | solution.py:13
  124.9 1.1 fusion.4
  125.9 11.9 %all_to_all.70 = f32[16,16,512]{2,1,0:T(8,128)S(1)} all-to-all(f32[16,16,512]{2,1,0:T(8,128)S(1)} %bitcast.72), channel_id=1, replica_groups={{0,1,2,3,64,65,66,67,128,129,130,131,192,193,194,195},{4,5,6,7,68,69,70..., dimensions={0} | all-to-all | bytes 1048576 | tf_op jit(solution)/shard_map/all_to_all | solution.py:42
  137.9 11.9 %all_to_all.71 = f32[8,16,512]{2,1,0:T(8,128)S(1)} all-to-all(f32[8,16,512]{2,1,0:T(8,128)S(1)} %broadcast_in_dim.19), channel_id=1, replica_groups={{0,4,8,12,16,20,24,28},{1,5,9,13,17,21,25,29},{2,6,10,14,18,22,26,30},{..., dimensions={0} | all-to-all | bytes 524288 | tf_op jit(solution)/shard_map/all_to_all | solution.py:47
  149.9 0.2 fusion.22
  150.2 11.9 %all_to_all.72 = f32[16,16,512]{2,1,0:T(8,128)S(1)} all-to-all(f32[16,16,512]{2,1,0:T(8,128)S(1)} %broadcast_in_dim.20), channel_id=1, replica_groups={{0,1,2,3,64,65,66,67,128,129,130,131,192,193,194,195},{4,5,6,7,68,69,70..., dimensions={0} | all-to-all | bytes 1048576 | tf_op jit(solution)/shard_map/all_to_all | solution.py:42
  162.2 2.4 %slice_add_fusion = f32[256,256]{1,0:T(8,128)} fusion(f32[256,512]{1,0:T(8,128)} %get-tuple-element.18, f32[256,512]{1,0:T(8,128)S(1)} %bitcast.67, f32[512,256]{1,0:T(8,128)S(1)} %copy-done.2), kind=kOutput, calls=%fused_computation.40 | convolution fusion | flops 402784256 | bytes 1572864 | tf_op jit(solution)/shard_map/dot_general | solution.py:13
  164.5 10.7 %collective-permute-start.3 = (f32[256,256]{1,0:T(8,128)}, f32[256,256]{1,0:T(8,128)S(1)}, u32[]{:S(2)}, u32[]{:S(2)}) collective-permute-start(f32[256,256]{1,0:T(8,128)} %slice_add_fusion), channel_id=1, source_target_pairs={{0,32},{32,0},{64,96},{96,64},{128,160},{160,128},{192,224},{224,1... | collective-permute-start | bytes 786440 | tf_op jit(solution)/shard_map/ppermute | solution.py:98
  175.3 1.4 collective-permute-done.3
  176.6 1.5 broadcast_select_fusion.1
  178.2 0.9 maximum_add_fusion
  (40 shorter events, 1.9 us)
Async XLA Ops:
  1.9 12.2 %slice-start = ((f32[3,512,256]{2,1,0:T(8,128)}), f32[2,512,256]{2,1,0:T(8,128)S(1)}, s32[]{:S(2)}) async-start(f32[3,512,256]{2,1,0:T(8,128)} %param.6), calls=%async_computation.10 | async-start | bytes 2097152 | tf_op jit(solution)/shard_map/slice | solution.py:52
  1.9 12.2 %copy-start.5 = (f32[512,256]{1,0:T(8,128)S(1)}, f32[512,256]{1,0:T(8,128)}, u32[]{:S(2)}) copy-start(f32[512,256]{1,0:T(8,128)} %param.5) | copy-start | bytes 1572868
  1.9 28.4 %all-to-all-start = ((f32[16,32,256]{2,0,1:T(8,128)}), f32[16,32,256]{2,0,1:T(8,128)S(1)}, u32[]{:S(2)}, u32[]{:S(2)}) async-start(f32[16,32,256]{2,0,1:T(8,128)} %bitcast.66), calls=%async_computation | async-start | bytes 1048576 | tf_op jit(solution)/shard_map/all_to_all | solution.py:51
  14.1 1.2 copy-start.6
  14.2 3.0 %collective-permute-start = (f32[3,256,256]{2,1,0:T(8,128)S(1)}, f32[3,256,256]{2,1,0:T(8,128)S(1)}, u32[]{:S(2)}, u32[]{:S(2)}) collective-permute-start(f32[3,256,256]{2,1,0:T(8,128)S(1)} %get-tuple-element.12), channel_id=1, source_target_pairs={{0,32},{32,0},{64,96},{96,64},{128,160},{160,128},{192,224},{224,1... | collective-permute-start | bytes 2359304 | tf_op jit(solution)/shard_map/ppermute | solution.py:53
  15.3 1.9 %collective-permute-start.1 = (f32[256]{0:T(256)S(1)}, f32[256]{0:T(256)S(1)}, u32[]{:S(2)}, u32[]{:S(2)}) collective-permute-start(f32[256]{0:T(256)S(1)} %copy-done.6), channel_id=1, source_target_pairs={{0,32},{32,0},{64,96},{96,64},{128,160},{160,128},{192,224},{224,1... | collective-permute-start | bytes 3080 | tf_op jit(solution)/shard_map/ppermute | solution.py:56
  30.4 3.9 %collective-permute-start.2 = (f32[512,256]{1,0:T(8,128)S(1)}, f32[512,256]{1,0:T(8,128)S(1)}, u32[]{:S(2)}, u32[]{:S(2)}) collective-permute-start(f32[512,256]{1,0:T(8,128)S(1)} %bitcast.69), channel_id=1, source_target_pairs={{0,32},{32,0},{64,96},{96,64},{128,160},{160,128},{192,224},{224,1... | collective-permute-start | bytes 1572872 | tf_op jit(solution)/shard_map/ppermute | solution.py:60
  34.3 0.8 copy-start.1
  80.8 0.8 copy-start.3
  109.0 12.5 %copy-start.4 = (f32[256,512]{1,0:T(8,128)S(1)}, f32[256,512]{1,0:T(8,128)}, u32[]{:S(2)}) copy-start(f32[256,512]{1,0:T(8,128)} %copy-done.3) | copy-start | bytes 1572868
  137.8 24.3 %copy-start.2 = (f32[512,256]{1,0:T(8,128)S(1)}, f32[512,256]{1,0:T(8,128)}, u32[]{:S(2)}) copy-start(f32[512,256]{1,0:T(8,128)} %copy-done.1) | copy-start | bytes 1572868
  162.2 16.0 %copy-start = (f32[3,512,256]{2,1,0:T(8,128)S(1)}, f32[3,512,256]{2,1,0:T(8,128)}, u32[]{:S(2)}) copy-start(f32[3,512,256]{2,1,0:T(8,128)} %param.6) | copy-start | bytes 4718596
  164.5 12.1 %collective-permute-start.3 = (f32[256,256]{1,0:T(8,128)}, f32[256,256]{1,0:T(8,128)S(1)}, u32[]{:S(2)}, u32[]{:S(2)}) collective-permute-start(f32[256,256]{1,0:T(8,128)} %slice_add_fusion), channel_id=1, source_target_pairs={{0,32},{32,0},{64,96},{96,64},{128,160},{160,128},{192,224},{224,1... | collective-permute-start | bytes 786440 | tf_op jit(solution)/shard_map/ppermute | solution.py:98

commit v5 on v4

v5 whole, which is shorter than its diff:
```python
import functools
import math

import jax
import jax.numpy as jnp
from jax import lax
from jax.experimental import pallas as pl
from jax.experimental.pallas import tpu as pltpu
from jax.sharding import PartitionSpec as P

ITERS = 3
DEPTH = 8
AXES = ("space", "mem")
VMEM = pl.BlockSpec(memory_space=pltpu.VMEM)
SMEM = pl.BlockSpec(memory_space=pltpu.SMEM)


def constants(step):
    t = 1.0 - step / ITERS
    dt = 1.0 / ITERS
    alpha = 1.0 - 0.5 * t
    drift = -0.5 / alpha
    g2 = 1.0 + t / alpha
    damp = 1.0 - t
    keep = 1.0 - dt * drift - dt * g2 / t
    gain = dt * g2 * alpha / t
    pull = dt * g2 * damp * 4.0
    noise = math.sqrt(dt * g2)
    return alpha, t, keep, gain, pull, noise


A0, T0, KEEP0, GAIN0, PULL0, NOISE0 = constants(0)
A1, T1, KEEP1, GAIN1, PULL1, NOISE1 = constants(1)
A2, T2, KEEP2, GAIN2, PULL2, NOISE2 = constants(2)


def product(a, b, axis):
    return lax.dot_general(
        a,
        b,
        (((1,), (axis,)), ((), ())),
        precision=lax.Precision.HIGHEST,
        preferred_element_type=jnp.float32,
    )


def misfit(z, angles):
    x = jnp.abs(z)
    square = 1.0 + z * z
    far = x > 2.414213562373095
    mid = x > 0.4142135623730951
    num = jnp.where(far, -1.0, jnp.where(mid, x - 1.0, x))
    den = jnp.where(far, x, jnp.where(mid, x + 1.0, 1.0))
    base = jnp.where(far, math.pi / 2, jnp.where(mid, math.pi / 4, 0.0))
    r = 1.0 / (den * square)
    q = num * square * r
    s = q * q
    p = 8.05374449538e-2 * s - 1.38776856032e-1
    p = (p * s + 1.99777106478e-1) * s - 3.33329491539e-1
    y = base + (p * s * q + q)
    return (angles - jnp.where(z < 0.0, -y, y)) * (den * r)


def softmax(raw, scale):
    logits = raw * (1.0 / scale)
    e = jnp.exp(logits - jnp.max(logits, axis=1, keepdims=True))
    return e / jnp.sum(e, axis=1, keepdims=True)


def tree_sum(terms):
    while len(terms) > 1:
        terms = [a + b for a, b in zip(terms[::2], terms[1::2])]
    return terms[0]


def first_kernel(core, own, far, z, lengths, members, out):
    width = own.shape[1]
    peers, rows = out.shape[0], out.shape[1] // 2
    count = peers * rows
    members[:, :width] = own[...]
    members[:, width:] = far[...]
    half = members[pl.ds(pl.multiple_of(core[0] * count, count), count), :]
    gram = product(jnp.concatenate([z[...], half]), members[...], 1)
    raw = 2.0 * A0 * gram[:count] - A0 * A0 * lengths[...]
    out[:, :rows, :] = raw.reshape(peers, rows, -1)
    out[:, rows:, :] = gram[count:].reshape(peers, rows, -1)


def spread_kernel(got, out):
    total = tree_sum([got[i] for i in range(got.shape[0])])
    for i in range(out.shape[0]):
        out[i] = total


def weigh_kernel(scale, got, out):
    total = tree_sum([got[i] for i in range(got.shape[0])])
    rows = out.shape[1] // 2
    weights = softmax(total[:rows], scale)
    for i in range(out.shape[0]):
        out[i, :rows, :] = weights
        out[i, rows:, :] = total[rows:]


def step_kernel(got, members, u, noise, angles, lengths, out, y_out, pairs):
    peers, rows = out.shape[0], out.shape[1] // 2
    count = peers * rows
    pairs[...] = got[:, rows:, :].reshape(count, -1)
    blend = product(got[:, :rows, :].reshape(count, -1), members[...], 0)
    z = u[...] + GAIN0 * blend
    y = KEEP1 * z + PULL1 * misfit(z, angles[...]) + NOISE1 * noise[...]
    y_out[...] = y
    gram = product(jnp.concatenate([z, y]), members[...], 1)
    raw1 = 2.0 * A1 * gram[:count] - A1 * A1 * lengths[...]
    raw2 = 2.0 * A2 * gram[count:] - A2 * A2 * lengths[...]
    out[:, :rows, :] = raw1.reshape(peers, rows, -1)
    out[:, rows:, :] = raw2.reshape(peers, rows, -1)


def weigh_twice_kernel(scale1, scale2, core, got, near, far, out):
    total = tree_sum([got[i] for i in range(got.shape[0])])
    rows = out.shape[1] // 2
    w1 = softmax(total[:rows], scale1)
    width = near.shape[0]
    low, high = w1[:, :width], w1[:, width:]
    first = core[0] == 0
    w1_pairs = product(jnp.where(first, low, high), near[...], 0) + product(
        jnp.where(first, high, low), far[...], 0
    )
    w2 = softmax(total[rows:] + (2.0 * A2 * GAIN1) * w1_pairs, scale2)
    for i in range(out.shape[0]):
        out[i, :rows, :] = w1
        out[i, rows:, :] = w2


def last_kernel(got, members, y, angles, kept, sent):
    peers, rows = got.shape[0], got.shape[1] // 2
    count = peers * rows
    weights = jnp.concatenate(
        [
            got[:, :rows, :].reshape(count, -1),
            got[:, rows:, :].reshape(count, -1),
        ]
    )
    blend = product(weights, members[...], 0)
    z = y[...] + GAIN1 * blend[:count]
    z = KEEP2 * z + PULL2 * misfit(z, angles[...]) + GAIN2 * blend[count:]
    width = kept.shape[1]
    kept[...] = z[:, :width]
    sent[...] = z[:, width:]


def call(kernel, name, outs, *args):
    shapes = tuple(jax.ShapeDtypeStruct(s, jnp.float32) for s in outs)
    specs = [SMEM if a.dtype == jnp.int32 else VMEM for a in args]
    result = pl.pallas_call(
        kernel,
        out_shape=shapes,
        in_specs=specs,
        out_specs=tuple(VMEM for _ in outs),
        compiler_params=pltpu.CompilerParams(vmem_limit_bytes=24 << 20),
        name=name,
    )(*args)
    return result if len(outs) > 1 else result[0]


def half(array, which, axis):
    size = array.shape[axis] // 2
    return lax.dynamic_slice_in_dim(array, which * size, size, axis)


def per_device(prior_ensemble, terminal_particles, reverse_perturbation, measured_angles):
    space, mem = lax.axis_size("space"), lax.axis_size("mem")
    core = lax.rem(lax.axis_index("space"), 2)
    core_ref = core.astype(jnp.int32).reshape(1)
    swap = [(i, i ^ 1) for i in range(space)]
    span = mem // DEPTH
    planes = [
        [s * mem + z * span + y for s in range(c, space, 2) for y in range(span)]
        for c in range(2)
        for z in range(DEPTH)
    ]
    columns = [[z * span + y for z in range(DEPTH)] for y in range(span)]
    peers = len(planes[0])

    def other_core(array):
        return lax.ppermute(array, "space", swap)

    def in_plane(blocks):
        return lax.all_to_all(
            blocks, AXES, split_axis=0, concat_axis=0, axis_index_groups=planes
        )

    def in_column(blocks):
        return lax.all_to_all(
            blocks, "mem", split_axis=0, concat_axis=0, axis_index_groups=columns
        )

    temper = math.sqrt(measured_angles.shape[0] * space * mem)
    own = lax.all_to_all(prior_ensemble, "mem", split_axis=1, concat_axis=0, tiled=True)
    samples = jnp.concatenate([terminal_particles[None], reverse_perturbation[:-1]])
    other = other_core(half(samples, 1 - core, 1))
    samples = jnp.concatenate([half(samples, core, 1), other], axis=-1)
    angles = jnp.concatenate([measured_angles, other_core(measured_angles)])[None, :]
    z0 = samples[0]
    u0 = KEEP0 * z0 + PULL0 * misfit(z0, angles) + NOISE0 * samples[1]
    own, z0, u0, e1, angles = lax.optimization_barrier(
        (own, z0, u0, samples[2], angles)
    )
    far = other_core(own)
    lengths = (jnp.sum(own * own, axis=1) + jnp.sum(far * far, axis=1))[None, :]
    total, width = own.shape
    count = z0.shape[0]
    rows = count // peers
    wide = (peers, 2 * rows, total)
    deep = (DEPTH, 2 * rows, total)

    members, blocks = call(
        first_kernel, "first", [(total, 2 * width), wide], core_ref, own, far, z0, lengths
    )
    blocks = call(spread_kernel, "spread", [deep], in_plane(blocks))
    weigh = functools.partial(weigh_kernel, 2.0 * T0 * temper)
    blocks = call(weigh, "weigh", [wide], in_column(blocks))
    blocks, y, near = call(
        step_kernel,
        "step",
        [wide, z0.shape, (count, total)],
        in_plane(blocks),
        members,
        u0,
        e1,
        angles,
        lengths,
    )
    pairs_far = other_core(near)
    blocks = call(spread_kernel, "spread", [deep], in_plane(blocks))
    weigh = functools.partial(weigh_twice_kernel, 2.0 * T1 * temper, 2.0 * T2 * temper)
    blocks = call(
        weigh, "weigh_twice", [wide], core_ref, in_column(blocks), near, pairs_far
    )
    kept, sent = call(
        last_kernel,
        "last",
        [(count, width), (count, width)],
        in_plane(blocks),
        members,
        y,
        angles,
    )
    back = other_core(sent)
    first = core == 0
    return (
        jnp.concatenate(
            [jnp.where(first, kept, back), jnp.where(first, back, kept)], axis=0
        )
        + NOISE2 * reverse_perturbation[-1]
    )


def solution(mesh):
    in_specs = (
        P("mem", "space"),
        P(None, ("space", "mem")),
        P(None, None, ("space", "mem")),
        P(("space", "mem")),
    )
    out_specs = P(None, ("space", "mem"))
    return jax.shard_map(
        per_device, mesh=mesh, in_specs=in_specs, out_specs=out_specs, check_vma=False
    )
```

time: 180 us -> 164 us (0.911)
  blocking collectives: 114 us -> 88.5 us
  matrix products: 12.2 us -> 0 us
  Pallas kernels: 0 us -> 9.92 us
  starting transfers between devices: 26.8 us -> 33.4 us
  waiting for transfers between devices: 17.2 us -> 22.9 us
    all_to_all x3 -> x1, blocking collectives: 36.3 us -> 17 us  [in_column(): lax.all_to_all(blocks, 'mem', split_axis=0, concat_axis=0, axis_index_gro...]
    dot_general x7 -> x0, matrix products: 12.2 us -> none  [product(): lax.dot_general(a, b, (((1,), (axis,)), ((), ())), precision=lax.Precisio...]
    pallas_call x0 -> x7, Pallas kernels: none -> 9.92 us  [call(): pl.pallas_call(kernel, out_shape=shapes, in_specs=specs, out_specs=tuple(...]
    all_to_all x6 -> x4, blocking collectives: 77.7 us -> 71.6 us  [in_plane(): lax.all_to_all(blocks, AXES, split_axis=0, concat_axis=0, axis_index_grou...]
    all_to_all x0 -> x1, starting transfers between devices: none -> 5.95 us  [in_column(): lax.all_to_all(blocks, 'mem', split_axis=0, concat_axis=0, axis_index_gro...]
    all_to_all x0 -> x1, waiting for transfers between devices: none -> 5.26 us  [in_column(): lax.all_to_all(blocks, 'mem', split_axis=0, concat_axis=0, axis_index_gro...]
    ppermute x4 -> x5, starting transfers between devices: 14.6 us -> 18 us  [other_core(): return lax.ppermute(array, 'space', swap)]
    all_to_all x1, starting transfers between devices: 12.2 us -> 9.47 us  [per_device(): lax.all_to_all(prior_ensemble, 'mem', split_axis=1, concat_axis=0, tiled=...]
  transfers between devices with their start and end apart: 5 -> 7, of which waited for: 4 -> 6; matrix products, arithmetic and copies ran while one was open for 0% -> 2% of each run, Pallas kernels for 0% -> 0%
where the time goes in v5:
time: 164 us
  blocking collectives  88.5 us (54%)
  starting transfers between devices  33.4 us (20%)
  waiting for transfers between devices  22.9 us (14%)
  Pallas kernels  9.92 us (6%)
  other arithmetic  4.99 us (3%)
  local copies, waits for them, and re-layouts  3.93 us (2%)
    all_to_all x4, blocking collectives, in_plane(): lax.all_to_all(blocks, AXES, split_axis=0, concat_axis=0, axis_index_grou...  71.6 us
    ppermute x5, starting transfers between devices, other_core(): return lax.ppermute(array, 'space', swap)  18 us
    all_to_all x1, blocking collectives, in_column(): lax.all_to_all(blocks, 'mem', split_axis=0, concat_axis=0, axis_index_gro...  17 us
    all_to_all x1, waiting for transfers between devices, per_device(): lax.all_to_all(prior_ensemble, 'mem', split_axis=1, concat_axis=0, tiled=...  12.7 us
    pallas_call x7, Pallas kernels, call(): pl.pallas_call(kernel, out_shape=shapes, in_specs=specs, out_specs=tuple(...  9.92 us
    all_to_all x1, starting transfers between devices, per_device(): lax.all_to_all(prior_ensemble, 'mem', split_axis=1, concat_axis=0, tiled=...  9.47 us
    all_to_all x1, starting transfers between devices, in_column(): lax.all_to_all(blocks, 'mem', split_axis=0, concat_axis=0, axis_index_gro...  5.95 us
    all_to_all x1, waiting for transfers between devices, in_column(): lax.all_to_all(blocks, 'mem', split_axis=0, concat_axis=0, axis_index_gro...  5.26 us
  transfers between devices with their start and end apart: 7, of which 6 were waited for; matrix products, arithmetic and copies ran while one was open for 2% of the time, Pallas kernels for 0%

profile of v5, /device:TPU:1, one launch (start us, length us, event | category | flops | bytes accessed | tf_op | source)
XLA Modules:
  0.0 163.7 jit_solution(16077863563171049331)
XLA Ops:
  0.0 1.2 slice-done
  1.4 1.0 fusion
  2.4 3.2 %collective-permute-start = (f32[3,256,256]{2,1,0:T(8,128)}, f32[3,256,256]{2,1,0:T(8,128)S(1)}, u32[]{:S(2)}, u32[]{:S(2)}) collective-permute-start(f32[3,256,256]{2,1,0:T(8,128)} %get-tuple-element.31), channel_id=1, source_target_pairs={{0,32},{32,0},{64,96},{96,64},{128,160},{160,128},{192,224},{224,1... | collective-permute-start | bytes 2359304 | tf_op jit(solution)/shard_map/ppermute | solution.py:186
  5.6 0.9 copy.8
  6.5 9.5 %all-to-all-start = ((f32[16,32,256]{2,0,1:T(8,128)}), f32[16,32,256]{2,0,1:T(8,128)S(1)}, u32[]{:S(2)}, u32[]{:S(2)}) async-start(f32[16,32,256]{2,0,1:T(8,128)} %bitcast.21), calls=%async_computation | async-start | bytes 1048576 | tf_op jit(solution)/shard_map/all_to_all | solution.py:199
  15.9 0.5 collective-permute-start.1
  16.5 0.8 collective-permute-done.1
  17.3 0.9 copy-done.2
  18.3 1.7 %fusion.10 = (f32[256,512]{1,0:T(8,128)S(1)}, f32[256,512]{1,0:T(8,128)S(1)}) fusion(f32[3,256,256]{2,1,0:T(8,128)S(1)} %get-tuple-element.32, f32[3,256,256]{2,1,0:T(8,128)} %copy-done.2, f32[512]{0:T(512)S(1)} %constant_dynamic-update-slice_fusion), kind=kLoop, calls=%fused_computation.21 | loop fusion | flops 5242880 | bytes 2623488 | tf_op jit(solution)/shard_map/add | solution.py:205
  20.0 12.7 %all-to-all-done = f32[16,32,256]{2,0,1:T(8,128)S(1)} async-done(((f32[16,32,256]{2,0,1:T(8,128)}), f32[16,32,256]{2,0,1:T(8,128)S(1)}, u32[]{:S(2)}, u32[]{:S(2)}) %all-to-all-start) | async-done | bytes 524320 | tf_op jit(solution)/shard_map/all_to_all | solution.py:199
  32.7 1.9 %collective-permute-start.2 = (f32[512,256]{1,0:T(8,128)S(1)}, f32[512,256]{1,0:T(8,128)S(1)}, u32[]{:S(2)}, u32[]{:S(2)}) collective-permute-start(f32[512,256]{1,0:T(8,128)S(1)} %bitcast.22), channel_id=1, source_target_pairs={{0,32},{32,0},{64,96},{96,64},{128,160},{160,128},{192,224},{224,1... | collective-permute-start | bytes 1572872 | tf_op jit(solution)/shard_map/ppermute | solution.py:186
  34.6 0.1 multiply_reduce_fusion.1
  34.7 1.4 collective-permute-done.2.far
  36.3 1.9 %first.1 = (f32[512,512]{1,0:T(8,128)S(1)}, f32[16,32,512]{2,1,0:T(8,128)S(1)}) custom-call(s32[1]{0:T(128)} %bitcast.core, f32[512,256]{1,0:T(8,128)S(1)} %bitcast.24, f32[512,256]{1,0:T(8,128)S(1)} %collective-permute-done.2.far, f32[256,512]{1,0:T(8,128)S(1)} %get-tuple-element.18.z, f32[1,512]{1,0:T(1,128)S(1)} %bitcast.25), custom_call_target="tpu_custom_call" | custom-call | tf_op jit(solution)/shard_map/first/pallas_call | solution.py:155
  38.2 21.8 %all_to_all.49.got = f32[16,32,512]{2,1,0:T(8,128)S(1)} all-to-all(f32[16,32,512]{2,1,0:T(8,128)S(1)} %get-tuple-element.19), channel_id=1, replica_groups={{0,1,2,3,64,65,66,67,128,129,130,131,192,193,194,195},{4,5,6,7,68,69,70..., dimensions={0} | all-to-all | bytes 2097152 | tf_op jit(solution)/shard_map/all_to_all | solution.py:189
  60.0 17.0 %all_to_all.50.got = f32[8,32,512]{2,1,0:T(8,128)S(1)} all-to-all(f32[8,32,512]{2,1,0:T(8,128)S(1)} %spread.2), channel_id=1, replica_groups={{0,4,8,12,16,20,24,28},{1,5,9,13,17,21,25,29},{2,6,10,14,18,22,26,30},{..., dimensions={0} | all-to-all | bytes 1048576 | tf_op jit(solution)/shard_map/all_to_all | solution.py:194
  77.0 0.2 weigh.1
  77.2 17.5 %all_to_all.51.got = f32[16,32,512]{2,1,0:T(8,128)S(1)} all-to-all(f32[16,32,512]{2,1,0:T(8,128)S(1)} %weigh.1), channel_id=1, replica_groups={{0,1,2,3,64,65,66,67,128,129,130,131,192,193,194,195},{4,5,6,7,68,69,70..., dimensions={0} | all-to-all | bytes 2097152 | tf_op jit(solution)/shard_map/all_to_all | solution.py:189
  94.7 3.4 %step.1 = (f32[16,32,512]{2,1,0:T(8,128)S(1)}, f32[256,512]{1,0:T(8,128)S(1)}, f32[256,512]{1,0:T(8,128)S(1)}) custom-call(f32[16,32,512]{2,1,0:T(8,128)S(1)} %all_to_all.51.got, f32[512,512]{1,0:T(8,128)S(1)} %get-tuple-element.20.members, f32[256,512]{1,0:T(8,128)S(1)} %get-tuple-element.21.u, f32[256,512]{1,0:T(8,128)S(1)} %fusion.15.noise, ...), custom_call_target="tpu_custom_call" | custom-call | tf_op jit(solution)/shard_map/step/pallas_call | solution.py:155
  98.2 0.8 copy-done
  99.0 15.5 %all_to_all.52.got = f32[16,32,512]{2,1,0:T(8,128)S(1)} all-to-all(f32[16,32,512]{2,1,0:T(8,128)S(1)} %get-tuple-element.24), channel_id=1, replica_groups={{0,1,2,3,64,65,66,67,128,129,130,131,192,193,194,195},{4,5,6,7,68,69,70..., dimensions={0} | all-to-all | bytes 2097152 | tf_op jit(solution)/shard_map/all_to_all | solution.py:189
  114.4 0.9 spread.3
  115.3 5.9 %all-to-all-start.5 = ((f32[8,32,512]{2,1,0:T(8,128)}), f32[8,32,512]{2,1,0:T(8,128)S(1)}, u32[]{:S(2)}, u32[]{:S(2)}) async-start(f32[8,32,512]{2,1,0:T(8,128)} %spread.3), calls=%async_computation.5 | async-start | bytes 1048576 | tf_op jit(solution)/shard_map/all_to_all | solution.py:194
  121.3 5.4 %collective-permute-start.3 = (f32[256,512]{1,0:T(8,128)S(1)}, f32[256,512]{1,0:T(8,128)S(1)}, u32[]{:S(2)}, u32[]{:S(2)}) collective-permute-start(f32[256,512]{1,0:T(8,128)S(1)} %copy-done.1), channel_id=1, source_target_pairs={{0,32},{32,0},{64,96},{96,64},{128,160},{160,128},{192,224},{224,1... | collective-permute-start | bytes 1572872 | tf_op jit(solution)/shard_map/ppermute | solution.py:186
  126.6 1.5 collective-permute-done.3.far
  128.2 5.3 %all-to-all-done.5.got = f32[8,32,512]{2,1,0:T(8,128)S(1)} async-done(((f32[8,32,512]{2,1,0:T(8,128)}), f32[8,32,512]{2,1,0:T(8,128)S(1)}, u32[]{:S(2)}, u32[]{:S(2)}) %all-to-all-start.5) | async-done | bytes 524320 | tf_op jit(solution)/shard_map/all_to_all | solution.py:194
  133.4 0.9 weigh_twice.1
  134.4 16.8 %all_to_all.53.got = f32[16,32,512]{2,1,0:T(8,128)S(1)} all-to-all(f32[16,32,512]{2,1,0:T(8,128)S(1)} %weigh_twice.1), channel_id=1, replica_groups={{0,1,2,3,64,65,66,67,128,129,130,131,192,193,194,195},{4,5,6,7,68,69,70..., dimensions={0} | all-to-all | bytes 2097152 | tf_op jit(solution)/shard_map/all_to_all | solution.py:189
  151.2 2.5 %last.1 = (f32[256,256]{1,0:T(8,128)S(1)}, f32[256,256]{1,0:T(8,128)S(1)}) custom-call(f32[16,32,512]{2,1,0:T(8,128)S(1)} %all_to_all.53.got, f32[512,512]{1,0:T(8,128)S(1)} %get-tuple-element.20.members, f32[256,512]{1,0:T(8,128)S(1)} %get-tuple-element.26.y, f32[1,512]{1,0:T(1,128)S(1)} %bitcast.28), custom_call_target="tpu_custom_call" | custom-call | tf_op jit(solution)/shard_map/last/pallas_call | solution.py:155
  153.7 6.9 %collective-permute-start.4 = (f32[256,256]{1,0:T(8,128)S(1)}, f32[256,256]{1,0:T(8,128)S(1)}, u32[]{:S(2)}, u32[]{:S(2)}) collective-permute-start(f32[256,256]{1,0:T(8,128)S(1)} %get-tuple-element.28), channel_id=1, source_target_pairs={{0,32},{32,0},{64,96},{96,64},{128,160},{160,128},{192,224},{224,1... | collective-permute-start | bytes 786440 | tf_op jit(solution)/shard_map/ppermute | solution.py:186
  160.6 1.2 collective-permute-done.4
  161.8 1.9 %maximum_add_fusion = f32[512,256]{1,0:T(8,128)} fusion(f32[256,256]{1,0:T(8,128)S(1)} %get-tuple-element.34, f32[256,256]{1,0:T(8,128)S(1)} %get-tuple-element.33, f32[3,512,256]{2,1,0:T(8,128)} %param.6), kind=kLoop, calls=%fused_computation.29 | loop fusion | flops 393216 | bytes 1572864 | tf_op jit(solution)/shard_map/add | solution.py:252
  (20 shorter events, 0.5 us)
Async XLA Ops:
  0.0 1.2 slice-start
  0.0 1.4 copy-start.4
  1.4 4.2 %copy-start.3 = (f32[16,8192]{1,0:T(8,128)S(1)}, f32[16,8192]{1,0:T(8,128)}, u32[]{:S(2)}) copy-start(f32[16,8192]{1,0:T(8,128)} %param.4) | copy-start | bytes 1572868
  2.4 13.6 %copy-start.5 = (f32[256]{0:T(256)S(1)}, f32[256]{0:T(256)}, u32[]{:S(2)}) copy-start(f32[256]{0:T(256)} %param.7) | copy-start | bytes 3076
  2.4 14.9 %collective-permute-start = (f32[3,256,256]{2,1,0:T(8,128)}, f32[3,256,256]{2,1,0:T(8,128)S(1)}, u32[]{:S(2)}, u32[]{:S(2)}) collective-permute-start(f32[3,256,256]{2,1,0:T(8,128)} %get-tuple-element.31), channel_id=1, source_target_pairs={{0,32},{32,0},{64,96},{96,64},{128,160},{160,128},{192,224},{224,1... | collective-permute-start | bytes 2359304 | tf_op jit(solution)/shard_map/ppermute | solution.py:186
  6.5 26.2 %all-to-all-start = ((f32[16,32,256]{2,0,1:T(8,128)}), f32[16,32,256]{2,0,1:T(8,128)S(1)}, u32[]{:S(2)}, u32[]{:S(2)}) async-start(f32[16,32,256]{2,0,1:T(8,128)} %bitcast.21), calls=%async_computation | async-start | bytes 1048576 | tf_op jit(solution)/shard_map/all_to_all | solution.py:199
  15.9 1.3 collective-permute-start.1
  17.3 0.9 copy-start.2
  32.7 3.5 %collective-permute-start.2 = (f32[512,256]{1,0:T(8,128)S(1)}, f32[512,256]{1,0:T(8,128)S(1)}, u32[]{:S(2)}, u32[]{:S(2)}) collective-permute-start(f32[512,256]{1,0:T(8,128)S(1)} %bitcast.22), channel_id=1, source_target_pairs={{0,32},{32,0},{64,96},{96,64},{128,160},{160,128},{192,224},{224,1... | collective-permute-start | bytes 1572872 | tf_op jit(solution)/shard_map/ppermute | solution.py:186
  98.2 0.8 copy-start
  114.4 6.8 %copy-start.1 = (f32[256,512]{1,0:T(8,128)S(1)}, f32[256,512]{1,0:T(8,128)}, u32[]{:S(2)}) copy-start(f32[256,512]{1,0:T(8,128)} %copy-done) | copy-start | bytes 1572868
  115.3 18.1 %all-to-all-start.5 = ((f32[8,32,512]{2,1,0:T(8,128)}), f32[8,32,512]{2,1,0:T(8,128)S(1)}, u32[]{:S(2)}, u32[]{:S(2)}) async-start(f32[8,32,512]{2,1,0:T(8,128)} %spread.3), calls=%async_computation.5 | async-start | bytes 1048576 | tf_op jit(solution)/shard_map/all_to_all | solution.py:194
  121.3 6.9 %collective-permute-start.3 = (f32[256,512]{1,0:T(8,128)S(1)}, f32[256,512]{1,0:T(8,128)S(1)}, u32[]{:S(2)}, u32[]{:S(2)}) collective-permute-start(f32[256,512]{1,0:T(8,128)S(1)} %copy-done.1), channel_id=1, source_target_pairs={{0,32},{32,0},{64,96},{96,64},{128,160},{160,128},{192,224},{224,1... | collective-permute-start | bytes 1572872 | tf_op jit(solution)/shard_map/ppermute | solution.py:186
  153.7 8.1 %collective-permute-start.4 = (f32[256,256]{1,0:T(8,128)S(1)}, f32[256,256]{1,0:T(8,128)S(1)}, u32[]{:S(2)}, u32[]{:S(2)}) collective-permute-start(f32[256,256]{1,0:T(8,128)S(1)} %get-tuple-element.28), channel_id=1, source_target_pairs={{0,32},{32,0},{64,96},{96,64},{128,160},{160,128},{192,224},{224,1... | collective-permute-start | bytes 786440 | tf_op jit(solution)/shard_map/ppermute | solution.py:186

commit v6 on v5

--- a/solution.py
+++ b/solution.py
@@ -13,6 +13,8 @@
 AXES = ("space", "mem")
 VMEM = pl.BlockSpec(memory_space=pltpu.VMEM)
 SMEM = pl.BlockSpec(memory_space=pltpu.SMEM)
+ANY = pl.BlockSpec(memory_space=pl.ANY)
+DMA = pltpu.SemaphoreType.DMA
 
 
 def constants(step):
@@ -101,63 +103,107 @@
         out[i, rows:, :] = total[rows:]
 
 
-def step_kernel(got, members, u, noise, angles, lengths, out, y_out, pairs):
+def step_kernel(
+    got, members, u, noise, angles, lengths, out, y_out, pairs, y_ref, y_sem, pairs_sem
+):
     peers, rows = out.shape[0], out.shape[1] // 2
     count = peers * rows
-    pairs[...] = got[:, rows:, :].reshape(count, -1)
+    pairs_copy = pltpu.make_async_copy(got.at[:, pl.ds(rows, rows), :], pairs, pairs_sem)
+    pairs_copy.start()
     blend = product(got[:, :rows, :].reshape(count, -1), members[...], 0)
     z = u[...] + GAIN0 * blend
     y = KEEP1 * z + PULL1 * misfit(z, angles[...]) + NOISE1 * noise[...]
-    y_out[...] = y
+    y_ref[...] = y
+    y_copy = pltpu.make_async_copy(y_ref, y_out, y_sem)
+    y_copy.start()
     gram = product(jnp.concatenate([z, y]), members[...], 1)
     raw1 = 2.0 * A1 * gram[:count] - A1 * A1 * lengths[...]
     raw2 = 2.0 * A2 * gram[count:] - A2 * A2 * lengths[...]
     out[:, :rows, :] = raw1.reshape(peers, rows, -1)
     out[:, rows:, :] = raw2.reshape(peers, rows, -1)
-
-
-def weigh_twice_kernel(scale1, scale2, core, got, near, far, out):
+    pairs_copy.wait()
+    y_copy.wait()
+
+
+def weigh_twice_kernel(
+    scale1, scale2, core, got, near_in, far_in, out, near, far, near_sem, far_sem
+):
+    near_copy = pltpu.make_async_copy(near_in, near, near_sem)
+    far_copy = pltpu.make_async_copy(far_in, far, far_sem)
+    near_copy.start()
+    far_copy.start()
     total = tree_sum([got[i] for i in range(got.shape[0])])
     rows = out.shape[1] // 2
     w1 = softmax(total[:rows], scale1)
+    for i in range(out.shape[0]):
+        out[i, :rows, :] = w1
     width = near.shape[0]
     low, high = w1[:, :width], w1[:, width:]
     first = core[0] == 0
-    w1_pairs = product(jnp.where(first, low, high), near[...], 0) + product(
-        jnp.where(first, high, low), far[...], 0
-    )
+    near_copy.wait()
+    w1_pairs = product(jnp.where(first, low, high), near[...], 0)
+    far_copy.wait()
+    w1_pairs += product(jnp.where(first, high, low), far[...], 0)
     w2 = softmax(total[rows:] + (2.0 * A2 * GAIN1) * w1_pairs, scale2)
     for i in range(out.shape[0]):
-        out[i, :rows, :] = w1
         out[i, rows:, :] = w2
 
 
-def last_kernel(got, members, y, angles, kept, sent):
+def last_kernel(first_lane, got, members, y, noise, angles, out):
     peers, rows = got.shape[0], got.shape[1] // 2
     count = peers * rows
+    lanes = pl.ds(first_lane, out.shape[1])
     weights = jnp.concatenate(
         [
             got[:, :rows, :].reshape(count, -1),
             got[:, rows:, :].reshape(count, -1),
         ]
     )
-    blend = product(weights, members[...], 0)
-    z = y[...] + GAIN1 * blend[:count]
-    z = KEEP2 * z + PULL2 * misfit(z, angles[...]) + GAIN2 * blend[count:]
-    width = kept.shape[1]
-    kept[...] = z[:, :width]
-    sent[...] = z[:, width:]
-
-
-def call(kernel, name, outs, *args):
+    blend = product(weights, members[:, lanes], 0)
+    z = y[:, lanes] + GAIN1 * blend[:count]
+    z = KEEP2 * z + PULL2 * misfit(z, angles[:, lanes]) + GAIN2 * blend[count:]
+    out[...] = z + NOISE2 * noise[:, lanes]
+
+
+def place_kernel(core, kept, back, out):
+    count = kept.shape[0]
+    out[pl.ds(pl.multiple_of(core[0] * count, count), count), :] = kept[...]
+    out[pl.ds(pl.multiple_of((1 - core[0]) * count, count), count), :] = back[...]
+
+
+def cut_kernel(array, out, sems):
+    width = out.shape[2]
+    copies = [
+        pltpu.make_async_copy(
+            array.at[:, pl.ds(i * width, width)], out.at[i], sems.at[i]
+        )
+        for i in range(out.shape[0])
+    ]
+    for copy in copies:
+        copy.start()
+    for copy in copies:
+        copy.wait()
+
+
+def call(kernel, name, outs, *args, products=1, anywhere=(), scratch=()):
     shapes = tuple(jax.ShapeDtypeStruct(s, jnp.float32) for s in outs)
-    specs = [SMEM if a.dtype == jnp.int32 else VMEM for a in args]
     result = pl.pallas_call(
         kernel,
         out_shape=shapes,
-        in_specs=specs,
-        out_specs=tuple(VMEM for _ in outs),
+        in_specs=[
+            SMEM if a.dtype == jnp.int32 else ANY if i in anywhere else VMEM
+            for i, a in enumerate(args)
+        ],
+        out_specs=tuple(
+            ANY if len(args) + i in anywhere else VMEM for i in range(len(outs))
+        ),
+        scratch_shapes=list(scratch),
         compiler_params=pltpu.CompilerParams(vmem_limit_bytes=24 << 20),
+        cost_estimate=pl.CostEstimate(
+            flops=12 * 256 * 512 * 512 * products,
+            bytes_accessed=sum(4 * math.prod(s) for s in outs),
+            transcendentals=0,
+        ),
         name=name,
     )(*args)
     return result if len(outs) > 1 else result[0]
@@ -196,15 +242,29 @@
         )
 
     temper = math.sqrt(measured_angles.shape[0] * space * mem)
-    own = lax.all_to_all(prior_ensemble, "mem", split_axis=1, concat_axis=0, tiled=True)
-    samples = jnp.concatenate([terminal_particles[None], reverse_perturbation[:-1]])
-    other = other_core(half(samples, 1 - core, 1))
-    samples = jnp.concatenate([half(samples, core, 1), other], axis=-1)
+    width = measured_angles.shape[0]
+    cut = call(
+        cut_kernel,
+        "cut",
+        [(mem, prior_ensemble.shape[0], width)],
+        prior_ensemble,
+        anywhere=(0, 1),
+        scratch=[DMA((mem,))],
+    )
+    own = lax.all_to_all(cut, "mem", split_axis=0, concat_axis=0)
+    own = own.reshape(mem * prior_ensemble.shape[0], width)
+    def pair_up(arrays):
+        other = other_core(half(arrays, 1 - core, 1))
+        return jnp.concatenate([half(arrays, core, 1), other], axis=-1)
+
+    e1, e2 = pair_up(reverse_perturbation[1:])
+    z0, e0 = pair_up(
+        jnp.concatenate([terminal_particles[None], reverse_perturbation[:1]])
+    )
     angles = jnp.concatenate([measured_angles, other_core(measured_angles)])[None, :]
-    z0 = samples[0]
-    u0 = KEEP0 * z0 + PULL0 * misfit(z0, angles) + NOISE0 * samples[1]
-    own, z0, u0, e1, angles = lax.optimization_barrier(
-        (own, z0, u0, samples[2], angles)
+    u0 = KEEP0 * z0 + PULL0 * misfit(z0, angles) + NOISE0 * e0
+    own, z0, u0, e1, e2, angles = lax.optimization_barrier(
+        (own, z0, u0, e1, e2, angles)
     )
     far = other_core(own)
     lengths = (jnp.sum(own * own, axis=1) + jnp.sum(far * far, axis=1))[None, :]
@@ -223,37 +283,40 @@
     blocks, y, near = call(
         step_kernel,
         "step",
-        [wide, z0.shape, (count, total)],
+        [wide, z0.shape, (peers, rows, total)],
         in_plane(blocks),
         members,
         u0,
         e1,
         angles,
         lengths,
-    )
+        products=3,
+        anywhere=(7, 8),
+        scratch=[pltpu.VMEM(z0.shape, jnp.float32), DMA, DMA],
+    )
+    near = near.reshape(count, total)
     pairs_far = other_core(near)
     blocks = call(spread_kernel, "spread", [deep], in_plane(blocks))
     weigh = functools.partial(weigh_twice_kernel, 2.0 * T1 * temper, 2.0 * T2 * temper)
+    half_pairs = pltpu.VMEM((count, total), jnp.float32)
     blocks = call(
-        weigh, "weigh_twice", [wide], core_ref, in_column(blocks), near, pairs_far
-    )
-    kept, sent = call(
-        last_kernel,
-        "last",
-        [(count, width), (count, width)],
-        in_plane(blocks),
-        members,
-        y,
-        angles,
-    )
+        weigh,
+        "weigh_twice",
+        [wide],
+        core_ref,
+        in_column(blocks),
+        near,
+        pairs_far,
+        anywhere=(2, 3),
+        scratch=[half_pairs, half_pairs, DMA, DMA],
+    )
+    blocks = in_plane(blocks)
+    last = functools.partial(last_kernel, width)
+    sent = call(last, "last_far", [(count, width)], blocks, members, y, e2, angles)
     back = other_core(sent)
-    first = core == 0
-    return (
-        jnp.concatenate(
-            [jnp.where(first, kept, back), jnp.where(first, back, kept)], axis=0
-        )
-        + NOISE2 * reverse_perturbation[-1]
-    )
+    last = functools.partial(last_kernel, 0)
+    kept = call(last, "last_near", [(count, width)], blocks, members, y, e2, angles)
+    return call(place_kernel, "place", [(2 * count, width)], core_ref, kept, back)
 
 
 def solution(mesh):

time: 164 us -> 161 us (0.982)
  waiting for transfers between devices: 22.9 us -> 18.8 us
  Pallas kernels: 9.92 us -> 12.4 us
  other arithmetic: 4.99 us -> 2.79 us
    add x2 -> x1, other arithmetic: 3.6 us -> 0.66 us  [per_device(): u0 = KEEP0 * z0 + PULL0 * misfit(z0, angles) + NOISE0 * e0]
    all_to_all x1, waiting for transfers between devices: 12.7 us -> 9.95 us  [per_device(): own = lax.all_to_all(cut, 'mem', split_axis=0, concat_axis=0)]
    all_to_all x1, starting transfers between devices: 9.47 us -> 12.2 us  [per_device(): own = lax.all_to_all(cut, 'mem', split_axis=0, concat_axis=0)]
    pallas_call x7 -> x10, Pallas kernels: 9.92 us -> 12.4 us  [call(): pl.pallas_call(kernel, out_shape=shapes, in_specs=[SMEM if a.dtype == jnp...]
    ppermute x5 -> x6, starting transfers between devices: 18 us -> 16 us  [other_core(): return lax.ppermute(array, 'space', swap)]
    ppermute x5 -> x6, waiting for transfers between devices: 4.89 us -> 4.29 us  [other_core(): return lax.ppermute(array, 'space', swap)]
  transfers between devices with their start and end apart: 7 -> 8, of which waited for: 6 -> 5; matrix products, arithmetic and copies ran while one was open for 2% -> 2% of each run, Pallas kernels for 0% -> 1%
where the time goes in v6:
time: 161 us
  blocking collectives  88.6 us (55%)
  starting transfers between devices  34.2 us (21%)
  waiting for transfers between devices  18.8 us (12%)
  Pallas kernels  12.4 us (8%)
  local copies, waits for them, and re-layouts  3.83 us (2%)
  other arithmetic  2.79 us (2%)
    all_to_all x4, blocking collectives, in_plane(): lax.all_to_all(blocks, AXES, split_axis=0, concat_axis=0, axis_index_grou...  71.7 us
    all_to_all x1, blocking collectives, in_column(): lax.all_to_all(blocks, 'mem', split_axis=0, concat_axis=0, axis_index_gro...  17 us
    ppermute x6, starting transfers between devices, other_core(): return lax.ppermute(array, 'space', swap)  16 us
    pallas_call x10, Pallas kernels, call(): pl.pallas_call(kernel, out_shape=shapes, in_specs=[SMEM if a.dtype == jnp...  12.4 us
    all_to_all x1, starting transfers between devices, per_device(): own = lax.all_to_all(cut, 'mem', split_axis=0, concat_axis=0)  12.2 us
    all_to_all x1, waiting for transfers between devices, per_device(): own = lax.all_to_all(cut, 'mem', split_axis=0, concat_axis=0)  9.95 us
    all_to_all x1, starting transfers between devices, in_column(): lax.all_to_all(blocks, 'mem', split_axis=0, concat_axis=0, axis_index_gro...  5.98 us
    all_to_all x1, waiting for transfers between devices, in_column(): lax.all_to_all(blocks, 'mem', split_axis=0, concat_axis=0, axis_index_gro...  4.56 us
  transfers between devices with their start and end apart: 8, of which 5 were waited for; matrix products, arithmetic and copies ran while one was open for 2% of the time, Pallas kernels for 1%

profile of v6, /device:TPU:1, one launch (start us, length us, event | category | flops | bytes accessed | tf_op | source)
XLA Modules:
  0.0 160.8 jit_solution(2557335374470999076)
XLA Ops:
  0.0 1.0 copy-done.1
  1.0 1.1 cut.1
  2.1 12.2 %all-to-all-start = ((f32[32,16,256]{2,1,0:T(8,128)}), f32[32,16,256]{2,1,0:T(8,128)S(1)}, u32[]{:S(2)}, u32[]{:S(2)}) async-start(f32[32,16,256]{2,1,0:T(8,128)} %cut.1), calls=%async_computation | async-start | bytes 1048576 | tf_op jit(solution)/shard_map/all_to_all | solution.py:254
  14.3 0.9 constant_dynamic-slice_fusion
  15.3 1.0 collective-permute-start.2
  16.2 0.9 fusion.14
  17.1 0.5 collective-permute-start
  17.6 1.4 collective-permute-done.1
  19.0 1.0 fusion.15
  20.0 0.7 fusion.8
  20.6 10.0 %all-to-all-done = f32[32,16,256]{2,1,0:T(8,128)S(1)} async-done(((f32[32,16,256]{2,1,0:T(8,128)}), f32[32,16,256]{2,1,0:T(8,128)S(1)}, u32[]{:S(2)}, u32[]{:S(2)}) %all-to-all-start) | async-done | bytes 524320 | tf_op jit(solution)/shard_map/all_to_all | solution.py:254
  30.6 2.4 %collective-permute-start.3 = (f32[512,256]{1,0:T(8,128)S(1)}, f32[512,256]{1,0:T(8,128)S(1)}, u32[]{:S(2)}, u32[]{:S(2)}) collective-permute-start(f32[512,256]{1,0:T(8,128)S(1)} %bitcast.17), channel_id=1, source_target_pairs={{0,32},{32,0},{64,96},{96,64},{128,160},{160,128},{192,224},{224,1... | collective-permute-start | bytes 1572872 | tf_op jit(solution)/shard_map/ppermute | solution.py:232
  33.1 1.4 collective-permute-done.3.far
  34.7 1.9 %first.1 = (f32[512,512]{1,0:T(8,128)S(1)}, f32[16,32,512]{2,1,0:T(8,128)S(1)}) custom-call(s32[1]{0:T(128)} %bitcast.core, f32[512,256]{1,0:T(8,128)S(1)} %bitcast.19, f32[512,256]{1,0:T(8,128)S(1)} %collective-permute-done.3.far, f32[256,512]{1,0:T(8,128)S(1)} %get-tuple-element.17.z, f32[1,512]{1,0:T(1,128)S(1)} %bitcast.23), custom_call_target="tpu_custom_call" | custom-call | flops 805306368 | bytes 2097152 | tf_op jit(solution)/shard_map/first/pallas_call | solution.py:190
  36.6 21.7 %all_to_all.35.got = f32[16,32,512]{2,1,0:T(8,128)S(1)} all-to-all(f32[16,32,512]{2,1,0:T(8,128)S(1)} %get-tuple-element.18), channel_id=1, replica_groups={{0,1,2,3,64,65,66,67,128,129,130,131,192,193,194,195},{4,5,6,7,68,69,70..., dimensions={0} | all-to-all | bytes 2097152 | tf_op jit(solution)/shard_map/all_to_all | solution.py:235
  58.4 17.0 %all_to_all.36.got = f32[8,32,512]{2,1,0:T(8,128)S(1)} all-to-all(f32[8,32,512]{2,1,0:T(8,128)S(1)} %spread.2), channel_id=1, replica_groups={{0,4,8,12,16,20,24,28},{1,5,9,13,17,21,25,29},{2,6,10,14,18,22,26,30},{..., dimensions={0} | all-to-all | bytes 1048576 | tf_op jit(solution)/shard_map/all_to_all | solution.py:240
  75.6 17.6 %all_to_all.37.got = f32[16,32,512]{2,1,0:T(8,128)S(1)} all-to-all(f32[16,32,512]{2,1,0:T(8,128)S(1)} %weigh.1), channel_id=1, replica_groups={{0,1,2,3,64,65,66,67,128,129,130,131,192,193,194,195},{4,5,6,7,68,69,70..., dimensions={0} | all-to-all | bytes 2097152 | tf_op jit(solution)/shard_map/all_to_all | solution.py:235
  93.2 3.6 %step.1 = (f32[16,32,512]{2,1,0:T(8,128)S(1)}, f32[256,512]{1,0:T(8,128)S(1)}, f32[16,16,512]{2,1,0:T(8,128)S(1)}) custom-call(f32[16,32,512]{2,1,0:T(8,128)S(1)} %all_to_all.37.got, f32[512,512]{1,0:T(8,128)S(1)} %get-tuple-element.19.members, f32[256,512]{1,0:T(8,128)S(1)} %get-tuple-element.20.u, f32[256,512]{1,0:T(8,128)S(1)} %copy-done, ...), custom_call_target="tpu_custom_call" | custom-call | flops 2415919104 | bytes 2097152 | tf_op jit(solution)/shard_map/step/pallas_call | solution.py:190
  96.8 15.5 %all_to_all.38.got = f32[16,32,512]{2,1,0:T(8,128)S(1)} all-to-all(f32[16,32,512]{2,1,0:T(8,128)S(1)} %get-tuple-element.23), channel_id=1, replica_groups={{0,1,2,3,64,65,66,67,128,129,130,131,192,193,194,195},{4,5,6,7,68,69,70..., dimensions={0} | all-to-all | bytes 2097152 | tf_op jit(solution)/shard_map/all_to_all | solution.py:235
  112.3 0.9 spread.3
  113.2 6.0 %all-to-all-start.5 = ((f32[8,32,512]{2,1,0:T(8,128)}), f32[8,32,512]{2,1,0:T(8,128)S(1)}, u32[]{:S(2)}, u32[]{:S(2)}) async-start(f32[8,32,512]{2,1,0:T(8,128)} %spread.3), calls=%async_computation.5 | async-start | bytes 1048576 | tf_op jit(solution)/shard_map/all_to_all | solution.py:240
  119.1 5.2 %collective-permute-start.4 = (f32[256,512]{1,0:T(8,128)S(1)}, f32[256,512]{1,0:T(8,128)S(1)}, u32[]{:S(2)}, u32[]{:S(2)}) collective-permute-start(f32[256,512]{1,0:T(8,128)S(1)} %bitcast.25), channel_id=1, source_target_pairs={{0,32},{32,0},{64,96},{96,64},{128,160},{160,128},{192,224},{224,1... | collective-permute-start | bytes 1572872 | tf_op jit(solution)/shard_map/ppermute | solution.py:232
  124.4 1.5 collective-permute-done.4.far_in
  125.9 0.8 copy-done.2
  126.7 4.6 %all-to-all-done.5.got = f32[8,32,512]{2,1,0:T(8,128)S(1)} async-done(((f32[8,32,512]{2,1,0:T(8,128)}), f32[8,32,512]{2,1,0:T(8,128)S(1)}, u32[]{:S(2)}, u32[]{:S(2)}) %all-to-all-start.5) | async-done | bytes 524320 | tf_op jit(solution)/shard_map/all_to_all | solution.py:240
  131.3 1.0 copy-done.3
  132.3 1.1 weigh_twice.1
  133.5 16.8 %all_to_all.39.got = f32[16,32,512]{2,1,0:T(8,128)S(1)} all-to-all(f32[16,32,512]{2,1,0:T(8,128)S(1)} %weigh_twice.1), channel_id=1, replica_groups={{0,1,2,3,64,65,66,67,128,129,130,131,192,193,194,195},{4,5,6,7,68,69,70..., dimensions={0} | all-to-all | bytes 2097152 | tf_op jit(solution)/shard_map/all_to_all | solution.py:235
  150.3 1.4 last_far.1
  151.7 6.9 %collective-permute-start.5 = (f32[256,256]{1,0:T(8,128)S(1)}, f32[256,256]{1,0:T(8,128)S(1)}, u32[]{:S(2)}, u32[]{:S(2)}) collective-permute-start(f32[256,256]{1,0:T(8,128)S(1)} %last_far.1), channel_id=1, source_target_pairs={{0,32},{32,0},{64,96},{96,64},{128,160},{160,128},{192,224},{224,1... | collective-permute-start | bytes 786440 | tf_op jit(solution)/shard_map/ppermute | solution.py:232
  158.6 1.4 last_near.1.kept
  160.0 0.8 place.1
  (25 shorter events, 0.7 us)
Async XLA Ops:
  0.0 1.0 copy-start.1
  2.1 12.2 %slice-start = ((f32[3,512,256]{2,1,0:T(8,128)}), f32[2,512,256]{2,1,0:T(8,128)S(1)}, s32[]{:S(2)}) async-start(f32[3,512,256]{2,1,0:T(8,128)} %param.6), calls=%async_computation.7 | async-start | bytes 2097152 | tf_op jit(solution)/shard_map/slice | solution.py:260
  2.1 28.5 %all-to-all-start = ((f32[32,16,256]{2,1,0:T(8,128)}), f32[32,16,256]{2,1,0:T(8,128)S(1)}, u32[]{:S(2)}, u32[]{:S(2)}) async-start(f32[32,16,256]{2,1,0:T(8,128)} %cut.1), calls=%async_computation | async-start | bytes 1048576 | tf_op jit(solution)/shard_map/all_to_all | solution.py:254
  14.3 1.9 %slice-start.1 = ((f32[3,512,256]{2,1,0:T(8,128)}), f32[1,512,256]{2,1,0:T(8,128)S(1)}, s32[]{:S(2)}) async-start(f32[3,512,256]{2,1,0:T(8,128)} %param.6), calls=%async_computation.8 | async-start | bytes 1048576 | tf_op jit(solution)/shard_map/slice | solution.py:262
  14.3 1.9 %copy-start.4 = (f32[512,256]{1,0:T(8,128)S(1)}, f32[512,256]{1,0:T(8,128)}, u32[]{:S(2)}) copy-start(f32[512,256]{1,0:T(8,128)} %param.5) | copy-start | bytes 1572868
  15.3 2.3 %copy-start.5 = (f32[256]{0:T(256)S(1)}, f32[256]{0:T(256)}, u32[]{:S(2)}) copy-start(f32[256]{0:T(256)} %param.7) | copy-start | bytes 3076
  15.3 3.8 %collective-permute-start.2 = (f32[2,256,256]{2,1,0:T(8,128)}, f32[2,256,256]{2,1,0:T(8,128)S(1)}, u32[]{:S(2)}, u32[]{:S(2)}) collective-permute-start(f32[2,256,256]{2,1,0:T(8,128)} %get-tuple-element.31), channel_id=1, source_target_pairs={{0,32},{32,0},{64,96},{96,64},{128,160},{160,128},{192,224},{224,1... | collective-permute-start | bytes 1572872 | tf_op jit(solution)/shard_map/ppermute | solution.py:232
  17.1 2.9 %collective-permute-start = (f32[2,256,256]{2,1,0:T(8,128)}, f32[2,256,256]{2,1,0:T(8,128)S(1)}, u32[]{:S(2)}, u32[]{:S(2)}) collective-permute-start(f32[2,256,256]{2,1,0:T(8,128)} %get-tuple-element.34), channel_id=1, source_target_pairs={{0,32},{32,0},{64,96},{96,64},{128,160},{160,128},{192,224},{224,1... | collective-permute-start | bytes 1572872 | tf_op jit(solution)/shard_map/ppermute | solution.py:232
  17.6 1.4 collective-permute-start.1
  30.6 3.9 %collective-permute-start.3 = (f32[512,256]{1,0:T(8,128)S(1)}, f32[512,256]{1,0:T(8,128)S(1)}, u32[]{:S(2)}, u32[]{:S(2)}) collective-permute-start(f32[512,256]{1,0:T(8,128)S(1)} %bitcast.17), channel_id=1, source_target_pairs={{0,32},{32,0},{64,96},{96,64},{128,160},{160,128},{192,224},{224,1... | collective-permute-start | bytes 1572872 | tf_op jit(solution)/shard_map/ppermute | solution.py:232
  75.6 17.6 %copy-start = (f32[256,512]{1,0:T(8,128)S(1)}, f32[256,512]{1,0:T(8,128)}, u32[]{:S(2)}) copy-start(f32[256,512]{1,0:T(8,128)} %get-tuple-element.21.noise) | copy-start | bytes 1572868
  113.2 18.1 %all-to-all-start.5 = ((f32[8,32,512]{2,1,0:T(8,128)}), f32[8,32,512]{2,1,0:T(8,128)S(1)}, u32[]{:S(2)}, u32[]{:S(2)}) async-start(f32[8,32,512]{2,1,0:T(8,128)} %spread.3), calls=%async_computation.5 | async-start | bytes 1048576 | tf_op jit(solution)/shard_map/all_to_all | solution.py:240
  119.1 6.8 %collective-permute-start.4 = (f32[256,512]{1,0:T(8,128)S(1)}, f32[256,512]{1,0:T(8,128)S(1)}, u32[]{:S(2)}, u32[]{:S(2)}) collective-permute-start(f32[256,512]{1,0:T(8,128)S(1)} %bitcast.25), channel_id=1, source_target_pairs={{0,32},{32,0},{64,96},{96,64},{128,160},{160,128},{192,224},{224,1... | collective-permute-start | bytes 1572872 | tf_op jit(solution)/shard_map/ppermute | solution.py:232
  125.9 0.8 copy-start.2
  131.3 1.0 copy-start.3
  151.7 8.3 %collective-permute-start.5 = (f32[256,256]{1,0:T(8,128)S(1)}, f32[256,256]{1,0:T(8,128)S(1)}, u32[]{:S(2)}, u32[]{:S(2)}) collective-permute-start(f32[256,256]{1,0:T(8,128)S(1)} %last_far.1), channel_id=1, source_target_pairs={{0,32},{32,0},{64,96},{96,64},{128,160},{160,128},{192,224},{224,1... | collective-permute-start | bytes 786440 | tf_op jit(solution)/shard_map/ppermute | solution.py:232

commit v7 on v6

--- a/solution.py
+++ b/solution.py
@@ -75,17 +75,60 @@
     return terms[0]
 
 
-def first_kernel(core, own, far, z, lengths, members, out):
+def pack_pairs(first, gram):
+    rows = gram.shape[0] // 2
+    low, high = gram[:rows], gram[rows:]
+
+    def blocks(array, start):
+        wrapped = jnp.concatenate([array, array], axis=1)
+        return wrapped[:, start * rows : (start + 3) * rows]
+
+    low = jnp.where(first, blocks(low, 0), blocks(low, 2))
+    high = jnp.where(first, blocks(high, 1), blocks(high, 3))
+    return jnp.concatenate([low, high])
+
+
+def times_pairs(first, w, near, far):
+    rows = near.shape[0] // 2
+    low, high = w[:, : 2 * rows], w[:, 2 * rows :]
+    w = jnp.where(first, w, jnp.concatenate([high, low], axis=1))
+    parts = [w[:, i * rows : (i + 1) * rows] for i in range(4)]
+    packed = [near[:rows], near[rows:], far[:rows], far[rows:]]
+    sums = [product(parts[(i + 1) % 4], packed[i][:, rows : 2 * rows], 1) for i in range(4)]
+    for i in range(4):
+        ahead = product(parts[i], packed[i], 0)
+        for k in range(3):
+            sums[(i + k) % 4] += ahead[:, k * rows : (k + 1) * rows]
+    low = jnp.concatenate(sums[:2], axis=1)
+    high = jnp.concatenate(sums[2:], axis=1)
+    return jnp.concatenate(
+        [jnp.where(first, low, high), jnp.where(first, high, low)], axis=1
+    )
+
+
+def my_members(core, members):
+    count = members.shape[0] // 2
+    return members[pl.ds(pl.multiple_of(core[0] * count, count), count), :]
+
+
+def own_kernel(core, own, z, out):
+    stack = jnp.concatenate([z[:, : own.shape[1]], my_members(core, own)])
+    out[...] = product(stack, own[...], 1)
+
+
+def first_kernel(core, own, far, z, lengths, gram_own, members, out):
     width = own.shape[1]
-    peers, rows = out.shape[0], out.shape[1] // 2
+    total = own.shape[0]
+    peers, rows = out.shape[0], out.shape[1]
     count = peers * rows
     members[:, :width] = own[...]
     members[:, width:] = far[...]
-    half = members[pl.ds(pl.multiple_of(core[0] * count, count), count), :]
-    gram = product(jnp.concatenate([z[...], half]), members[...], 1)
+    stack = jnp.concatenate([z[:, width:], my_members(core, far)])
+    gram = gram_own[...] + product(stack, far[...], 1)
     raw = 2.0 * A0 * gram[:count] - A0 * A0 * lengths[...]
-    out[:, :rows, :] = raw.reshape(peers, rows, -1)
-    out[:, rows:, :] = gram[count:].reshape(peers, rows, -1)
+    out[:, :, :total] = raw.reshape(peers, rows, -1)
+    pairs = pack_pairs(core[0] == 0, gram[count:])
+    out[:, :, total:] = pairs.reshape(peers, rows, -1)
 
 
 def spread_kernel(got, out):
@@ -94,13 +137,12 @@
         out[i] = total
 
 
-def weigh_kernel(scale, got, out):
+def weigh_kernel(scale, members, got, out):
     total = tree_sum([got[i] for i in range(got.shape[0])])
-    rows = out.shape[1] // 2
-    weights = softmax(total[:rows], scale)
+    weights = softmax(total[:, :members], scale)
     for i in range(out.shape[0]):
-        out[i, :rows, :] = weights
-        out[i, rows:, :] = total[rows:]
+        out[i, :, :members] = weights
+        out[i, :, members:] = total[:, members:]
 
 
 def step_kernel(
@@ -108,9 +150,12 @@
 ):
     peers, rows = out.shape[0], out.shape[1] // 2
     count = peers * rows
-    pairs_copy = pltpu.make_async_copy(got.at[:, pl.ds(rows, rows), :], pairs, pairs_sem)
+    total, packed = members.shape[0], pairs.shape[2]
+    pairs_copy = pltpu.make_async_copy(
+        got.at[:, :, pl.ds(total, packed)], pairs, pairs_sem
+    )
     pairs_copy.start()
-    blend = product(got[:, :rows, :].reshape(count, -1), members[...], 0)
+    blend = product(got[:, :, :total].reshape(count, -1), members[...], 0)
     z = u[...] + GAIN0 * blend
     y = KEEP1 * z + PULL1 * misfit(z, angles[...]) + NOISE1 * noise[...]
     y_ref[...] = y
@@ -137,13 +182,9 @@
     w1 = softmax(total[:rows], scale1)
     for i in range(out.shape[0]):
         out[i, :rows, :] = w1
-    width = near.shape[0]
-    low, high = w1[:, :width], w1[:, width:]
-    first = core[0] == 0
     near_copy.wait()
-    w1_pairs = product(jnp.where(first, low, high), near[...], 0)
     far_copy.wait()
-    w1_pairs += product(jnp.where(first, high, low), far[...], 0)
+    w1_pairs = times_pairs(core[0] == 0, w1, near[...], far[...])
     w2 = softmax(total[rows:] + (2.0 * A2 * GAIN1) * w1_pairs, scale2)
     for i in range(out.shape[0]):
         out[i, rows:, :] = w2
@@ -271,19 +312,31 @@
     total, width = own.shape
     count = z0.shape[0]
     rows = count // peers
+    packed = 3 * total // 4
     wide = (peers, 2 * rows, total)
     deep = (DEPTH, 2 * rows, total)
 
+    gram_own = call(own_kernel, "own", [(2 * count, total)], core_ref, own, z0)
     members, blocks = call(
-        first_kernel, "first", [(total, 2 * width), wide], core_ref, own, far, z0, lengths
-    )
-    blocks = call(spread_kernel, "spread", [deep], in_plane(blocks))
-    weigh = functools.partial(weigh_kernel, 2.0 * T0 * temper)
-    blocks = call(weigh, "weigh", [wide], in_column(blocks))
+        first_kernel,
+        "first",
+        [(total, 2 * width), (peers, rows, total + packed)],
+        core_ref,
+        own,
+        far,
+        z0,
+        lengths,
+        gram_own,
+    )
+    blocks = call(
+        spread_kernel, "spread", [(DEPTH, rows, total + packed)], in_plane(blocks)
+    )
+    weigh = functools.partial(weigh_kernel, 2.0 * T0 * temper, total)
+    blocks = call(weigh, "weigh", [(peers, rows, total + packed)], in_column(blocks))
     blocks, y, near = call(
         step_kernel,
         "step",
-        [wide, z0.shape, (peers, rows, total)],
+        [wide, z0.shape, (peers, rows, packed)],
         in_plane(blocks),
         members,
         u0,
@@ -294,11 +347,11 @@
         anywhere=(7, 8),
         scratch=[pltpu.VMEM(z0.shape, jnp.float32), DMA, DMA],
     )
-    near = near.reshape(count, total)
+    near = near.reshape(count, packed)
     pairs_far = other_core(near)
     blocks = call(spread_kernel, "spread", [deep], in_plane(blocks))
     weigh = functools.partial(weigh_twice_kernel, 2.0 * T1 * temper, 2.0 * T2 * temper)
-    half_pairs = pltpu.VMEM((count, total), jnp.float32)
+    half_pairs = pltpu.VMEM((count, packed), jnp.float32)
     blocks = call(
         weigh,
         "weigh_twice",

time: 161 us -> 156 us (0.969)
  blocking collectives: 88.6 us -> 84.7 us
  local copies, waits for them, and re-layouts: 3.83 us -> 2.01 us
    all_to_all x4, blocking collectives: 71.7 us -> 69.6 us  [in_plane(): lax.all_to_all(blocks, AXES, split_axis=0, concat_axis=0, axis_index_grou...]
    unnamed x13 -> x9, local copies, waits for them, and re-layouts: 2.9 us -> 1.07 us
    all_to_all x1, blocking collectives: 17 us -> 15.2 us  [in_column(): lax.all_to_all(blocks, 'mem', split_axis=0, concat_axis=0, axis_index_gro...]
    pallas_call x10 -> x11, Pallas kernels: 12.4 us -> 13.3 us  [call(): pl.pallas_call(kernel, out_shape=shapes, in_specs=[SMEM if a.dtype == jnp...]
  transfers between devices with their start and end apart: 8 -> 8, of which waited for: 5 -> 5; matrix products, arithmetic and copies ran while one was open for 2% -> 2% of each run, Pallas kernels for 1% -> 2%
where the time goes in v7:
time: 156 us; the launch traced here: 155 us
  blocking collectives  84.7 us (54%)
  starting transfers between devices  33.8 us (22%)
  waiting for transfers between devices  18.5 us (12%)
  Pallas kernels  13.3 us (9%)
  other arithmetic  2.81 us (2%)
  local copies, waits for them, and re-layouts  2.01 us (1%)
    all_to_all x4, blocking collectives, in_plane(): lax.all_to_all(blocks, AXES, split_axis=0, concat_axis=0, axis_index_grou...  69.6 us
    ppermute x6, starting transfers between devices, other_core(): return lax.ppermute(array, 'space', swap)  16 us
    all_to_all x1, blocking collectives, in_column(): lax.all_to_all(blocks, 'mem', split_axis=0, concat_axis=0, axis_index_gro...  15.2 us
    pallas_call x11, Pallas kernels, call(): pl.pallas_call(kernel, out_shape=shapes, in_specs=[SMEM if a.dtype == jnp...  13.3 us
    all_to_all x1, starting transfers between devices, per_device(): own = lax.all_to_all(cut, 'mem', split_axis=0, concat_axis=0)  12.2 us
    all_to_all x1, waiting for transfers between devices, per_device(): own = lax.all_to_all(cut, 'mem', split_axis=0, concat_axis=0)  9.92 us
    all_to_all x1, starting transfers between devices, in_column(): lax.all_to_all(blocks, 'mem', split_axis=0, concat_axis=0, axis_index_gro...  5.65 us
    all_to_all x1, waiting for transfers between devices, in_column(): lax.all_to_all(blocks, 'mem', split_axis=0, concat_axis=0, axis_index_gro...  5.53 us
  transfers between devices with their start and end apart: 8, of which 5 were waited for; matrix products, arithmetic and copies ran while one was open for 2% of the time, Pallas kernels for 2%

profile of v7, /device:TPU:1, one launch (start us, length us, event | category | flops | bytes accessed | tf_op | source)
XLA Modules:
  0.0 155.3 jit_solution(4250507429839241890)
XLA Ops:
  0.0 1.0 copy-done.1
  1.0 1.1 cut.1
  2.1 12.2 %all-to-all-start = ((f32[32,16,256]{2,1,0:T(8,128)}), f32[32,16,256]{2,1,0:T(8,128)S(1)}, u32[]{:S(2)}, u32[]{:S(2)}) async-start(f32[32,16,256]{2,1,0:T(8,128)} %cut.1), calls=%async_computation | async-start | bytes 1048576 | tf_op jit(solution)/shard_map/all_to_all | solution.py:295
  14.3 0.9 constant_dynamic-slice_fusion
  15.3 1.0 collective-permute-start.2
  16.2 0.9 fusion.14
  17.1 0.5 collective-permute-start
  17.7 1.4 collective-permute-done.1
  19.0 1.0 fusion.15
  20.0 0.7 fusion.8
  20.7 9.9 %all-to-all-done = f32[32,16,256]{2,1,0:T(8,128)S(1)} async-done(((f32[32,16,256]{2,1,0:T(8,128)}), f32[32,16,256]{2,1,0:T(8,128)S(1)}, u32[]{:S(2)}, u32[]{:S(2)}) %all-to-all-start) | async-done | bytes 524320 | tf_op jit(solution)/shard_map/all_to_all | solution.py:295
  30.6 2.4 %collective-permute-start.3 = (f32[512,256]{1,0:T(8,128)S(1)}, f32[512,256]{1,0:T(8,128)S(1)}, u32[]{:S(2)}, u32[]{:S(2)}) collective-permute-start(f32[512,256]{1,0:T(8,128)S(1)} %bitcast.17), channel_id=1, source_target_pairs={{0,32},{32,0},{64,96},{96,64},{128,160},{160,128},{192,224},{224,1... | collective-permute-start | bytes 1572872 | tf_op jit(solution)/shard_map/ppermute | solution.py:273
  33.0 1.0 own.1.gram_own
  34.2 0.3 collective-permute-done.3.far
  34.7 1.1 first.1
  35.8 19.9 %all_to_all.35.got = f32[16,16,896]{2,1,0:T(8,128)S(1)} all-to-all(f32[16,16,896]{2,1,0:T(8,128)S(1)} %get-tuple-element.18), channel_id=1, replica_groups={{0,1,2,3,64,65,66,67,128,129,130,131,192,193,194,195},{4,5,6,7,68,69,70..., dimensions={0} | all-to-all | bytes 1835008 | tf_op jit(solution)/shard_map/all_to_all | solution.py:276
  55.7 15.2 %all_to_all.36.got = f32[8,16,896]{2,1,0:T(8,128)S(1)} all-to-all(f32[8,16,896]{2,1,0:T(8,128)S(1)} %spread.2), channel_id=1, replica_groups={{0,4,8,12,16,20,24,28},{1,5,9,13,17,21,25,29},{2,6,10,14,18,22,26,30},{..., dimensions={0} | all-to-all | bytes 917504 | tf_op jit(solution)/shard_map/all_to_all | solution.py:281
  70.9 0.2 weigh.1
  71.1 18.0 %all_to_all.37.got = f32[16,16,896]{2,1,0:T(8,128)S(1)} all-to-all(f32[16,16,896]{2,1,0:T(8,128)S(1)} %weigh.1), channel_id=1, replica_groups={{0,1,2,3,64,65,66,67,128,129,130,131,192,193,194,195},{4,5,6,7,68,69,70..., dimensions={0} | all-to-all | bytes 1835008 | tf_op jit(solution)/shard_map/all_to_all | solution.py:276
  89.1 3.6 %step.1 = (f32[16,32,512]{2,1,0:T(8,128)S(1)}, f32[256,512]{1,0:T(8,128)S(1)}, f32[16,16,384]{2,1,0:T(8,128)S(1)}) custom-call(f32[16,16,896]{2,1,0:T(8,128)S(1)} %all_to_all.37.got, f32[512,512]{1,0:T(8,128)S(1)} %get-tuple-element.19.members, f32[256,512]{1,0:T(8,128)S(1)} %get-tuple-element.20.u, f32[256,512]{1,0:T(8,128)S(1)} %copy-done, ...), custom_call_target="tpu_custom_call" | custom-call | flops 2415919104 | bytes 1966080 | tf_op jit(solution)/shard_map/step/pallas_call | solution.py:231
  92.7 14.9 %all_to_all.38.got = f32[16,32,512]{2,1,0:T(8,128)S(1)} all-to-all(f32[16,32,512]{2,1,0:T(8,128)S(1)} %get-tuple-element.23), channel_id=1, replica_groups={{0,1,2,3,64,65,66,67,128,129,130,131,192,193,194,195},{4,5,6,7,68,69,70..., dimensions={0} | all-to-all | bytes 2097152 | tf_op jit(solution)/shard_map/all_to_all | solution.py:276
  107.6 0.9 spread.3
  108.4 5.6 %all-to-all-start.5 = ((f32[8,32,512]{2,1,0:T(8,128)}), f32[8,32,512]{2,1,0:T(8,128)S(1)}, u32[]{:S(2)}, u32[]{:S(2)}) async-start(f32[8,32,512]{2,1,0:T(8,128)} %spread.3), calls=%async_computation.5 | async-start | bytes 1048576 | tf_op jit(solution)/shard_map/all_to_all | solution.py:281
  114.1 5.2 %collective-permute-start.4 = (f32[256,384]{1,0:T(8,128)S(1)}, f32[256,384]{1,0:T(8,128)S(1)}, u32[]{:S(2)}, u32[]{:S(2)}) collective-permute-start(f32[256,384]{1,0:T(8,128)S(1)} %bitcast.26), channel_id=1, source_target_pairs={{0,32},{32,0},{64,96},{96,64},{128,160},{160,128},{192,224},{224,1... | collective-permute-start | bytes 1179656 | tf_op jit(solution)/shard_map/ppermute | solution.py:273
  119.3 1.3 collective-permute-done.4.far_in
  120.7 5.5 %all-to-all-done.5.got = f32[8,32,512]{2,1,0:T(8,128)S(1)} async-done(((f32[8,32,512]{2,1,0:T(8,128)}), f32[8,32,512]{2,1,0:T(8,128)S(1)}, u32[]{:S(2)}, u32[]{:S(2)}) %all-to-all-start.5) | async-done | bytes 524320 | tf_op jit(solution)/shard_map/all_to_all | solution.py:281
  126.2 1.8 %weigh_twice.1 = f32[16,32,512]{2,1,0:T(8,128)S(1)} custom-call(s32[1]{0:T(128)} %bitcast.core, f32[8,32,512]{2,1,0:T(8,128)S(1)} %all-to-all-done.5.got, f32[256,384]{1,0:T(8,128)S(1)} %bitcast.27, f32[256,384]{1,0:T(8,128)S(1)} %collective-permute-done.4.far_in), custom_call_target="tpu_custom_call" | custom-call | flops 805306368 | bytes 1048576 | tf_op jit(solution)/shard_map/weigh_twice/pallas_call | solution.py:231
  128.0 16.8 %all_to_all.39.got = f32[16,32,512]{2,1,0:T(8,128)S(1)} all-to-all(f32[16,32,512]{2,1,0:T(8,128)S(1)} %weigh_twice.1), channel_id=1, replica_groups={{0,1,2,3,64,65,66,67,128,129,130,131,192,193,194,195},{4,5,6,7,68,69,70..., dimensions={0} | all-to-all | bytes 2097152 | tf_op jit(solution)/shard_map/all_to_all | solution.py:276
  144.8 1.4 last_far.1
  146.2 6.9 %collective-permute-start.5 = (f32[256,256]{1,0:T(8,128)S(1)}, f32[256,256]{1,0:T(8,128)S(1)}, u32[]{:S(2)}, u32[]{:S(2)}) collective-permute-start(f32[256,256]{1,0:T(8,128)S(1)} %last_far.1), channel_id=1, source_target_pairs={{0,32},{32,0},{64,96},{96,64},{128,160},{160,128},{192,224},{224,1... | collective-permute-start | bytes 786440 | tf_op jit(solution)/shard_map/ppermute | solution.py:273
  153.1 1.4 last_near.1.kept
  154.5 0.8 place.1
  (22 shorter events, 0.5 us)
Async XLA Ops:
  0.0 1.0 copy-start.1
  2.1 12.2 %slice-start = ((f32[3,512,256]{2,1,0:T(8,128)}), f32[2,512,256]{2,1,0:T(8,128)S(1)}, s32[]{:S(2)}) async-start(f32[3,512,256]{2,1,0:T(8,128)} %param.6), calls=%async_computation.7 | async-start | bytes 2097152 | tf_op jit(solution)/shard_map/slice | solution.py:301
  2.1 28.5 %all-to-all-start = ((f32[32,16,256]{2,1,0:T(8,128)}), f32[32,16,256]{2,1,0:T(8,128)S(1)}, u32[]{:S(2)}, u32[]{:S(2)}) async-start(f32[32,16,256]{2,1,0:T(8,128)} %cut.1), calls=%async_computation | async-start | bytes 1048576 | tf_op jit(solution)/shard_map/all_to_all | solution.py:295
  14.3 1.9 %slice-start.1 = ((f32[3,512,256]{2,1,0:T(8,128)}), f32[1,512,256]{2,1,0:T(8,128)S(1)}, s32[]{:S(2)}) async-start(f32[3,512,256]{2,1,0:T(8,128)} %param.6), calls=%async_computation.8 | async-start | bytes 1048576 | tf_op jit(solution)/shard_map/slice | solution.py:303
  14.3 1.9 %copy-start.2 = (f32[512,256]{1,0:T(8,128)S(1)}, f32[512,256]{1,0:T(8,128)}, u32[]{:S(2)}) copy-start(f32[512,256]{1,0:T(8,128)} %param.5) | copy-start | bytes 1572868
  15.3 2.3 %copy-start.3 = (f32[256]{0:T(256)S(1)}, f32[256]{0:T(256)}, u32[]{:S(2)}) copy-start(f32[256]{0:T(256)} %param.7) | copy-start | bytes 3076
  15.3 3.8 %collective-permute-start.2 = (f32[2,256,256]{2,1,0:T(8,128)}, f32[2,256,256]{2,1,0:T(8,128)S(1)}, u32[]{:S(2)}, u32[]{:S(2)}) collective-permute-start(f32[2,256,256]{2,1,0:T(8,128)} %get-tuple-element.31), channel_id=1, source_target_pairs={{0,32},{32,0},{64,96},{96,64},{128,160},{160,128},{192,224},{224,1... | collective-permute-start | bytes 1572872 | tf_op jit(solution)/shard_map/ppermute | solution.py:273
  17.1 2.9 %collective-permute-start = (f32[2,256,256]{2,1,0:T(8,128)}, f32[2,256,256]{2,1,0:T(8,128)S(1)}, u32[]{:S(2)}, u32[]{:S(2)}) collective-permute-start(f32[2,256,256]{2,1,0:T(8,128)} %get-tuple-element.34), channel_id=1, source_target_pairs={{0,32},{32,0},{64,96},{96,64},{128,160},{160,128},{192,224},{224,1... | collective-permute-start | bytes 1572872 | tf_op jit(solution)/shard_map/ppermute | solution.py:273
  17.6 1.4 collective-permute-start.1
  30.6 3.9 %collective-permute-start.3 = (f32[512,256]{1,0:T(8,128)S(1)}, f32[512,256]{1,0:T(8,128)S(1)}, u32[]{:S(2)}, u32[]{:S(2)}) collective-permute-start(f32[512,256]{1,0:T(8,128)S(1)} %bitcast.17), channel_id=1, source_target_pairs={{0,32},{32,0},{64,96},{96,64},{128,160},{160,128},{192,224},{224,1... | collective-permute-start | bytes 1572872 | tf_op jit(solution)/shard_map/ppermute | solution.py:273
  71.1 18.0 %copy-start = (f32[256,512]{1,0:T(8,128)S(1)}, f32[256,512]{1,0:T(8,128)}, u32[]{:S(2)}) copy-start(f32[256,512]{1,0:T(8,128)} %get-tuple-element.21.noise) | copy-start | bytes 1572868
  108.4 17.8 %all-to-all-start.5 = ((f32[8,32,512]{2,1,0:T(8,128)}), f32[8,32,512]{2,1,0:T(8,128)S(1)}, u32[]{:S(2)}, u32[]{:S(2)}) async-start(f32[8,32,512]{2,1,0:T(8,128)} %spread.3), calls=%async_computation.5 | async-start | bytes 1048576 | tf_op jit(solution)/shard_map/all_to_all | solution.py:281
  114.1 6.6 %collective-permute-start.4 = (f32[256,384]{1,0:T(8,128)S(1)}, f32[256,384]{1,0:T(8,128)S(1)}, u32[]{:S(2)}, u32[]{:S(2)}) collective-permute-start(f32[256,384]{1,0:T(8,128)S(1)} %bitcast.26), channel_id=1, source_target_pairs={{0,32},{32,0},{64,96},{96,64},{128,160},{160,128},{192,224},{224,1... | collective-permute-start | bytes 1179656 | tf_op jit(solution)/shard_map/ppermute | solution.py:273
  146.2 8.3 %collective-permute-start.5 = (f32[256,256]{1,0:T(8,128)S(1)}, f32[256,256]{1,0:T(8,128)S(1)}, u32[]{:S(2)}, u32[]{:S(2)}) collective-permute-start(f32[256,256]{1,0:T(8,128)S(1)} %last_far.1), channel_id=1, source_target_pairs={{0,32},{32,0},{64,96},{96,64},{128,160},{160,128},{192,224},{224,1... | collective-permute-start | bytes 786440 | tf_op jit(solution)/shard_map/ppermute | solution.py:273

commit v8 on v7

--- a/solution.py
+++ b/solution.py
@@ -76,34 +76,73 @@
 
 
 def pack_pairs(first, gram):
-    rows = gram.shape[0] // 2
-    low, high = gram[:rows], gram[rows:]
-
-    def blocks(array, start):
-        wrapped = jnp.concatenate([array, array], axis=1)
-        return wrapped[:, start * rows : (start + 3) * rows]
-
-    low = jnp.where(first, blocks(low, 0), blocks(low, 2))
-    high = jnp.where(first, blocks(high, 1), blocks(high, 3))
-    return jnp.concatenate([low, high])
+    size = gram.shape[0] // 2
+
+    def block(row, column, other):
+        rows = gram[row * size : (row + 1) * size]
+        return jnp.where(
+            first,
+            rows[:, column * size : (column + 1) * size],
+            rows[:, other * size : (other + 1) * size],
+        )
+
+    return jnp.concatenate(
+        [block(0, 0, 2), block(0, 1, 3), block(1, 1, 3), block(0, 2, 1), block(1, 3, 0)],
+        axis=1,
+    )
+
+
+def thirds(array):
+    high = array.astype(jnp.bfloat16)
+    rest = array - high.astype(jnp.float32)
+    mid = rest.astype(jnp.bfloat16)
+    return high, mid, (rest - mid.astype(jnp.float32)).astype(jnp.bfloat16)
 
 
 def times_pairs(first, w, near, far):
-    rows = near.shape[0] // 2
-    low, high = w[:, : 2 * rows], w[:, 2 * rows :]
-    w = jnp.where(first, w, jnp.concatenate([high, low], axis=1))
-    parts = [w[:, i * rows : (i + 1) * rows] for i in range(4)]
-    packed = [near[:rows], near[rows:], far[:rows], far[rows:]]
-    sums = [product(parts[(i + 1) % 4], packed[i][:, rows : 2 * rows], 1) for i in range(4)]
-    for i in range(4):
-        ahead = product(parts[i], packed[i], 0)
-        for k in range(3):
-            sums[(i + k) % 4] += ahead[:, k * rows : (k + 1) * rows]
-    low = jnp.concatenate(sums[:2], axis=1)
-    high = jnp.concatenate(sums[2:], axis=1)
-    return jnp.concatenate(
-        [jnp.where(first, low, high), jnp.where(first, high, low)], axis=1
-    )
+    size, rows = near.shape[0], w.shape[0]
+    w_high, w_mid, w_low = thirds(w)
+    stacks = (
+        jnp.concatenate([w_high, w_mid, w_low]),
+        jnp.concatenate([w_high, w_mid]),
+        w_high,
+    )
+    halves = jnp.where(first, near, far), jnp.where(first, far, near)
+    places = ((0, 0), (0, 1), (1, 1), (0, 2), (1, 3)), ((2, 2), (2, 3), (3, 3), (2, 1), (3, 0))
+    terms = [[[] for _ in range(4)] for _ in stacks]
+
+    def add(third, a, b, block, axis):
+        part = stacks[third][:, a * size : (a + 1) * size]
+        terms[third][b].append(
+            lax.dot_general(
+                part,
+                block,
+                (((1,), (axis,)), ((), ())),
+                preferred_element_type=jnp.float32,
+            )
+        )
+
+    for half_pairs, which in zip(halves, places):
+        for third, array in enumerate(thirds(half_pairs)):
+            for k, (a, b) in enumerate(which):
+                block = array[:, k * size : (k + 1) * size]
+                add(third, a, b, block, 0)
+                if a != b:
+                    add(third, b, a, block, 1)
+    p, q, r = (
+        jnp.concatenate([tree_sum(t) for t in third], axis=1) for third in terms
+    )
+    small = p[2 * rows :] + q[rows:] + r
+    return (small + (p[rows : 2 * rows] + q[:rows])) + p[:rows]
+
+
+def to_halves(rows):
+    size = rows.shape[-2] // 2
+    return jnp.concatenate([rows[..., :size, :], rows[..., size:, :]], axis=-1)
+
+
+def from_halves(rows, total):
+    return jnp.concatenate([rows[..., :total], rows[..., total : 2 * total]], axis=-2)
 
 
 def my_members(core, members):
@@ -119,16 +158,16 @@
 def first_kernel(core, own, far, z, lengths, gram_own, members, out):
     width = own.shape[1]
     total = own.shape[0]
-    peers, rows = out.shape[0], out.shape[1]
+    peers, rows = out.shape[0], 2 * out.shape[1]
     count = peers * rows
     members[:, :width] = own[...]
     members[:, width:] = far[...]
     stack = jnp.concatenate([z[:, width:], my_members(core, far)])
     gram = gram_own[...] + product(stack, far[...], 1)
     raw = 2.0 * A0 * gram[:count] - A0 * A0 * lengths[...]
-    out[:, :, :total] = raw.reshape(peers, rows, -1)
+    out[:, :, : 2 * total] = to_halves(raw.reshape(peers, rows, -1))
     pairs = pack_pairs(core[0] == 0, gram[count:])
-    out[:, :, total:] = pairs.reshape(peers, rows, -1)
+    out[:, :, 2 * total :] = pairs.reshape(peers, rows // 2, -1)
 
 
 def spread_kernel(got, out):
@@ -139,10 +178,10 @@
 
 def weigh_kernel(scale, members, got, out):
     total = tree_sum([got[i] for i in range(got.shape[0])])
-    weights = softmax(total[:, :members], scale)
+    weights = to_halves(softmax(from_halves(total, members), scale))
     for i in range(out.shape[0]):
-        out[i, :, :members] = weights
-        out[i, :, members:] = total[:, members:]
+        out[i, :, : 2 * members] = weights
+        out[i, :, 2 * members :] = total[:, 2 * members :]
 
 
 def step_kernel(
@@ -152,10 +191,11 @@
     count = peers * rows
     total, packed = members.shape[0], pairs.shape[2]
     pairs_copy = pltpu.make_async_copy(
-        got.at[:, :, pl.ds(total, packed)], pairs, pairs_sem
+        got.at[:, :, pl.ds(2 * total, packed)], pairs, pairs_sem
     )
     pairs_copy.start()
-    blend = product(got[:, :, :total].reshape(count, -1), members[...], 0)
+    weights = from_halves(got[...], total).reshape(count, -1)
+    blend = product(weights, members[...], 0)
     z = u[...] + GAIN0 * blend
     y = KEEP1 * z + PULL1 * misfit(z, angles[...]) + NOISE1 * noise[...]
     y_ref[...] = y
@@ -312,7 +352,8 @@
     total, width = own.shape
     count = z0.shape[0]
     rows = count // peers
-    packed = 3 * total // 4
+    packed = 5 * total // 4
+    mixed = 2 * total + packed
     wide = (peers, 2 * rows, total)
     deep = (DEPTH, 2 * rows, total)
 
@@ -320,7 +361,7 @@
     members, blocks = call(
         first_kernel,
         "first",
-        [(total, 2 * width), (peers, rows, total + packed)],
+        [(total, 2 * width), (peers, rows // 2, mixed)],
         core_ref,
         own,
         far,
@@ -329,14 +370,14 @@
         gram_own,
     )
     blocks = call(
-        spread_kernel, "spread", [(DEPTH, rows, total + packed)], in_plane(blocks)
+        spread_kernel, "spread", [(DEPTH, rows // 2, mixed)], in_plane(blocks)
     )
     weigh = functools.partial(weigh_kernel, 2.0 * T0 * temper, total)
-    blocks = call(weigh, "weigh", [(peers, rows, total + packed)], in_column(blocks))
+    blocks = call(weigh, "weigh", [(peers, rows // 2, mixed)], in_column(blocks))
     blocks, y, near = call(
         step_kernel,
         "step",
-        [wide, z0.shape, (peers, rows, packed)],
+        [wide, z0.shape, (peers, rows // 2, packed)],
         in_plane(blocks),
         members,
         u0,
@@ -347,11 +388,11 @@
         anywhere=(7, 8),
         scratch=[pltpu.VMEM(z0.shape, jnp.float32), DMA, DMA],
     )
-    near = near.reshape(count, packed)
+    near = near.reshape(count // 2, packed)
     pairs_far = other_core(near)
     blocks = call(spread_kernel, "spread", [deep], in_plane(blocks))
     weigh = functools.partial(weigh_twice_kernel, 2.0 * T1 * temper, 2.0 * T2 * temper)
-    half_pairs = pltpu.VMEM((count, packed), jnp.float32)
+    half_pairs = pltpu.VMEM((count // 2, packed), jnp.float32)
     blocks = call(
         weigh,
         "weigh_twice",

time: 156 us -> 154 us (0.987)
  no operation moved by 1% of the time
where the time goes in v8:
time: 154 us; the launch traced here: 153 us
  blocking collectives  83.3 us (54%)
  starting transfers between devices  33.3 us (22%)
  waiting for transfers between devices  18.8 us (12%)
  Pallas kernels  12.9 us (8%)
  other arithmetic  2.81 us (2%)
  local copies, waits for them, and re-layouts  2.01 us (1%)
    all_to_all x4, blocking collectives, in_plane(): lax.all_to_all(blocks, AXES, split_axis=0, concat_axis=0, axis_index_grou...  68.3 us
    ppermute x6, starting transfers between devices, other_core(): return lax.ppermute(array, 'space', swap)  15.5 us
    all_to_all x1, blocking collectives, in_column(): lax.all_to_all(blocks, 'mem', split_axis=0, concat_axis=0, axis_index_gro...  15 us
    pallas_call x11, Pallas kernels, call(): pl.pallas_call(kernel, out_shape=shapes, in_specs=[SMEM if a.dtype == jnp...  12.9 us
    all_to_all x1, starting transfers between devices, per_device(): own = lax.all_to_all(cut, 'mem', split_axis=0, concat_axis=0)  12.2 us
    all_to_all x1, waiting for transfers between devices, per_device(): own = lax.all_to_all(cut, 'mem', split_axis=0, concat_axis=0)  9.92 us
    all_to_all x1, waiting for transfers between devices, in_column(): lax.all_to_all(blocks, 'mem', split_axis=0, concat_axis=0, axis_index_gro...  5.89 us
    all_to_all x1, starting transfers between devices, in_column(): lax.all_to_all(blocks, 'mem', split_axis=0, concat_axis=0, axis_index_gro...  5.61 us
  transfers between devices with their start and end apart: 8, of which 5 were waited for; matrix products, arithmetic and copies ran while one was open for 2% of the time, Pallas kernels for 2%

profile of v8, /device:TPU:1, one launch (start us, length us, event | category | flops | bytes accessed | tf_op | source)
XLA Modules:
  0.0 153.3 jit_solution(7259890968543467977)
XLA Ops:
  0.0 1.0 copy-done.1
  1.0 1.1 cut.1
  2.1 12.2 %all-to-all-start = ((f32[32,16,256]{2,1,0:T(8,128)}), f32[32,16,256]{2,1,0:T(8,128)S(1)}, u32[]{:S(2)}, u32[]{:S(2)}) async-start(f32[32,16,256]{2,1,0:T(8,128)} %cut.1), calls=%async_computation | async-start | bytes 1048576 | tf_op jit(solution)/shard_map/all_to_all | solution.py:335
  14.3 0.9 constant_dynamic-slice_fusion
  15.3 1.0 collective-permute-start.2
  16.2 0.9 fusion.14
  17.1 0.5 collective-permute-start
  17.7 1.4 collective-permute-done.1
  19.0 1.0 fusion.15
  20.0 0.7 fusion.8
  20.7 9.9 %all-to-all-done = f32[32,16,256]{2,1,0:T(8,128)S(1)} async-done(((f32[32,16,256]{2,1,0:T(8,128)}), f32[32,16,256]{2,1,0:T(8,128)S(1)}, u32[]{:S(2)}, u32[]{:S(2)}) %all-to-all-start) | async-done | bytes 524320 | tf_op jit(solution)/shard_map/all_to_all | solution.py:335
  30.6 2.4 %collective-permute-start.3 = (f32[512,256]{1,0:T(8,128)S(1)}, f32[512,256]{1,0:T(8,128)S(1)}, u32[]{:S(2)}, u32[]{:S(2)}) collective-permute-start(f32[512,256]{1,0:T(8,128)S(1)} %bitcast.17), channel_id=1, source_target_pairs={{0,32},{32,0},{64,96},{96,64},{128,160},{160,128},{192,224},{224,1... | collective-permute-start | bytes 1572872 | tf_op jit(solution)/shard_map/ppermute | solution.py:313
  33.0 1.0 own.1.gram_own
  34.2 0.3 collective-permute-done.3.far
  34.7 1.1 first.1
  35.8 19.5 %all_to_all.35.got = f32[16,8,1664]{2,1,0:T(8,128)S(1)} all-to-all(f32[16,8,1664]{2,1,0:T(8,128)S(1)} %get-tuple-element.18), channel_id=1, replica_groups={{0,1,2,3,64,65,66,67,128,129,130,131,192,193,194,195},{4,5,6,7,68,69,70..., dimensions={0} | all-to-all | bytes 1703936 | tf_op jit(solution)/shard_map/all_to_all | solution.py:316
  55.3 15.0 %all_to_all.36.got = f32[8,8,1664]{2,1,0:T(8,128)S(1)} all-to-all(f32[8,8,1664]{2,1,0:T(8,128)S(1)} %spread.2), channel_id=1, replica_groups={{0,4,8,12,16,20,24,28},{1,5,9,13,17,21,25,29},{2,6,10,14,18,22,26,30},{..., dimensions={0} | all-to-all | bytes 851968 | tf_op jit(solution)/shard_map/all_to_all | solution.py:321
  70.3 0.2 weigh.1
  70.6 16.2 %all_to_all.37.got = f32[16,8,1664]{2,1,0:T(8,128)S(1)} all-to-all(f32[16,8,1664]{2,1,0:T(8,128)S(1)} %weigh.1), channel_id=1, replica_groups={{0,1,2,3,64,65,66,67,128,129,130,131,192,193,194,195},{4,5,6,7,68,69,70..., dimensions={0} | all-to-all | bytes 1703936 | tf_op jit(solution)/shard_map/all_to_all | solution.py:316
  86.8 3.6 %step.1 = (f32[16,32,512]{2,1,0:T(8,128)S(1)}, f32[256,512]{1,0:T(8,128)S(1)}, f32[16,8,640]{2,1,0:T(8,128)S(1)}) custom-call(f32[16,8,1664]{2,1,0:T(8,128)S(1)} %all_to_all.37.got, f32[512,512]{1,0:T(8,128)S(1)} %get-tuple-element.19.members, f32[256,512]{1,0:T(8,128)S(1)} %get-tuple-element.20.u, f32[256,512]{1,0:T(8,128)S(1)} %copy-done, ...), custom_call_target="tpu_custom_call" | custom-call | flops 2415919104 | bytes 1900544 | tf_op jit(solution)/shard_map/step/pallas_call | solution.py:271
  90.4 15.7 %all_to_all.38.got = f32[16,32,512]{2,1,0:T(8,128)S(1)} all-to-all(f32[16,32,512]{2,1,0:T(8,128)S(1)} %get-tuple-element.23), channel_id=1, replica_groups={{0,1,2,3,64,65,66,67,128,129,130,131,192,193,194,195},{4,5,6,7,68,69,70..., dimensions={0} | all-to-all | bytes 2097152 | tf_op jit(solution)/shard_map/all_to_all | solution.py:316
  106.1 0.9 spread.3
  107.0 5.6 %all-to-all-start.5 = ((f32[8,32,512]{2,1,0:T(8,128)}), f32[8,32,512]{2,1,0:T(8,128)S(1)}, u32[]{:S(2)}, u32[]{:S(2)}) async-start(f32[8,32,512]{2,1,0:T(8,128)} %spread.3), calls=%async_computation.5 | async-start | bytes 1048576 | tf_op jit(solution)/shard_map/all_to_all | solution.py:321
  112.6 4.9 %collective-permute-start.4 = (f32[128,640]{1,0:T(8,128)S(1)}, f32[128,640]{1,0:T(8,128)S(1)}, u32[]{:S(2)}, u32[]{:S(2)}) collective-permute-start(f32[128,640]{1,0:T(8,128)S(1)} %bitcast.26), channel_id=1, source_target_pairs={{0,32},{32,0},{64,96},{96,64},{128,160},{160,128},{192,224},{224,1... | collective-permute-start | bytes 983048 | tf_op jit(solution)/shard_map/ppermute | solution.py:313
  117.5 1.3 collective-permute-done.4.far_in
  118.8 5.9 %all-to-all-done.5.got = f32[8,32,512]{2,1,0:T(8,128)S(1)} async-done(((f32[8,32,512]{2,1,0:T(8,128)}), f32[8,32,512]{2,1,0:T(8,128)S(1)}, u32[]{:S(2)}, u32[]{:S(2)}) %all-to-all-start.5) | async-done | bytes 524320 | tf_op jit(solution)/shard_map/all_to_all | solution.py:321
  124.6 1.4 weigh_twice.1
  126.0 16.9 %all_to_all.39.got = f32[16,32,512]{2,1,0:T(8,128)S(1)} all-to-all(f32[16,32,512]{2,1,0:T(8,128)S(1)} %weigh_twice.1), channel_id=1, replica_groups={{0,1,2,3,64,65,66,67,128,129,130,131,192,193,194,195},{4,5,6,7,68,69,70..., dimensions={0} | all-to-all | bytes 2097152 | tf_op jit(solution)/shard_map/all_to_all | solution.py:316
  143.0 1.4 last_far.1
  144.3 6.7 %collective-permute-start.5 = (f32[256,256]{1,0:T(8,128)S(1)}, f32[256,256]{1,0:T(8,128)S(1)}, u32[]{:S(2)}, u32[]{:S(2)}) collective-permute-start(f32[256,256]{1,0:T(8,128)S(1)} %last_far.1), channel_id=1, source_target_pairs={{0,32},{32,0},{64,96},{96,64},{128,160},{160,128},{192,224},{224,1... | collective-permute-start | bytes 786440 | tf_op jit(solution)/shard_map/ppermute | solution.py:313
  151.1 1.4 last_near.1.kept
  152.5 0.8 place.1
  (22 shorter events, 0.5 us)
Async XLA Ops:
  0.0 1.0 copy-start.1
  2.1 12.2 %slice-start = ((f32[3,512,256]{2,1,0:T(8,128)}), f32[2,512,256]{2,1,0:T(8,128)S(1)}, s32[]{:S(2)}) async-start(f32[3,512,256]{2,1,0:T(8,128)} %param.6), calls=%async_computation.7 | async-start | bytes 2097152 | tf_op jit(solution)/shard_map/slice | solution.py:341
  2.1 28.5 %all-to-all-start = ((f32[32,16,256]{2,1,0:T(8,128)}), f32[32,16,256]{2,1,0:T(8,128)S(1)}, u32[]{:S(2)}, u32[]{:S(2)}) async-start(f32[32,16,256]{2,1,0:T(8,128)} %cut.1), calls=%async_computation | async-start | bytes 1048576 | tf_op jit(solution)/shard_map/all_to_all | solution.py:335
  14.3 1.9 %slice-start.1 = ((f32[3,512,256]{2,1,0:T(8,128)}), f32[1,512,256]{2,1,0:T(8,128)S(1)}, s32[]{:S(2)}) async-start(f32[3,512,256]{2,1,0:T(8,128)} %param.6), calls=%async_computation.8 | async-start | bytes 1048576 | tf_op jit(solution)/shard_map/slice | solution.py:343
  14.3 1.9 %copy-start.2 = (f32[512,256]{1,0:T(8,128)S(1)}, f32[512,256]{1,0:T(8,128)}, u32[]{:S(2)}) copy-start(f32[512,256]{1,0:T(8,128)} %param.5) | copy-start | bytes 1572868
  15.3 2.3 %copy-start.3 = (f32[256]{0:T(256)S(1)}, f32[256]{0:T(256)}, u32[]{:S(2)}) copy-start(f32[256]{0:T(256)} %param.7) | copy-start | bytes 3076
  15.3 3.8 %collective-permute-start.2 = (f32[2,256,256]{2,1,0:T(8,128)}, f32[2,256,256]{2,1,0:T(8,128)S(1)}, u32[]{:S(2)}, u32[]{:S(2)}) collective-permute-start(f32[2,256,256]{2,1,0:T(8,128)} %get-tuple-element.31), channel_id=1, source_target_pairs={{0,32},{32,0},{64,96},{96,64},{128,160},{160,128},{192,224},{224,1... | collective-permute-start | bytes 1572872 | tf_op jit(solution)/shard_map/ppermute | solution.py:313
  17.1 2.9 %collective-permute-start = (f32[2,256,256]{2,1,0:T(8,128)}, f32[2,256,256]{2,1,0:T(8,128)S(1)}, u32[]{:S(2)}, u32[]{:S(2)}) collective-permute-start(f32[2,256,256]{2,1,0:T(8,128)} %get-tuple-element.34), channel_id=1, source_target_pairs={{0,32},{32,0},{64,96},{96,64},{128,160},{160,128},{192,224},{224,1... | collective-permute-start | bytes 1572872 | tf_op jit(solution)/shard_map/ppermute | solution.py:313
  17.6 1.4 collective-permute-start.1
  30.6 3.9 %collective-permute-start.3 = (f32[512,256]{1,0:T(8,128)S(1)}, f32[512,256]{1,0:T(8,128)S(1)}, u32[]{:S(2)}, u32[]{:S(2)}) collective-permute-start(f32[512,256]{1,0:T(8,128)S(1)} %bitcast.17), channel_id=1, source_target_pairs={{0,32},{32,0},{64,96},{96,64},{128,160},{160,128},{192,224},{224,1... | collective-permute-start | bytes 1572872 | tf_op jit(solution)/shard_map/ppermute | solution.py:313
  70.6 16.2 %copy-start = (f32[256,512]{1,0:T(8,128)S(1)}, f32[256,512]{1,0:T(8,128)}, u32[]{:S(2)}) copy-start(f32[256,512]{1,0:T(8,128)} %get-tuple-element.21.noise) | copy-start | bytes 1572868
  107.0 17.7 %all-to-all-start.5 = ((f32[8,32,512]{2,1,0:T(8,128)}), f32[8,32,512]{2,1,0:T(8,128)S(1)}, u32[]{:S(2)}, u32[]{:S(2)}) async-start(f32[8,32,512]{2,1,0:T(8,128)} %spread.3), calls=%async_computation.5 | async-start | bytes 1048576 | tf_op jit(solution)/shard_map/all_to_all | solution.py:321
  112.6 6.2 %collective-permute-start.4 = (f32[128,640]{1,0:T(8,128)S(1)}, f32[128,640]{1,0:T(8,128)S(1)}, u32[]{:S(2)}, u32[]{:S(2)}) collective-permute-start(f32[128,640]{1,0:T(8,128)S(1)} %bitcast.26), channel_id=1, source_target_pairs={{0,32},{32,0},{64,96},{96,64},{128,160},{160,128},{192,224},{224,1... | collective-permute-start | bytes 983048 | tf_op jit(solution)/shard_map/ppermute | solution.py:313
  144.3 8.1 %collective-permute-start.5 = (f32[256,256]{1,0:T(8,128)S(1)}, f32[256,256]{1,0:T(8,128)S(1)}, u32[]{:S(2)}, u32[]{:S(2)}) collective-permute-start(f32[256,256]{1,0:T(8,128)S(1)} %last_far.1), channel_id=1, source_target_pairs={{0,32},{32,0},{64,96},{96,64},{128,160},{160,128},{192,224},{224,1... | collective-permute-start | bytes 786440 | tf_op jit(solution)/shard_map/ppermute | solution.py:313

commit v9 on v7

--- a/solution.py
+++ b/solution.py
@@ -9,7 +9,7 @@
 from jax.sharding import PartitionSpec as P
 
 ITERS = 3
-DEPTH = 8
+DEPTH = 4
 AXES = ("space", "mem")
 VMEM = pl.BlockSpec(memory_space=pltpu.VMEM)
 SMEM = pl.BlockSpec(memory_space=pltpu.SMEM)
@@ -88,22 +88,52 @@
     return jnp.concatenate([low, high])
 
 
+def thirds(array):
+    high = array.astype(jnp.bfloat16)
+    rest = array - high.astype(jnp.float32)
+    mid = rest.astype(jnp.bfloat16)
+    return high, mid, (rest - mid.astype(jnp.float32)).astype(jnp.bfloat16)
+
+
 def times_pairs(first, w, near, far):
-    rows = near.shape[0] // 2
-    low, high = w[:, : 2 * rows], w[:, 2 * rows :]
+    size, rows = near.shape[0] // 2, w.shape[0]
+    low, high = w[:, : 2 * size], w[:, 2 * size :]
     w = jnp.where(first, w, jnp.concatenate([high, low], axis=1))
-    parts = [w[:, i * rows : (i + 1) * rows] for i in range(4)]
-    packed = [near[:rows], near[rows:], far[:rows], far[rows:]]
-    sums = [product(parts[(i + 1) % 4], packed[i][:, rows : 2 * rows], 1) for i in range(4)]
-    for i in range(4):
-        ahead = product(parts[i], packed[i], 0)
-        for k in range(3):
-            sums[(i + k) % 4] += ahead[:, k * rows : (k + 1) * rows]
-    low = jnp.concatenate(sums[:2], axis=1)
-    high = jnp.concatenate(sums[2:], axis=1)
-    return jnp.concatenate(
-        [jnp.where(first, low, high), jnp.where(first, high, low)], axis=1
-    )
+    w_high, w_mid, w_low = thirds(w)
+    stacks = (
+        jnp.concatenate([w_high, w_mid, w_low]),
+        jnp.concatenate([w_high, w_mid]),
+        w_high,
+    )
+    results = []
+    packed = [thirds(half_pairs) for half_pairs in (near, far)]
+    for third, stack in enumerate(stacks):
+        parts = [stack[:, i * size : (i + 1) * size] for i in range(4)]
+        sums = [[] for _ in range(4)]
+        for i in range(4):
+            block = packed[i // 2][third][(i % 2) * size : (i % 2 + 1) * size]
+            ahead = lax.dot_general(
+                parts[i],
+                block,
+                (((1,), (0,)), ((), ())),
+                preferred_element_type=jnp.float32,
+            )
+            for k in range(3):
+                sums[(i + k) % 4].append(ahead[:, k * size : (k + 1) * size])
+            sums[i].append(
+                lax.dot_general(
+                    parts[(i + 1) % 4],
+                    block[:, size : 2 * size],
+                    (((1,), (1,)), ((), ())),
+                    preferred_element_type=jnp.float32,
+                )
+            )
+        results.append(jnp.concatenate([tree_sum(t) for t in sums], axis=1))
+    p, q, r = results
+    small = p[2 * rows :] + q[rows:] + r
+    total = (small + (p[rows : 2 * rows] + q[:rows])) + p[:rows]
+    low, high = total[:, : 2 * size], total[:, 2 * size :]
+    return jnp.where(first, total, jnp.concatenate([high, low], axis=1))
 
 
 def my_members(core, members):
@@ -260,13 +290,22 @@
     core = lax.rem(lax.axis_index("space"), 2)
     core_ref = core.astype(jnp.int32).reshape(1)
     swap = [(i, i ^ 1) for i in range(space)]
-    span = mem // DEPTH
+    span, pair = 4, mem // 4 // DEPTH
     planes = [
-        [s * mem + z * span + y for s in range(c, space, 2) for y in range(span)]
+        [
+            s * mem + (k * pair + z) * span + y
+            for s in range(c, space, 2)
+            for z in range(pair)
+            for y in range(span)
+        ]
         for c in range(2)
-        for z in range(DEPTH)
+        for k in range(DEPTH)
     ]
-    columns = [[z * span + y for z in range(DEPTH)] for y in range(span)]
+    columns = [
+        [(k * pair + z) * span + y for k in range(DEPTH)]
+        for z in range(pair)
+        for y in range(span)
+    ]
     peers = len(planes[0])
 
     def other_core(array):

time: 156 us -> 147 us (0.942)
  blocking collectives: 84.7 us -> 62.9 us
  waiting for transfers between devices: 18.5 us -> 29.1 us
    all_to_all x4 -> x3, blocking collectives: 69.6 us -> 53.1 us  [in_plane(): lax.all_to_all(blocks, AXES, split_axis=0, concat_axis=0, axis_index_grou...]
    all_to_all x0 -> x1, waiting for transfers between devices: none -> 10.2 us  [in_plane(): lax.all_to_all(blocks, AXES, split_axis=0, concat_axis=0, axis_index_grou...]
    all_to_all x1, blocking collectives: 15.2 us -> 9.73 us  [in_column(): lax.all_to_all(blocks, 'mem', split_axis=0, concat_axis=0, axis_index_gro...]
    all_to_all x0 -> x1, starting transfers between devices: none -> 4.52 us  [in_plane(): lax.all_to_all(blocks, AXES, split_axis=0, concat_axis=0, axis_index_grou...]
    all_to_all x1, starting transfers between devices: 5.65 us -> 3.33 us  [in_column(): lax.all_to_all(blocks, 'mem', split_axis=0, concat_axis=0, axis_index_gro...]
    all_to_all x1, waiting for transfers between devices: 5.53 us -> 7.18 us  [in_column(): lax.all_to_all(blocks, 'mem', split_axis=0, concat_axis=0, axis_index_gro...]
  transfers between devices with their start and end apart: 8 -> 9, of which waited for: 5 -> 5; matrix products, arithmetic and copies ran while one was open for 2% -> 2% of each run, Pallas kernels for 2% -> 2%
where the time goes in v9:
time: 147 us; the launch traced here: 146 us
  blocking collectives  62.9 us (43%)
  starting transfers between devices  34.7 us (24%)
  waiting for transfers between devices  29.1 us (20%)
  Pallas kernels  14.3 us (10%)
  other arithmetic  2.79 us (2%)
  local copies, waits for them, and re-layouts  2 us (1%)
    all_to_all x3, blocking collectives, in_plane(): lax.all_to_all(blocks, AXES, split_axis=0, concat_axis=0, axis_index_grou...  53.1 us
    ppermute x6, starting transfers between devices, other_core(): return lax.ppermute(array, 'space', swap)  14.7 us
    pallas_call x11, Pallas kernels, call(): pl.pallas_call(kernel, out_shape=shapes, in_specs=[SMEM if a.dtype == jnp...  14.3 us
    all_to_all x1, starting transfers between devices, per_device(): own = lax.all_to_all(cut, 'mem', split_axis=0, concat_axis=0)  12.2 us
    all_to_all x1, waiting for transfers between devices, in_plane(): lax.all_to_all(blocks, AXES, split_axis=0, concat_axis=0, axis_index_grou...  10.2 us
    all_to_all x1, waiting for transfers between devices, per_device(): own = lax.all_to_all(cut, 'mem', split_axis=0, concat_axis=0)  9.95 us
    all_to_all x1, blocking collectives, in_column(): lax.all_to_all(blocks, 'mem', split_axis=0, concat_axis=0, axis_index_gro...  9.73 us
    all_to_all x1, waiting for transfers between devices, in_column(): lax.all_to_all(blocks, 'mem', split_axis=0, concat_axis=0, axis_index_gro...  7.18 us
  transfers between devices with their start and end apart: 9, of which 5 were waited for; matrix products, arithmetic and copies ran while one was open for 2% of the time, Pallas kernels for 2%

profile of v9, /device:TPU:1, one launch (start us, length us, event | category | flops | bytes accessed | tf_op | source)
XLA Modules:
  0.0 145.9 jit_solution(15566707990964046682)
XLA Ops:
  0.0 1.0 copy-done.1
  1.0 1.1 cut.1
  2.1 12.2 %all-to-all-start = ((f32[32,16,256]{2,1,0:T(8,128)}), f32[32,16,256]{2,1,0:T(8,128)S(1)}, u32[]{:S(2)}, u32[]{:S(2)}) async-start(f32[32,16,256]{2,1,0:T(8,128)} %cut.1), calls=%async_computation | async-start | bytes 1048576 | tf_op jit(solution)/shard_map/all_to_all | solution.py:334
  14.3 0.9 constant_dynamic-slice_fusion
  15.3 1.0 collective-permute-start.2
  16.2 0.9 fusion.14
  17.1 0.5 collective-permute-start
  17.6 1.4 collective-permute-done.1
  19.0 1.0 fusion.15
  20.0 0.7 fusion.8
  20.6 10.0 %all-to-all-done = f32[32,16,256]{2,1,0:T(8,128)S(1)} async-done(((f32[32,16,256]{2,1,0:T(8,128)}), f32[32,16,256]{2,1,0:T(8,128)S(1)}, u32[]{:S(2)}, u32[]{:S(2)}) %all-to-all-start) | async-done | bytes 524320 | tf_op jit(solution)/shard_map/all_to_all | solution.py:334
  30.6 2.4 %collective-permute-start.3 = (f32[512,256]{1,0:T(8,128)S(1)}, f32[512,256]{1,0:T(8,128)S(1)}, u32[]{:S(2)}, u32[]{:S(2)}) collective-permute-start(f32[512,256]{1,0:T(8,128)S(1)} %bitcast.17), channel_id=1, source_target_pairs={{0,32},{32,0},{64,96},{96,64},{128,160},{160,128},{192,224},{224,1... | collective-permute-start | bytes 1572872 | tf_op jit(solution)/shard_map/ppermute | solution.py:312
  33.0 1.0 own.1.gram_own
  34.2 0.3 collective-permute-done.3.far
  34.7 1.1 first.1
  35.8 20.5 %all_to_all.35.got = f32[32,8,896]{2,1,0:T(8,128)S(1)} all-to-all(f32[32,8,896]{2,1,0:T(8,128)S(1)} %get-tuple-element.18), channel_id=1, replica_groups={{0,1,2,3,4,5,6,7,64,65,66,67,68,69,70,71,128,129,130,131,132,133,134,13..., dimensions={0} | all-to-all | bytes 1835008 | tf_op jit(solution)/shard_map/all_to_all | solution.py:315
  56.3 9.7 %all_to_all.36.got = f32[4,8,896]{2,1,0:T(8,128)S(1)} all-to-all(f32[4,8,896]{2,1,0:T(8,128)S(1)} %spread.2), channel_id=1, replica_groups={{0,8,16,24},{1,9,17,25},{2,10,18,26},{3,11,19,27},{4,12,20,28},{5,13,21..., dimensions={0} | all-to-all | bytes 229376 | tf_op jit(solution)/shard_map/all_to_all | solution.py:320
  66.0 0.2 weigh.1
  66.3 17.1 %all_to_all.37.got = f32[32,8,896]{2,1,0:T(8,128)S(1)} all-to-all(f32[32,8,896]{2,1,0:T(8,128)S(1)} %weigh.1), channel_id=1, replica_groups={{0,1,2,3,4,5,6,7,64,65,66,67,68,69,70,71,128,129,130,131,132,133,134,13..., dimensions={0} | all-to-all | bytes 1835008 | tf_op jit(solution)/shard_map/all_to_all | solution.py:315
  83.3 4.6 %step.1 = (f32[32,16,512]{2,1,0:T(8,128)}, f32[256,512]{1,0:T(8,128)S(1)}, f32[32,8,384]{2,1,0:T(8,128)S(1)}) custom-call(f32[32,8,896]{2,1,0:T(8,128)S(1)} %all_to_all.37.got, f32[512,512]{1,0:T(8,128)S(1)} %get-tuple-element.19.members, f32[256,512]{1,0:T(8,128)S(1)} %get-tuple-element.20.u, f32[256,512]{1,0:T(8,128)S(1)} %copy-done, ...), custom_call_target="tpu_custom_call" | custom-call | flops 2415919104 | bytes 1966080 | tf_op jit(solution)/shard_map/step/pallas_call | solution.py:261
  88.0 4.5 %all-to-all-start.4 = ((f32[32,16,512]{2,1,0:T(8,128)}), f32[32,16,512]{2,1,0:T(8,128)S(1)}, u32[]{:S(2)}, u32[]{:S(2)}) async-start(f32[32,16,512]{2,1,0:T(8,128)} %get-tuple-element.23), calls=%async_computation.4 | async-start | bytes 2097152 | tf_op jit(solution)/shard_map/all_to_all | solution.py:315
  92.5 3.8 %collective-permute-start.4 = (f32[256,384]{1,0:T(8,128)S(1)}, f32[256,384]{1,0:T(8,128)}, u32[]{:S(2)}, u32[]{:S(2)}) collective-permute-start(f32[256,384]{1,0:T(8,128)S(1)} %bitcast.26), channel_id=1, source_target_pairs={{0,32},{32,0},{64,96},{96,64},{128,160},{160,128},{192,224},{224,1... | collective-permute-start | bytes 1179656 | tf_op jit(solution)/shard_map/ppermute | solution.py:312
  96.3 10.2 %all-to-all-done.4.got = f32[32,16,512]{2,1,0:T(8,128)S(1)} async-done(((f32[32,16,512]{2,1,0:T(8,128)}), f32[32,16,512]{2,1,0:T(8,128)S(1)}, u32[]{:S(2)}, u32[]{:S(2)}) %all-to-all-start.4) | async-done | bytes 1048608 | tf_op jit(solution)/shard_map/all_to_all | solution.py:315
  106.5 0.7 spread.3
  107.3 3.3 %all-to-all-start.5 = ((f32[4,16,512]{2,1,0:T(8,128)}), f32[4,16,512]{2,1,0:T(8,128)S(1)}, u32[]{:S(2)}, u32[]{:S(2)}) async-start(f32[4,16,512]{2,1,0:T(8,128)} %spread.3), calls=%async_computation.5 | async-start | bytes 262144 | tf_op jit(solution)/shard_map/all_to_all | solution.py:320
  110.6 7.2 %all-to-all-done.5.got = f32[4,16,512]{2,1,0:T(8,128)S(1)} async-done(((f32[4,16,512]{2,1,0:T(8,128)}), f32[4,16,512]{2,1,0:T(8,128)S(1)}, u32[]{:S(2)}, u32[]{:S(2)}) %all-to-all-start.5) | async-done | bytes 131104 | tf_op jit(solution)/shard_map/all_to_all | solution.py:320
  117.8 1.9 %weigh_twice.1 = f32[32,16,512]{2,1,0:T(8,128)S(1)} custom-call(s32[1]{0:T(128)} %bitcast.core, f32[4,16,512]{2,1,0:T(8,128)S(1)} %all-to-all-done.5.got, f32[256,384]{1,0:T(8,128)S(1)} %bitcast.27, f32[256,384]{1,0:T(8,128)} %collective-permute-done.4.far_in), custom_call_target="tpu_custom_call" | custom-call | flops 805306368 | bytes 1048576 | tf_op jit(solution)/shard_map/weigh_twice/pallas_call | solution.py:261
  119.7 15.6 %all_to_all.38.got = f32[32,16,512]{2,1,0:T(8,128)S(1)} all-to-all(f32[32,16,512]{2,1,0:T(8,128)S(1)} %weigh_twice.1), channel_id=1, replica_groups={{0,1,2,3,4,5,6,7,64,65,66,67,68,69,70,71,128,129,130,131,132,133,134,13..., dimensions={0} | all-to-all | bytes 2097152 | tf_op jit(solution)/shard_map/all_to_all | solution.py:315
  135.3 1.4 last_far.1
  136.7 7.0 %collective-permute-start.5 = (f32[256,256]{1,0:T(8,128)S(1)}, f32[256,256]{1,0:T(8,128)S(1)}, u32[]{:S(2)}, u32[]{:S(2)}) collective-permute-start(f32[256,256]{1,0:T(8,128)S(1)} %last_far.1), channel_id=1, source_target_pairs={{0,32},{32,0},{64,96},{96,64},{128,160},{160,128},{192,224},{224,1... | collective-permute-start | bytes 786440 | tf_op jit(solution)/shard_map/ppermute | solution.py:312
  143.7 1.4 last_near.1.kept
  145.1 0.8 place.1
  (23 shorter events, 0.5 us)
Async XLA Ops:
  0.0 1.0 copy-start.1
  2.1 12.2 %slice-start = ((f32[3,512,256]{2,1,0:T(8,128)}), f32[2,512,256]{2,1,0:T(8,128)S(1)}, s32[]{:S(2)}) async-start(f32[3,512,256]{2,1,0:T(8,128)} %param.6), calls=%async_computation.7 | async-start | bytes 2097152 | tf_op jit(solution)/shard_map/slice | solution.py:340
  2.1 28.5 %all-to-all-start = ((f32[32,16,256]{2,1,0:T(8,128)}), f32[32,16,256]{2,1,0:T(8,128)S(1)}, u32[]{:S(2)}, u32[]{:S(2)}) async-start(f32[32,16,256]{2,1,0:T(8,128)} %cut.1), calls=%async_computation | async-start | bytes 1048576 | tf_op jit(solution)/shard_map/all_to_all | solution.py:334
  14.3 1.9 %slice-start.1 = ((f32[3,512,256]{2,1,0:T(8,128)}), f32[1,512,256]{2,1,0:T(8,128)S(1)}, s32[]{:S(2)}) async-start(f32[3,512,256]{2,1,0:T(8,128)} %param.6), calls=%async_computation.8 | async-start | bytes 1048576 | tf_op jit(solution)/shard_map/slice | solution.py:342
  14.3 1.9 %copy-start.2 = (f32[512,256]{1,0:T(8,128)S(1)}, f32[512,256]{1,0:T(8,128)}, u32[]{:S(2)}) copy-start(f32[512,256]{1,0:T(8,128)} %param.5) | copy-start | bytes 1572868
  15.3 2.3 %copy-start.3 = (f32[256]{0:T(256)S(1)}, f32[256]{0:T(256)}, u32[]{:S(2)}) copy-start(f32[256]{0:T(256)} %param.7) | copy-start | bytes 3076
  15.3 3.8 %collective-permute-start.2 = (f32[2,256,256]{2,1,0:T(8,128)}, f32[2,256,256]{2,1,0:T(8,128)S(1)}, u32[]{:S(2)}, u32[]{:S(2)}) collective-permute-start(f32[2,256,256]{2,1,0:T(8,128)} %get-tuple-element.31), channel_id=1, source_target_pairs={{0,32},{32,0},{64,96},{96,64},{128,160},{160,128},{192,224},{224,1... | collective-permute-start | bytes 1572872 | tf_op jit(solution)/shard_map/ppermute | solution.py:312
  17.1 2.9 %collective-permute-start = (f32[2,256,256]{2,1,0:T(8,128)}, f32[2,256,256]{2,1,0:T(8,128)S(1)}, u32[]{:S(2)}, u32[]{:S(2)}) collective-permute-start(f32[2,256,256]{2,1,0:T(8,128)} %get-tuple-element.34), channel_id=1, source_target_pairs={{0,32},{32,0},{64,96},{96,64},{128,160},{160,128},{192,224},{224,1... | collective-permute-start | bytes 1572872 | tf_op jit(solution)/shard_map/ppermute | solution.py:312
  17.6 1.4 collective-permute-start.1
  30.6 3.9 %collective-permute-start.3 = (f32[512,256]{1,0:T(8,128)S(1)}, f32[512,256]{1,0:T(8,128)S(1)}, u32[]{:S(2)}, u32[]{:S(2)}) collective-permute-start(f32[512,256]{1,0:T(8,128)S(1)} %bitcast.17), channel_id=1, source_target_pairs={{0,32},{32,0},{64,96},{96,64},{128,160},{160,128},{192,224},{224,1... | collective-permute-start | bytes 1572872 | tf_op jit(solution)/shard_map/ppermute | solution.py:312
  66.3 17.1 %copy-start = (f32[256,512]{1,0:T(8,128)S(1)}, f32[256,512]{1,0:T(8,128)}, u32[]{:S(2)}) copy-start(f32[256,512]{1,0:T(8,128)} %get-tuple-element.21.noise) | copy-start | bytes 1572868
  88.0 18.6 %all-to-all-start.4 = ((f32[32,16,512]{2,1,0:T(8,128)}), f32[32,16,512]{2,1,0:T(8,128)S(1)}, u32[]{:S(2)}, u32[]{:S(2)}) async-start(f32[32,16,512]{2,1,0:T(8,128)} %get-tuple-element.23), calls=%async_computation.4 | async-start | bytes 2097152 | tf_op jit(solution)/shard_map/all_to_all | solution.py:315
  92.5 18.1 %collective-permute-start.4 = (f32[256,384]{1,0:T(8,128)S(1)}, f32[256,384]{1,0:T(8,128)}, u32[]{:S(2)}, u32[]{:S(2)}) collective-permute-start(f32[256,384]{1,0:T(8,128)S(1)} %bitcast.26), channel_id=1, source_target_pairs={{0,32},{32,0},{64,96},{96,64},{128,160},{160,128},{192,224},{224,1... | collective-permute-start | bytes 1179656 | tf_op jit(solution)/shard_map/ppermute | solution.py:312
  107.3 10.5 %all-to-all-start.5 = ((f32[4,16,512]{2,1,0:T(8,128)}), f32[4,16,512]{2,1,0:T(8,128)S(1)}, u32[]{:S(2)}, u32[]{:S(2)}) async-start(f32[4,16,512]{2,1,0:T(8,128)} %spread.3), calls=%async_computation.5 | async-start | bytes 262144 | tf_op jit(solution)/shard_map/all_to_all | solution.py:320
  136.7 8.4 %collective-permute-start.5 = (f32[256,256]{1,0:T(8,128)S(1)}, f32[256,256]{1,0:T(8,128)S(1)}, u32[]{:S(2)}, u32[]{:S(2)}) collective-permute-start(f32[256,256]{1,0:T(8,128)S(1)} %last_far.1), channel_id=1, source_target_pairs={{0,32},{32,0},{64,96},{96,64},{128,160},{160,128},{192,224},{224,1... | collective-permute-start | bytes 786440 | tf_op jit(solution)/shard_map/ppermute | solution.py:312

commit v10 on v9

--- a/solution.py
+++ b/solution.py
@@ -36,14 +36,30 @@
 A2, T2, KEEP2, GAIN2, PULL2, NOISE2 = constants(2)
 
 
+def thirds(array):
+    high = array.astype(jnp.bfloat16)
+    rest = array - high.astype(jnp.float32)
+    mid = rest.astype(jnp.bfloat16)
+    return high, mid, (rest - mid.astype(jnp.float32)).astype(jnp.bfloat16)
+
+
 def product(a, b, axis):
-    return lax.dot_general(
-        a,
-        b,
-        (((1,), (axis,)), ((), ())),
-        precision=lax.Precision.HIGHEST,
-        preferred_element_type=jnp.float32,
-    )
+    rows = a.shape[0]
+    high, mid, low = thirds(a)
+
+    def one(left, right):
+        return lax.dot_general(
+            left,
+            right,
+            (((1,), (axis,)), ((), ())),
+            preferred_element_type=jnp.float32,
+        )
+
+    b_high, b_mid, b_low = thirds(b)
+    p = one(jnp.concatenate([high, mid, low]), b_high)
+    q = one(jnp.concatenate([high, mid]), b_mid)
+    small = p[2 * rows :] + q[rows:] + one(high, b_low)
+    return (small + (p[rows : 2 * rows] + q[:rows])) + p[:rows]
 
 
 def misfit(z, angles):
@@ -86,13 +102,6 @@
     low = jnp.where(first, blocks(low, 0), blocks(low, 2))
     high = jnp.where(first, blocks(high, 1), blocks(high, 3))
     return jnp.concatenate([low, high])
-
-
-def thirds(array):
-    high = array.astype(jnp.bfloat16)
-    rest = array - high.astype(jnp.float32)
-    mid = rest.astype(jnp.bfloat16)
-    return high, mid, (rest - mid.astype(jnp.float32)).astype(jnp.bfloat16)
 
 
 def times_pairs(first, w, near, far):
@@ -256,7 +265,7 @@
         copy.wait()
 
 
-def call(kernel, name, outs, *args, products=1, anywhere=(), scratch=()):
+def call(kernel, name, outs, *args, products=0, anywhere=(), scratch=()):
     shapes = tuple(jax.ShapeDtypeStruct(s, jnp.float32) for s in outs)
     result = pl.pallas_call(
         kernel,
@@ -294,8 +303,8 @@
     planes = [
         [
             s * mem + (k * pair + z) * span + y
+            for z in range(pair)
             for s in range(c, space, 2)
-            for z in range(pair)
             for y in range(span)
         ]
         for c in range(2)
@@ -355,7 +364,7 @@
     wide = (peers, 2 * rows, total)
     deep = (DEPTH, 2 * rows, total)
 
-    gram_own = call(own_kernel, "own", [(2 * count, total)], core_ref, own, z0)
+    gram_own = call(own_kernel, "own", [(2 * count, total)], core_ref, own, z0, products=1)
     members, blocks = call(
         first_kernel,
         "first",
@@ -366,6 +375,7 @@
         z0,
         lengths,
         gram_own,
+        products=1,
     )
     blocks = call(
         spread_kernel, "spread", [(DEPTH, rows, total + packed)], in_plane(blocks)
@@ -404,10 +414,10 @@
     )
     blocks = in_plane(blocks)
     last = functools.partial(last_kernel, width)
-    sent = call(last, "last_far", [(count, width)], blocks, members, y, e2, angles)
+    sent = call(last, "last_far", [(count, width)], blocks, members, y, e2, angles, products=1)
     back = other_core(sent)
     last = functools.partial(last_kernel, 0)
-    kept = call(last, "last_near", [(count, width)], blocks, members, y, e2, angles)
+    kept = call(last, "last_near", [(count, width)], blocks, members, y, e2, angles, products=1)
     return call(place_kernel, "place", [(2 * count, width)], core_ref, kept, back)
 
 

time: 147 us -> 146 us (level)
  waiting for transfers between devices: 29.1 us -> 24.6 us
  local copies, waits for them, and re-layouts: 2 us -> 3.81 us
  starting transfers between devices: 34.7 us -> 36.2 us
    all_to_all x1, waiting for transfers between devices: 10.2 us -> 7.28 us  [in_plane(): lax.all_to_all(blocks, AXES, split_axis=0, concat_axis=0, axis_index_grou...]
    all_to_all x1, waiting for transfers between devices: 9.95 us -> 8.08 us  [per_device(): own = lax.all_to_all(cut, 'mem', split_axis=0, concat_axis=0)]
    unnamed x9 -> x13, local copies, waits for them, and re-layouts: 1.07 us -> 2.86 us
  transfers between devices with their start and end apart: 9 -> 9, of which waited for: 5 -> 5; matrix products, arithmetic and copies ran while one was open for 2% -> 3% of each run, Pallas kernels for 2% -> 2%
where the time goes in v10:
time: 146 us; the launch traced here: 145 us
  blocking collectives  63.3 us (43%)
  starting transfers between devices  36.2 us (25%)
  waiting for transfers between devices  24.6 us (17%)
  Pallas kernels  13 us (9%)
  other arithmetic  3.83 us (3%)
  local copies, waits for them, and re-layouts  3.81 us (3%)
    all_to_all x3, blocking collectives, in_plane(): lax.all_to_all(blocks, AXES, split_axis=0, concat_axis=0, axis_index_grou...  53.5 us
    ppermute x6, starting transfers between devices, other_core(): return lax.ppermute(array, 'space', swap)  15.4 us
    pallas_call x11, Pallas kernels, call(): pl.pallas_call(kernel, out_shape=shapes, in_specs=[SMEM if a.dtype == jnp...  13 us
    all_to_all x1, starting transfers between devices, per_device(): own = lax.all_to_all(cut, 'mem', split_axis=0, concat_axis=0)  12.2 us
    all_to_all x1, blocking collectives, in_column(): lax.all_to_all(blocks, 'mem', split_axis=0, concat_axis=0, axis_index_gro...  9.85 us
    all_to_all x1, waiting for transfers between devices, per_device(): own = lax.all_to_all(cut, 'mem', split_axis=0, concat_axis=0)  8.08 us
    all_to_all x1, waiting for transfers between devices, in_column(): lax.all_to_all(blocks, 'mem', split_axis=0, concat_axis=0, axis_index_gro...  7.51 us
    all_to_all x1, waiting for transfers between devices, in_plane(): lax.all_to_all(blocks, AXES, split_axis=0, concat_axis=0, axis_index_grou...  7.28 us
  transfers between devices with their start and end apart: 9, of which 5 were waited for; matrix products, arithmetic and copies ran while one was open for 3% of the time, Pallas kernels for 2%

profile of v10, /device:TPU:1, one launch (start us, length us, event | category | flops | bytes accessed | tf_op | source)
XLA Modules:
  0.0 145.0 jit_solution(3912682385087825028)
XLA Ops:
  0.0 1.0 copy-done.1
  1.0 1.1 cut.1
  2.1 12.2 %all-to-all-start = ((f32[32,16,256]{2,1,0:T(8,128)}), f32[32,16,256]{2,1,0:T(8,128)S(1)}, u32[]{:S(2)}, u32[]{:S(2)}) async-start(f32[32,16,256]{2,1,0:T(8,128)} %cut.1), calls=%async_computation | async-start | bytes 1048576 | tf_op jit(solution)/shard_map/all_to_all | solution.py:343
  14.3 0.9 constant_dynamic-slice_fusion
  15.3 1.0 collective-permute-start.2
  16.2 0.9 fusion.14
  17.1 0.4 collective-permute-start
  17.6 1.4 collective-permute-done.1
  19.0 1.0 fusion.15
  20.0 0.8 copy-done.3
  20.8 1.7 %fusion.8 = (f32[256,512]{1,0:T(8,128)S(1)}, f32[256,512]{1,0:T(8,128)S(1)}) fusion(f32[2,256,256]{2,1,0:T(8,128)} %copy-done.3, f32[2,256,256]{2,1,0:T(8,128)S(1)} %get-tuple-element.33, f32[512]{0:T(512)S(1)} %constant_dynamic-update-slice_fusion), kind=kLoop, calls=%fused_computation.19 | loop fusion | flops 5242880 | bytes 2099200 | tf_op jit(solution)/shard_map/add | solution.py:354
  22.5 8.1 %all-to-all-done = f32[32,16,256]{2,1,0:T(8,128)S(1)} async-done(((f32[32,16,256]{2,1,0:T(8,128)}), f32[32,16,256]{2,1,0:T(8,128)S(1)}, u32[]{:S(2)}, u32[]{:S(2)}) %all-to-all-start) | async-done | bytes 524320 | tf_op jit(solution)/shard_map/all_to_all | solution.py:343
  30.6 2.4 %collective-permute-start.3 = (f32[512,256]{1,0:T(8,128)S(1)}, f32[512,256]{1,0:T(8,128)S(1)}, u32[]{:S(2)}, u32[]{:S(2)}) collective-permute-start(f32[512,256]{1,0:T(8,128)S(1)} %bitcast.17), channel_id=1, source_target_pairs={{0,32},{32,0},{64,96},{96,64},{128,160},{160,128},{192,224},{224,1... | collective-permute-start | bytes 1572872 | tf_op jit(solution)/shard_map/ppermute | solution.py:321
  33.0 1.0 own.1.gram_own
  34.7 1.1 first.1
  35.8 20.0 %all_to_all.35.got = f32[32,8,896]{2,1,0:T(8,128)S(1)} all-to-all(f32[32,8,896]{2,1,0:T(8,128)S(1)} %get-tuple-element.18), channel_id=1, replica_groups={{0,1,2,3,64,65,66,67,128,129,130,131,192,193,194,195,4,5,6,7,68,69,70,7..., dimensions={0} | all-to-all | bytes 1835008 | tf_op jit(solution)/shard_map/all_to_all | solution.py:324
  55.8 9.9 %all_to_all.36.got = f32[4,8,896]{2,1,0:T(8,128)S(1)} all-to-all(f32[4,8,896]{2,1,0:T(8,128)S(1)} %spread.2), channel_id=1, replica_groups={{0,8,16,24},{1,9,17,25},{2,10,18,26},{3,11,19,27},{4,12,20,28},{5,13,21..., dimensions={0} | all-to-all | bytes 229376 | tf_op jit(solution)/shard_map/all_to_all | solution.py:329
  65.8 16.7 %all_to_all.37.got = f32[32,8,896]{2,1,0:T(8,128)S(1)} all-to-all(f32[32,8,896]{2,1,0:T(8,128)S(1)} %weigh.1), channel_id=1, replica_groups={{0,1,2,3,64,65,66,67,128,129,130,131,192,193,194,195,4,5,6,7,68,69,70,7..., dimensions={0} | all-to-all | bytes 1835008 | tf_op jit(solution)/shard_map/all_to_all | solution.py:324
  82.6 3.5 %step.1 = (f32[32,16,512]{2,1,0:T(8,128)S(1)}, f32[256,512]{1,0:T(8,128)S(1)}, f32[32,8,384]{2,1,0:T(8,128)S(1)}) custom-call(f32[32,8,896]{2,1,0:T(8,128)S(1)} %all_to_all.37.got, f32[512,512]{1,0:T(8,128)S(1)} %get-tuple-element.19.members, f32[256,512]{1,0:T(8,128)S(1)} %get-tuple-element.20.u, f32[256,512]{1,0:T(8,128)S(1)} %copy-done.2, ...), custom_call_target="tpu_custom_call" | custom-call | flops 2415919104 | bytes 1966080 | tf_op jit(solution)/shard_map/step/pallas_call | solution.py:270
  86.1 1.0 copy-done
  87.1 5.3 %all-to-all-start.4 = ((f32[32,16,512]{2,1,0:T(8,128)}), f32[32,16,512]{2,1,0:T(8,128)S(1)}, u32[]{:S(2)}, u32[]{:S(2)}) async-start(f32[32,16,512]{2,1,0:T(8,128)} %copy-done), calls=%async_computation.4 | async-start | bytes 2097152 | tf_op jit(solution)/shard_map/all_to_all | solution.py:324
  92.4 4.3 %collective-permute-start.4 = (f32[256,384]{1,0:T(8,128)S(1)}, f32[256,384]{1,0:T(8,128)}, u32[]{:S(2)}, u32[]{:S(2)}) collective-permute-start(f32[256,384]{1,0:T(8,128)S(1)} %bitcast.21), channel_id=1, source_target_pairs={{0,32},{32,0},{64,96},{96,64},{128,160},{160,128},{192,224},{224,1... | collective-permute-start | bytes 1179656 | tf_op jit(solution)/shard_map/ppermute | solution.py:321
  96.7 7.3 %all-to-all-done.4.got = f32[32,16,512]{2,1,0:T(8,128)S(1)} async-done(((f32[32,16,512]{2,1,0:T(8,128)}), f32[32,16,512]{2,1,0:T(8,128)S(1)}, u32[]{:S(2)}, u32[]{:S(2)}) %all-to-all-start.4) | async-done | bytes 1048608 | tf_op jit(solution)/shard_map/all_to_all | solution.py:324
  104.0 0.7 spread.3
  104.7 3.3 %all-to-all-start.5 = ((f32[4,16,512]{2,1,0:T(8,128)}), f32[4,16,512]{2,1,0:T(8,128)S(1)}, u32[]{:S(2)}, u32[]{:S(2)}) async-start(f32[4,16,512]{2,1,0:T(8,128)} %spread.3), calls=%async_computation.5 | async-start | bytes 262144 | tf_op jit(solution)/shard_map/all_to_all | solution.py:329
  108.1 7.5 %all-to-all-done.5.got = f32[4,16,512]{2,1,0:T(8,128)S(1)} async-done(((f32[4,16,512]{2,1,0:T(8,128)}), f32[4,16,512]{2,1,0:T(8,128)S(1)}, u32[]{:S(2)}, u32[]{:S(2)}) %all-to-all-start.5) | async-done | bytes 131104 | tf_op jit(solution)/shard_map/all_to_all | solution.py:329
  115.6 1.9 %weigh_twice.1 = f32[32,16,512]{2,1,0:T(8,128)S(1)} custom-call(s32[1]{0:T(128)} %bitcast.core, f32[4,16,512]{2,1,0:T(8,128)S(1)} %all-to-all-done.5.got, f32[256,384]{1,0:T(8,128)S(1)} %bitcast.22, f32[256,384]{1,0:T(8,128)} %collective-permute-done.4.far_in), custom_call_target="tpu_custom_call" | custom-call | bytes 1048576 | tf_op jit(solution)/shard_map/weigh_twice/pallas_call | solution.py:270
  117.6 16.8 %all_to_all.38.got = f32[32,16,512]{2,1,0:T(8,128)S(1)} all-to-all(f32[32,16,512]{2,1,0:T(8,128)S(1)} %weigh_twice.1), channel_id=1, replica_groups={{0,1,2,3,64,65,66,67,128,129,130,131,192,193,194,195,4,5,6,7,68,69,70,7..., dimensions={0} | all-to-all | bytes 2097152 | tf_op jit(solution)/shard_map/all_to_all | solution.py:324
  134.4 1.3 last_far.1
  135.6 7.3 %collective-permute-start.5 = (f32[256,256]{1,0:T(8,128)S(1)}, f32[256,256]{1,0:T(8,128)S(1)}, u32[]{:S(2)}, u32[]{:S(2)}) collective-permute-start(f32[256,256]{1,0:T(8,128)S(1)} %last_far.1), channel_id=1, source_target_pairs={{0,32},{32,0},{64,96},{96,64},{128,160},{160,128},{192,224},{224,1... | collective-permute-start | bytes 786440 | tf_op jit(solution)/shard_map/ppermute | solution.py:321
  142.9 1.3 last_near.1.kept
  144.2 0.8 place.1
  (27 shorter events, 1.1 us)
Async XLA Ops:
  0.0 1.0 copy-start.1
  2.1 12.2 %slice-start = ((f32[3,512,256]{2,1,0:T(8,128)}), f32[2,512,256]{2,1,0:T(8,128)S(1)}, s32[]{:S(2)}) async-start(f32[3,512,256]{2,1,0:T(8,128)} %param.6), calls=%async_computation.7 | async-start | bytes 2097152 | tf_op jit(solution)/shard_map/slice | solution.py:349
  2.1 28.5 %all-to-all-start = ((f32[32,16,256]{2,1,0:T(8,128)}), f32[32,16,256]{2,1,0:T(8,128)S(1)}, u32[]{:S(2)}, u32[]{:S(2)}) async-start(f32[32,16,256]{2,1,0:T(8,128)} %cut.1), calls=%async_computation | async-start | bytes 1048576 | tf_op jit(solution)/shard_map/all_to_all | solution.py:343
  14.3 1.9 %slice-start.1 = ((f32[3,512,256]{2,1,0:T(8,128)}), f32[1,512,256]{2,1,0:T(8,128)S(1)}, s32[]{:S(2)}) async-start(f32[3,512,256]{2,1,0:T(8,128)} %param.6), calls=%async_computation.8 | async-start | bytes 1048576 | tf_op jit(solution)/shard_map/slice | solution.py:351
  14.3 1.9 %copy-start.4 = (f32[512,256]{1,0:T(8,128)S(1)}, f32[512,256]{1,0:T(8,128)}, u32[]{:S(2)}) copy-start(f32[512,256]{1,0:T(8,128)} %param.5) | copy-start | bytes 1572868
  15.3 2.3 %copy-start.5 = (f32[256]{0:T(256)S(1)}, f32[256]{0:T(256)}, u32[]{:S(2)}) copy-start(f32[256]{0:T(256)} %param.7) | copy-start | bytes 3076
  15.3 3.8 %collective-permute-start.2 = (f32[2,256,256]{2,1,0:T(8,128)}, f32[2,256,256]{2,1,0:T(8,128)S(1)}, u32[]{:S(2)}, u32[]{:S(2)}) collective-permute-start(f32[2,256,256]{2,1,0:T(8,128)} %get-tuple-element.31), channel_id=1, source_target_pairs={{0,32},{32,0},{64,96},{96,64},{128,160},{160,128},{192,224},{224,1... | collective-permute-start | bytes 1572872 | tf_op jit(solution)/shard_map/ppermute | solution.py:321
  17.1 2.9 %collective-permute-start = (f32[2,256,256]{2,1,0:T(8,128)}, f32[2,256,256]{2,1,0:T(8,128)S(1)}, u32[]{:S(2)}, u32[]{:S(2)}) collective-permute-start(f32[2,256,256]{2,1,0:T(8,128)} %get-tuple-element.34), channel_id=1, source_target_pairs={{0,32},{32,0},{64,96},{96,64},{128,160},{160,128},{192,224},{224,1... | collective-permute-start | bytes 1572872 | tf_op jit(solution)/shard_map/ppermute | solution.py:321
  17.6 1.5 %collective-permute-start.1 = (f32[256]{0:T(256)S(1)}, f32[256]{0:T(256)S(1)}, u32[]{:S(2)}, u32[]{:S(2)}) collective-permute-start(f32[256]{0:T(256)S(1)} %copy-done.5), channel_id=1, source_target_pairs={{0,32},{32,0},{64,96},{96,64},{128,160},{160,128},{192,224},{224,1... | collective-permute-start | bytes 3080 | tf_op jit(solution)/shard_map/ppermute | solution.py:321
  20.0 0.8 copy-start.3
  30.6 3.9 %collective-permute-start.3 = (f32[512,256]{1,0:T(8,128)S(1)}, f32[512,256]{1,0:T(8,128)S(1)}, u32[]{:S(2)}, u32[]{:S(2)}) collective-permute-start(f32[512,256]{1,0:T(8,128)S(1)} %bitcast.17), channel_id=1, source_target_pairs={{0,32},{32,0},{64,96},{96,64},{128,160},{160,128},{192,224},{224,1... | collective-permute-start | bytes 1572872 | tf_op jit(solution)/shard_map/ppermute | solution.py:321
  55.8 26.8 %copy-start.2 = (f32[256,512]{1,0:T(8,128)S(1)}, f32[256,512]{1,0:T(8,128)}, u32[]{:S(2)}) copy-start(f32[256,512]{1,0:T(8,128)} %get-tuple-element.21.noise) | copy-start | bytes 1572868
  86.1 1.0 copy-start
  87.1 16.9 %all-to-all-start.4 = ((f32[32,16,512]{2,1,0:T(8,128)}), f32[32,16,512]{2,1,0:T(8,128)S(1)}, u32[]{:S(2)}, u32[]{:S(2)}) async-start(f32[32,16,512]{2,1,0:T(8,128)} %copy-done), calls=%async_computation.4 | async-start | bytes 2097152 | tf_op jit(solution)/shard_map/all_to_all | solution.py:324
  92.4 15.6 %collective-permute-start.4 = (f32[256,384]{1,0:T(8,128)S(1)}, f32[256,384]{1,0:T(8,128)}, u32[]{:S(2)}, u32[]{:S(2)}) collective-permute-start(f32[256,384]{1,0:T(8,128)S(1)} %bitcast.21), channel_id=1, source_target_pairs={{0,32},{32,0},{64,96},{96,64},{128,160},{160,128},{192,224},{224,1... | collective-permute-start | bytes 1179656 | tf_op jit(solution)/shard_map/ppermute | solution.py:321
  104.7 10.9 %all-to-all-start.5 = ((f32[4,16,512]{2,1,0:T(8,128)}), f32[4,16,512]{2,1,0:T(8,128)S(1)}, u32[]{:S(2)}, u32[]{:S(2)}) async-start(f32[4,16,512]{2,1,0:T(8,128)} %spread.3), calls=%async_computation.5 | async-start | bytes 262144 | tf_op jit(solution)/shard_map/all_to_all | solution.py:329
  135.6 8.5 %collective-permute-start.5 = (f32[256,256]{1,0:T(8,128)S(1)}, f32[256,256]{1,0:T(8,128)S(1)}, u32[]{:S(2)}, u32[]{:S(2)}) collective-permute-start(f32[256,256]{1,0:T(8,128)S(1)} %last_far.1), channel_id=1, source_target_pairs={{0,32},{32,0},{64,96},{96,64},{128,160},{160,128},{192,224},{224,1... | collective-permute-start | bytes 786440 | tf_op jit(solution)/shard_map/ppermute | solution.py:321

commit v11 on v10

--- a/solution.py
+++ b/solution.py
@@ -278,7 +278,7 @@
             ANY if len(args) + i in anywhere else VMEM for i in range(len(outs))
         ),
         scratch_shapes=list(scratch),
-        compiler_params=pltpu.CompilerParams(vmem_limit_bytes=24 << 20),
+        compiler_params=pltpu.CompilerParams(vmem_limit_bytes=14 << 20),
         cost_estimate=pl.CostEstimate(
             flops=12 * 256 * 512 * 512 * products,
             bytes_accessed=sum(4 * math.prod(s) for s in outs),

time: 146 us -> 146 us (level)
  no operation moved by 1% of the time
where the time goes in v11:
time: 146 us; the launch traced here: 145 us
  blocking collectives  63.3 us (43%)
  starting transfers between devices  36.2 us (25%)
  waiting for transfers between devices  24.6 us (17%)
  Pallas kernels  13 us (9%)
  other arithmetic  3.83 us (3%)
  local copies, waits for them, and re-layouts  3.81 us (3%)
    all_to_all x3, blocking collectives, in_plane(): lax.all_to_all(blocks, AXES, split_axis=0, concat_axis=0, axis_index_grou...  53.5 us
    ppermute x6, starting transfers between devices, other_core(): return lax.ppermute(array, 'space', swap)  15.4 us
    pallas_call x11, Pallas kernels, call(): pl.pallas_call(kernel, out_shape=shapes, in_specs=[SMEM if a.dtype == jnp...  13 us
    all_to_all x1, starting transfers between devices, per_device(): own = lax.all_to_all(cut, 'mem', split_axis=0, concat_axis=0)  12.2 us
    all_to_all x1, blocking collectives, in_column(): lax.all_to_all(blocks, 'mem', split_axis=0, concat_axis=0, axis_index_gro...  9.85 us
    all_to_all x1, waiting for transfers between devices, per_device(): own = lax.all_to_all(cut, 'mem', split_axis=0, concat_axis=0)  8.08 us
    all_to_all x1, waiting for transfers between devices, in_column(): lax.all_to_all(blocks, 'mem', split_axis=0, concat_axis=0, axis_index_gro...  7.51 us
    all_to_all x1, waiting for transfers between devices, in_plane(): lax.all_to_all(blocks, AXES, split_axis=0, concat_axis=0, axis_index_grou...  7.28 us
  transfers between devices with their start and end apart: 9, of which 5 were waited for; matrix products, arithmetic and copies ran while one was open for 3% of the time, Pallas kernels for 2%

profile of v11, /device:TPU:1, one launch (start us, length us, event | category | flops | bytes accessed | tf_op | source)
XLA Modules:
  0.0 145.0 jit_solution(18386304991891700220)
XLA Ops:
  0.0 1.0 copy-done.1
  1.0 1.1 cut.1
  2.1 12.2 %all-to-all-start = ((f32[32,16,256]{2,1,0:T(8,128)}), f32[32,16,256]{2,1,0:T(8,128)S(1)}, u32[]{:S(2)}, u32[]{:S(2)}) async-start(f32[32,16,256]{2,1,0:T(8,128)} %cut.1), calls=%async_computation | async-start | bytes 1048576 | tf_op jit(solution)/shard_map/all_to_all | solution.py:343
  14.3 0.9 constant_dynamic-slice_fusion
  15.3 1.0 collective-permute-start.2
  16.2 0.9 fusion.14
  17.1 0.4 collective-permute-start
  17.6 1.4 collective-permute-done.1
  19.0 1.0 fusion.15
  20.0 0.8 copy-done.3
  20.8 1.7 %fusion.8 = (f32[256,512]{1,0:T(8,128)S(1)}, f32[256,512]{1,0:T(8,128)S(1)}) fusion(f32[2,256,256]{2,1,0:T(8,128)} %copy-done.3, f32[2,256,256]{2,1,0:T(8,128)S(1)} %get-tuple-element.33, f32[512]{0:T(512)S(1)} %constant_dynamic-update-slice_fusion), kind=kLoop, calls=%fused_computation.19 | loop fusion | flops 5242880 | bytes 2099200 | tf_op jit(solution)/shard_map/add | solution.py:354
  22.5 8.1 %all-to-all-done = f32[32,16,256]{2,1,0:T(8,128)S(1)} async-done(((f32[32,16,256]{2,1,0:T(8,128)}), f32[32,16,256]{2,1,0:T(8,128)S(1)}, u32[]{:S(2)}, u32[]{:S(2)}) %all-to-all-start) | async-done | bytes 524320 | tf_op jit(solution)/shard_map/all_to_all | solution.py:343
  30.6 2.4 %collective-permute-start.3 = (f32[512,256]{1,0:T(8,128)S(1)}, f32[512,256]{1,0:T(8,128)S(1)}, u32[]{:S(2)}, u32[]{:S(2)}) collective-permute-start(f32[512,256]{1,0:T(8,128)S(1)} %bitcast.17), channel_id=1, source_target_pairs={{0,32},{32,0},{64,96},{96,64},{128,160},{160,128},{192,224},{224,1... | collective-permute-start | bytes 1572872 | tf_op jit(solution)/shard_map/ppermute | solution.py:321
  33.0 1.0 own.1.gram_own
  34.7 1.1 first.1
  35.8 20.0 %all_to_all.35.got = f32[32,8,896]{2,1,0:T(8,128)S(1)} all-to-all(f32[32,8,896]{2,1,0:T(8,128)S(1)} %get-tuple-element.18), channel_id=1, replica_groups={{0,1,2,3,64,65,66,67,128,129,130,131,192,193,194,195,4,5,6,7,68,69,70,7..., dimensions={0} | all-to-all | bytes 1835008 | tf_op jit(solution)/shard_map/all_to_all | solution.py:324
  55.8 9.9 %all_to_all.36.got = f32[4,8,896]{2,1,0:T(8,128)S(1)} all-to-all(f32[4,8,896]{2,1,0:T(8,128)S(1)} %spread.2), channel_id=1, replica_groups={{0,8,16,24},{1,9,17,25},{2,10,18,26},{3,11,19,27},{4,12,20,28},{5,13,21..., dimensions={0} | all-to-all | bytes 229376 | tf_op jit(solution)/shard_map/all_to_all | solution.py:329
  65.8 16.7 %all_to_all.37.got = f32[32,8,896]{2,1,0:T(8,128)S(1)} all-to-all(f32[32,8,896]{2,1,0:T(8,128)S(1)} %weigh.1), channel_id=1, replica_groups={{0,1,2,3,64,65,66,67,128,129,130,131,192,193,194,195,4,5,6,7,68,69,70,7..., dimensions={0} | all-to-all | bytes 1835008 | tf_op jit(solution)/shard_map/all_to_all | solution.py:324
  82.6 3.5 %step.1 = (f32[32,16,512]{2,1,0:T(8,128)S(1)}, f32[256,512]{1,0:T(8,128)S(1)}, f32[32,8,384]{2,1,0:T(8,128)S(1)}) custom-call(f32[32,8,896]{2,1,0:T(8,128)S(1)} %all_to_all.37.got, f32[512,512]{1,0:T(8,128)S(1)} %get-tuple-element.19.members, f32[256,512]{1,0:T(8,128)S(1)} %get-tuple-element.20.u, f32[256,512]{1,0:T(8,128)S(1)} %copy-done.2, ...), custom_call_target="tpu_custom_call" | custom-call | flops 2415919104 | bytes 1966080 | tf_op jit(solution)/shard_map/step/pallas_call | solution.py:270
  86.1 1.0 copy-done
  87.1 5.3 %all-to-all-start.4 = ((f32[32,16,512]{2,1,0:T(8,128)}), f32[32,16,512]{2,1,0:T(8,128)S(1)}, u32[]{:S(2)}, u32[]{:S(2)}) async-start(f32[32,16,512]{2,1,0:T(8,128)} %copy-done), calls=%async_computation.4 | async-start | bytes 2097152 | tf_op jit(solution)/shard_map/all_to_all | solution.py:324
  92.4 4.3 %collective-permute-start.4 = (f32[256,384]{1,0:T(8,128)S(1)}, f32[256,384]{1,0:T(8,128)}, u32[]{:S(2)}, u32[]{:S(2)}) collective-permute-start(f32[256,384]{1,0:T(8,128)S(1)} %bitcast.21), channel_id=1, source_target_pairs={{0,32},{32,0},{64,96},{96,64},{128,160},{160,128},{192,224},{224,1... | collective-permute-start | bytes 1179656 | tf_op jit(solution)/shard_map/ppermute | solution.py:321
  96.7 7.3 %all-to-all-done.4.got = f32[32,16,512]{2,1,0:T(8,128)S(1)} async-done(((f32[32,16,512]{2,1,0:T(8,128)}), f32[32,16,512]{2,1,0:T(8,128)S(1)}, u32[]{:S(2)}, u32[]{:S(2)}) %all-to-all-start.4) | async-done | bytes 1048608 | tf_op jit(solution)/shard_map/all_to_all | solution.py:324
  104.0 0.7 spread.3
  104.7 3.3 %all-to-all-start.5 = ((f32[4,16,512]{2,1,0:T(8,128)}), f32[4,16,512]{2,1,0:T(8,128)S(1)}, u32[]{:S(2)}, u32[]{:S(2)}) async-start(f32[4,16,512]{2,1,0:T(8,128)} %spread.3), calls=%async_computation.5 | async-start | bytes 262144 | tf_op jit(solution)/shard_map/all_to_all | solution.py:329
  108.1 7.5 %all-to-all-done.5.got = f32[4,16,512]{2,1,0:T(8,128)S(1)} async-done(((f32[4,16,512]{2,1,0:T(8,128)}), f32[4,16,512]{2,1,0:T(8,128)S(1)}, u32[]{:S(2)}, u32[]{:S(2)}) %all-to-all-start.5) | async-done | bytes 131104 | tf_op jit(solution)/shard_map/all_to_all | solution.py:329
  115.6 1.9 %weigh_twice.1 = f32[32,16,512]{2,1,0:T(8,128)S(1)} custom-call(s32[1]{0:T(128)} %bitcast.core, f32[4,16,512]{2,1,0:T(8,128)S(1)} %all-to-all-done.5.got, f32[256,384]{1,0:T(8,128)S(1)} %bitcast.22, f32[256,384]{1,0:T(8,128)} %collective-permute-done.4.far_in), custom_call_target="tpu_custom_call" | custom-call | bytes 1048576 | tf_op jit(solution)/shard_map/weigh_twice/pallas_call | solution.py:270
  117.6 16.8 %all_to_all.38.got = f32[32,16,512]{2,1,0:T(8,128)S(1)} all-to-all(f32[32,16,512]{2,1,0:T(8,128)S(1)} %weigh_twice.1), channel_id=1, replica_groups={{0,1,2,3,64,65,66,67,128,129,130,131,192,193,194,195,4,5,6,7,68,69,70,7..., dimensions={0} | all-to-all | bytes 2097152 | tf_op jit(solution)/shard_map/all_to_all | solution.py:324
  134.4 1.3 last_far.1
  135.6 7.3 %collective-permute-start.5 = (f32[256,256]{1,0:T(8,128)S(1)}, f32[256,256]{1,0:T(8,128)S(1)}, u32[]{:S(2)}, u32[]{:S(2)}) collective-permute-start(f32[256,256]{1,0:T(8,128)S(1)} %last_far.1), channel_id=1, source_target_pairs={{0,32},{32,0},{64,96},{96,64},{128,160},{160,128},{192,224},{224,1... | collective-permute-start | bytes 786440 | tf_op jit(solution)/shard_map/ppermute | solution.py:321
  142.9 1.3 last_near.1.kept
  144.2 0.8 place.1
  (27 shorter events, 1.1 us)
Async XLA Ops:
  0.0 1.0 copy-start.1
  2.1 12.2 %slice-start = ((f32[3,512,256]{2,1,0:T(8,128)}), f32[2,512,256]{2,1,0:T(8,128)S(1)}, s32[]{:S(2)}) async-start(f32[3,512,256]{2,1,0:T(8,128)} %param.6), calls=%async_computation.7 | async-start | bytes 2097152 | tf_op jit(solution)/shard_map/slice | solution.py:349
  2.1 28.5 %all-to-all-start = ((f32[32,16,256]{2,1,0:T(8,128)}), f32[32,16,256]{2,1,0:T(8,128)S(1)}, u32[]{:S(2)}, u32[]{:S(2)}) async-start(f32[32,16,256]{2,1,0:T(8,128)} %cut.1), calls=%async_computation | async-start | bytes 1048576 | tf_op jit(solution)/shard_map/all_to_all | solution.py:343
  14.3 1.9 %slice-start.1 = ((f32[3,512,256]{2,1,0:T(8,128)}), f32[1,512,256]{2,1,0:T(8,128)S(1)}, s32[]{:S(2)}) async-start(f32[3,512,256]{2,1,0:T(8,128)} %param.6), calls=%async_computation.8 | async-start | bytes 1048576 | tf_op jit(solution)/shard_map/slice | solution.py:351
  14.3 1.9 %copy-start.4 = (f32[512,256]{1,0:T(8,128)S(1)}, f32[512,256]{1,0:T(8,128)}, u32[]{:S(2)}) copy-start(f32[512,256]{1,0:T(8,128)} %param.5) | copy-start | bytes 1572868
  15.3 2.3 %copy-start.5 = (f32[256]{0:T(256)S(1)}, f32[256]{0:T(256)}, u32[]{:S(2)}) copy-start(f32[256]{0:T(256)} %param.7) | copy-start | bytes 3076
  15.3 3.8 %collective-permute-start.2 = (f32[2,256,256]{2,1,0:T(8,128)}, f32[2,256,256]{2,1,0:T(8,128)S(1)}, u32[]{:S(2)}, u32[]{:S(2)}) collective-permute-start(f32[2,256,256]{2,1,0:T(8,128)} %get-tuple-element.31), channel_id=1, source_target_pairs={{0,32},{32,0},{64,96},{96,64},{128,160},{160,128},{192,224},{224,1... | collective-permute-start | bytes 1572872 | tf_op jit(solution)/shard_map/ppermute | solution.py:321
  17.1 2.9 %collective-permute-start = (f32[2,256,256]{2,1,0:T(8,128)}, f32[2,256,256]{2,1,0:T(8,128)S(1)}, u32[]{:S(2)}, u32[]{:S(2)}) collective-permute-start(f32[2,256,256]{2,1,0:T(8,128)} %get-tuple-element.34), channel_id=1, source_target_pairs={{0,32},{32,0},{64,96},{96,64},{128,160},{160,128},{192,224},{224,1... | collective-permute-start | bytes 1572872 | tf_op jit(solution)/shard_map/ppermute | solution.py:321
  17.6 1.5 %collective-permute-start.1 = (f32[256]{0:T(256)S(1)}, f32[256]{0:T(256)S(1)}, u32[]{:S(2)}, u32[]{:S(2)}) collective-permute-start(f32[256]{0:T(256)S(1)} %copy-done.5), channel_id=1, source_target_pairs={{0,32},{32,0},{64,96},{96,64},{128,160},{160,128},{192,224},{224,1... | collective-permute-start | bytes 3080 | tf_op jit(solution)/shard_map/ppermute | solution.py:321
  20.0 0.8 copy-start.3
  30.6 3.9 %collective-permute-start.3 = (f32[512,256]{1,0:T(8,128)S(1)}, f32[512,256]{1,0:T(8,128)S(1)}, u32[]{:S(2)}, u32[]{:S(2)}) collective-permute-start(f32[512,256]{1,0:T(8,128)S(1)} %bitcast.17), channel_id=1, source_target_pairs={{0,32},{32,0},{64,96},{96,64},{128,160},{160,128},{192,224},{224,1... | collective-permute-start | bytes 1572872 | tf_op jit(solution)/shard_map/ppermute | solution.py:321
  55.8 26.8 %copy-start.2 = (f32[256,512]{1,0:T(8,128)S(1)}, f32[256,512]{1,0:T(8,128)}, u32[]{:S(2)}) copy-start(f32[256,512]{1,0:T(8,128)} %get-tuple-element.21.noise) | copy-start | bytes 1572868
  86.1 1.0 copy-start
  87.1 16.9 %all-to-all-start.4 = ((f32[32,16,512]{2,1,0:T(8,128)}), f32[32,16,512]{2,1,0:T(8,128)S(1)}, u32[]{:S(2)}, u32[]{:S(2)}) async-start(f32[32,16,512]{2,1,0:T(8,128)} %copy-done), calls=%async_computation.4 | async-start | bytes 2097152 | tf_op jit(solution)/shard_map/all_to_all | solution.py:324
  92.4 15.6 %collective-permute-start.4 = (f32[256,384]{1,0:T(8,128)S(1)}, f32[256,384]{1,0:T(8,128)}, u32[]{:S(2)}, u32[]{:S(2)}) collective-permute-start(f32[256,384]{1,0:T(8,128)S(1)} %bitcast.21), channel_id=1, source_target_pairs={{0,32},{32,0},{64,96},{96,64},{128,160},{160,128},{192,224},{224,1... | collective-permute-start | bytes 1179656 | tf_op jit(solution)/shard_map/ppermute | solution.py:321
  104.7 10.9 %all-to-all-start.5 = ((f32[4,16,512]{2,1,0:T(8,128)}), f32[4,16,512]{2,1,0:T(8,128)S(1)}, u32[]{:S(2)}, u32[]{:S(2)}) async-start(f32[4,16,512]{2,1,0:T(8,128)} %spread.3), calls=%async_computation.5 | async-start | bytes 262144 | tf_op jit(solution)/shard_map/all_to_all | solution.py:329
  135.6 8.5 %collective-permute-start.5 = (f32[256,256]{1,0:T(8,128)S(1)}, f32[256,256]{1,0:T(8,128)S(1)}, u32[]{:S(2)}, u32[]{:S(2)}) collective-permute-start(f32[256,256]{1,0:T(8,128)S(1)} %last_far.1), channel_id=1, source_target_pairs={{0,32},{32,0},{64,96},{96,64},{128,160},{160,128},{192,224},{224,1... | collective-permute-start | bytes 786440 | tf_op jit(solution)/shard_map/ppermute | solution.py:321
